TPU v7x, 32 devices: a whole 2x2x4 slice. The times are simulated.
32 devices in a mesh: dp: 4 (over y, core), tensor: 8 (over z, x).
Axes of the slice: x: 2, y: 2, z: 4, core: 2. Of those that a mesh axis runs over, the one named last changes fastest.
Arguments:
- src_ids: int32 [1024, 4], P('tensor', 'dp'), may hold values from 0 to 131071, as said below
- tgt_ids: int32 [1024, 4], P('tensor', 'dp'), may hold values from 0 to 131071, as said below
- src_segs: int32 [1024, 4], P(None, 'dp'), may hold values from -1 to 4, as said below
- tgt_segs: int32 [1024, 4], P(None, 'dp'), may hold values from -1 to 4, as said below
- embed_table: bfloat16 [131072, 1024], P(('dp', 'tensor')), may hold values from -6 to 6
- norm_gains: float32 [9, 1024], replicated, may hold values from 0.5 to 1.5
- enc_qkv: bfloat16 [3, 1024, 1024], P(None, None, 'tensor'), may hold values from -0.1875 to 0.1875
- enc_out: bfloat16 [1024, 1024], P('tensor'), may hold values from -1.5 to 1.5
- enc_up: bfloat16 [1024, 4096], P(None, 'tensor'), may hold values from -0.1875 to 0.1875
- enc_down: bfloat16 [4096, 1024], P('tensor'), may hold values from -0.09375 to 0.09375
- dec_qkv: bfloat16 [3, 1024, 1024], P(None, None, 'tensor'), may hold values from -0.1875 to 0.1875
- dec_out: bfloat16 [1024, 1024], P('tensor'), may hold values from -1.5 to 1.5
- cross_q: bfloat16 [1024, 1024], P(None, 'tensor'), may hold values from -0.1875 to 0.1875
- cross_kv: bfloat16 [2, 1024, 1024], P(None, None, 'tensor'), may hold values from -0.1875 to 0.1875
- cross_out: bfloat16 [1024, 1024], P('tensor'), may hold values from -1.5 to 1.5
- dec_up: bfloat16 [1024, 4096], P(None, 'tensor'), may hold values from -0.1875 to 0.1875
- dec_down: bfloat16 [4096, 1024], P('tensor'), may hold values from -0.09375 to 0.09375
- cotangent: float32 [1024, 4, 1024], P('tensor', 'dp'), may hold values from -6 to 6
Outputs:
- decoded: float32 [1024, 4, 1024], P('tensor', 'dp')
- table_grad: float32 [131072, 1024], P(('dp', 'tensor'))
- gain_grad: float32 [9, 1024], replicated
- enc_qkv_grad: float32 [3, 1024, 1024], P(None, 'dp', 'tensor')
- enc_out_grad: float32 [1024, 1024], P('tensor', 'dp')
- enc_up_grad: float32 [1024, 4096], P('dp', 'tensor')
- enc_down_grad: float32 [4096, 1024], P('tensor', 'dp')
- dec_qkv_grad: float32 [3, 1024, 1024], P(None, 'dp', 'tensor')
- dec_out_grad: float32 [1024, 1024], P('tensor', 'dp')
- cross_q_grad: float32 [1024, 1024], P('dp', 'tensor')
- cross_kv_grad: float32 [2, 1024, 1024], P(None, 'dp', 'tensor')
- cross_out_grad: float32 [1024, 1024], P('tensor', 'dp')
- dec_up_grad: float32 [1024, 4096], P('dp', 'tensor')
- dec_down_grad: float32 [4096, 1024], P('tensor', 'dp')
Inputs may be any that keep to these rules, and one draw needn't show every extreme that they name: `src_ids`: of the 256 source and target tokens that one device holds, at most 12 have ids in one block of 4096 consecutive table rows, and in every device's tokens one such block holds exactly 12. `tgt_ids`: drawn together with src_ids under the bound stated there. `src_segs`: each row holds 5 documents numbered 0 to 4 in order, each of 128 to 191 positions, then padding marked -1 on one position or more. `tgt_segs`: laid out as the source segments; document k of a target row translates document k of the same source row.
All inputs are finite; a program needn't handle non-finite values.
Results may differ from a plain program's by a relative error of at most 0.035.
Values may be sent and summed in bfloat16 or wider, within the bound.
No kernel may reach another device: no remote copies, remote signals or barrier semaphores. Data moves between devices by JAX's collectives and lax.ppermute only.
A program may use at most 192 MiB of HBM per device.

v0:
```python
import math

import jax
import jax.numpy as jnp
from jax import lax
from jax.sharding import PartitionSpec as P

HEAD_DIM = 64


NORM_EPS = 1e-05
MASKED = -1e30


def layer_norm(values, gain_row):
    centre = jnp.mean(values, axis=-1, keepdims=True)
    shifted = values - centre
    spread = jnp.mean(shifted * shifted, axis=-1, keepdims=True)
    return shifted * lax.rsqrt(spread + NORM_EPS) * gain_row


def embed_norm(token_rows, gain_row):
    return layer_norm(token_rows * math.sqrt(token_rows.shape[-1]), gain_row)


def gelu_exact(pre_act):
    return jax.nn.gelu(pre_act, approximate=False)


def split_heads(arranged):
    return arranged.reshape(arranged.shape[0], arranged.shape[1], -1, HEAD_DIM)


def allowed_keys(seg_query, seg_key, opening, causal):
    query_side = seg_query.T[:, :, None]
    key_side = seg_key.T[:, None, :]
    allowed = (query_side == key_side) | (query_side < 0)
    if causal:
        query_pos = opening + jnp.arange(seg_query.shape[0])
        key_pos = jnp.arange(seg_key.shape[0])
        allowed = allowed & (query_pos[:, None] >= key_pos[None, :])[None]
    return allowed


def block_scores(query_heads, key_heads, seg_query, seg_key, opening, causal, factor):
    scores = (
        jnp.einsum("qrhd,krhd->rhqk", query_heads, key_heads, preferred_element_type=jnp.float32)
        * factor
    )
    allowed = allowed_keys(seg_query, seg_key, opening, causal)
    return jnp.where(allowed[:, None], scores, MASKED)


def attend_forward(queries, keys_in, values_in, seg_query, seg_key, causal, factor):
    query_heads = split_heads(queries)
    key_heads = split_heads(keys_in)
    value_heads = split_heads(values_in)
    length = queries.shape[0]
    step_rows = min(512, length)
    pieces = []
    softmax_stats = []
    for opening in range(0, length, step_rows):
        closing = opening + step_rows
        scores = block_scores(
            query_heads[opening:closing],
            key_heads,
            seg_query[opening:closing],
            seg_key,
            opening,
            causal,
            factor,
        )
        row_peak = jnp.max(scores, axis=-1, keepdims=True)
        raised = jnp.exp(scores - row_peak)
        summed = jnp.sum(raised, axis=-1, keepdims=True)
        attn_probs = (raised / summed).astype(jnp.bfloat16)
        mixed_block = jnp.einsum(
            "rhqk,krhd->qrhd", attn_probs, value_heads, preferred_element_type=jnp.float32
        )
        pieces.append(mixed_block.astype(jnp.bfloat16))
        softmax_stats.append((row_peak, summed))
    return (jnp.concatenate(pieces, axis=0).reshape(queries.shape), softmax_stats)


def attend_backward(
    queries, keys_in, values_in, grad_mixed, seg_query, seg_key, causal, factor, softmax_stats
):
    query_heads = split_heads(queries)
    key_heads = split_heads(keys_in)
    value_heads = split_heads(values_in)
    grad_heads = split_heads(grad_mixed)
    length = queries.shape[0]
    step_rows = min(512, length)
    key_grad = jnp.zeros(key_heads.shape, jnp.float32)
    value_grad = jnp.zeros(value_heads.shape, jnp.float32)
    query_parts = []
    for opening in range(0, length, step_rows):
        closing = opening + step_rows
        row_peak, summed = softmax_stats[opening // step_rows]
        scores = block_scores(
            query_heads[opening:closing],
            key_heads,
            seg_query[opening:closing],
            seg_key,
            opening,
            causal,
            factor,
        )
        attn_probs = jnp.exp(scores - row_peak) / summed
        grad_probs = jnp.einsum(
            "qrhd,krhd->rhqk",
            grad_heads[opening:closing],
            value_heads,
            preferred_element_type=jnp.float32,
        )
        row_inner = jnp.sum(attn_probs * grad_probs, axis=-1, keepdims=True)
        grad_scores = (attn_probs * (grad_probs - row_inner)).astype(jnp.bfloat16)
        query_block = (
            jnp.einsum(
                "rhqk,krhd->qrhd", grad_scores, key_heads, preferred_element_type=jnp.float32
            )
            * factor
        )
        query_parts.append(query_block.astype(jnp.bfloat16))
        key_grad = (
            key_grad
            + jnp.einsum(
                "rhqk,qrhd->krhd",
                grad_scores,
                query_heads[opening:closing],
                preferred_element_type=jnp.float32,
            )
            * factor
        )
        value_grad = value_grad + jnp.einsum(
            "rhqk,qrhd->krhd",
            attn_probs.astype(jnp.bfloat16),
            grad_heads[opening:closing],
            preferred_element_type=jnp.float32,
        )
    query_grad = jnp.concatenate(query_parts, axis=0).reshape(queries.shape)
    return (
        query_grad,
        key_grad.astype(jnp.bfloat16).reshape(keys_in.shape),
        value_grad.astype(jnp.bfloat16).reshape(values_in.shape),
    )


def gather_inputs(local_rows):
    return lax.all_gather(local_rows, "tensor", axis=0, tiled=True)


def gather_grads(local_grad):
    return lax.all_gather(local_grad, "tensor", axis=0, tiled=True)


def sum_outputs(term_fn, row_count):
    return lax.psum_scatter(
        term_fn(jnp.int32(0), lax.axis_size("tensor") * row_count).astype(jnp.bfloat16),
        "tensor",
        scatter_dimension=0,
        tiled=True,
    ).astype(jnp.float32)


def sum_inputs(term_fn, row_count):
    return lax.psum_scatter(
        term_fn(jnp.int32(0), lax.axis_size("tensor") * row_count).astype(jnp.bfloat16),
        "tensor",
        scatter_dimension=0,
        tiled=True,
    ).astype(jnp.float32)


def inputs_again(local_rows):
    return lax.all_gather(local_rows, "tensor", axis=0, tiled=True)


def row_term(operand, weight, pattern):

    def term(start_at, row_count):
        return jnp.einsum(pattern, operand, weight, preferred_element_type=jnp.float32)

    return term


def attention_forward(hidden, gain_row, qkv_weight, out_weight, segments, causal, factor):
    normed, norm_back = jax.vjp(layer_norm, hidden, gain_row)
    normed_low = normed.astype(jnp.bfloat16)
    gathered = gather_inputs(normed_low)
    projected = jnp.einsum(
        "srd,cde->csre", gathered, qkv_weight, preferred_element_type=jnp.float32
    ).astype(jnp.bfloat16)
    mixed_heads, softmax_stats = attend_forward(
        projected[0], projected[1], projected[2], segments, segments, causal, factor
    )
    update = sum_outputs(row_term(mixed_heads, out_weight, "sre,ed->srd"), hidden.shape[0])
    return (
        hidden + update,
        (norm_back, normed_low, gathered, projected, mixed_heads, softmax_stats),
    )


def attention_backward(grad_hidden, saved_state, qkv_weight, out_weight, segments, causal, factor):
    norm_back, normed_low, gathered, projected, mixed_heads, softmax_stats = saved_state
    grad_full = gather_grads(grad_hidden.astype(jnp.bfloat16))
    grad_mixed = jnp.einsum(
        "srd,ed->sre", grad_full, out_weight, preferred_element_type=jnp.float32
    ).astype(jnp.bfloat16)
    out_grad = jnp.einsum("sre,srd->ed", mixed_heads, grad_full, preferred_element_type=jnp.float32)
    query_grad, key_grad, value_grad = attend_backward(
        projected[0],
        projected[1],
        projected[2],
        grad_mixed,
        segments,
        segments,
        causal,
        factor,
        softmax_stats,
    )
    grad_proj = jnp.stack([query_grad, key_grad, value_grad])
    inputs_full = inputs_again(normed_low)
    qkv_grad = jnp.einsum(
        "srd,csre->cde", inputs_full, grad_proj, preferred_element_type=jnp.float32
    )
    grad_normed = sum_inputs(row_term(grad_proj, qkv_weight, "csre,cde->srd"), grad_hidden.shape[0])
    grad_input, gain_grad = norm_back(grad_normed)
    return (grad_hidden + grad_input, gain_grad, qkv_grad, out_grad)


def cross_forward(
    dec_state,
    gain_row,
    memory_full,
    query_weight,
    pair_weight,
    out_weight,
    seg_target,
    seg_source,
    factor,
):
    normed, norm_back = jax.vjp(layer_norm, dec_state, gain_row)
    normed_low = normed.astype(jnp.bfloat16)
    gathered = gather_inputs(normed_low)
    queries = jnp.einsum(
        "srd,de->sre", gathered, query_weight, preferred_element_type=jnp.float32
    ).astype(jnp.bfloat16)
    paired = jnp.einsum(
        "srd,cde->csre", memory_full, pair_weight, preferred_element_type=jnp.float32
    ).astype(jnp.bfloat16)
    mixed_heads, softmax_stats = attend_forward(
        queries, paired[0], paired[1], seg_target, seg_source, False, factor
    )
    update = sum_outputs(row_term(mixed_heads, out_weight, "sre,ed->srd"), dec_state.shape[0])
    return (
        dec_state + update,
        (norm_back, normed_low, gathered, queries, paired, mixed_heads, softmax_stats),
    )


def cross_backward(
    grad_state,
    saved_state,
    memory_low,
    query_weight,
    pair_weight,
    out_weight,
    seg_target,
    seg_source,
    factor,
):
    norm_back, normed_low, gathered, queries, paired, mixed_heads, softmax_stats = saved_state
    grad_full = gather_grads(grad_state.astype(jnp.bfloat16))
    grad_mixed = jnp.einsum(
        "srd,ed->sre", grad_full, out_weight, preferred_element_type=jnp.float32
    ).astype(jnp.bfloat16)
    out_grad = jnp.einsum("sre,srd->ed", mixed_heads, grad_full, preferred_element_type=jnp.float32)
    query_grad, key_grad, value_grad = attend_backward(
        queries,
        paired[0],
        paired[1],
        grad_mixed,
        seg_target,
        seg_source,
        False,
        factor,
        softmax_stats,
    )
    grad_pair = jnp.stack([key_grad, value_grad])
    inputs_full = inputs_again(normed_low)
    memory_again = inputs_again(memory_low)
    query_wgrad = jnp.einsum(
        "srd,sre->de", inputs_full, query_grad, preferred_element_type=jnp.float32
    )
    pair_wgrad = jnp.einsum(
        "srd,csre->cde", memory_again, grad_pair, preferred_element_type=jnp.float32
    )
    local_rows = grad_state.shape[0]
    grad_normed = sum_inputs(row_term(query_grad, query_weight, "sre,de->srd"), local_rows)
    grad_memory = sum_inputs(row_term(grad_pair, pair_weight, "csre,cde->srd"), local_rows)
    grad_input, gain_grad = norm_back(grad_normed)
    return (grad_state + grad_input, gain_grad, grad_memory, query_wgrad, pair_wgrad, out_grad)


def ffn_forward(hidden, gain_row, up_weight, down_weight):
    normed, norm_back = jax.vjp(layer_norm, hidden, gain_row)
    normed_low = normed.astype(jnp.bfloat16)
    gathered = gather_inputs(normed_low)
    pre_act = jnp.einsum("srd,df->srf", gathered, up_weight, preferred_element_type=jnp.float32)
    activated, gelu_back = jax.vjp(gelu_exact, pre_act)
    act_low = activated.astype(jnp.bfloat16)
    update = sum_outputs(row_term(act_low, down_weight, "srf,fd->srd"), hidden.shape[0])
    saved_state = (norm_back, normed_low, gathered, act_low, gelu_back)
    return (hidden + update, saved_state)


def ffn_backward(grad_hidden, saved_state, up_weight, down_weight):
    norm_back, normed_low, gathered, act_low, gelu_back = saved_state
    grad_full = gather_grads(grad_hidden.astype(jnp.bfloat16))
    grad_act = jnp.einsum("srd,fd->srf", grad_full, down_weight, preferred_element_type=jnp.float32)
    grad_pre = gelu_back(grad_act)[0].astype(jnp.bfloat16)
    down_wgrad = jnp.einsum("srf,srd->fd", act_low, grad_full, preferred_element_type=jnp.float32)
    inputs_full = inputs_again(normed_low)
    up_wgrad = jnp.einsum("srd,srf->df", inputs_full, grad_pre, preferred_element_type=jnp.float32)
    grad_normed = sum_inputs(row_term(grad_pre, up_weight, "srf,df->srd"), grad_hidden.shape[0])
    grad_input, gain_grad = norm_back(grad_normed)
    return (grad_hidden + grad_input, gain_grad, up_wgrad, down_wgrad)


def table_lookup(src_ids, tgt_ids, src_live, tgt_live, embed_table):
    token_ids = jnp.concatenate([src_ids.reshape(-1), tgt_ids.reshape(-1)])
    token_live = jnp.concatenate([src_live.reshape(-1), tgt_live.reshape(-1)])
    shard_rows = embed_table.shape[0]
    size_dp = lax.axis_size("dp")
    size_tensor = lax.axis_size("tensor")
    owners = size_dp * size_tensor
    capacity = max(2, 3 * token_ids.shape[0] // (2 * owners))
    owner_of = token_ids // shard_rows
    row_of = token_ids - owner_of * shard_rows
    owner_flags = ((owner_of[:, None] == jnp.arange(owners)[None, :]) & token_live[:, None]).astype(
        jnp.int32
    )
    earlier = jnp.cumsum(owner_flags, axis=0) - owner_flags
    ranking = jnp.sum(earlier * owner_flags, axis=1)
    slot_of = jnp.where(token_live, owner_of * capacity + ranking, owners * capacity)
    requests = jnp.full((owners * capacity,), -1, jnp.int32).at[slot_of].set(row_of, mode="drop")
    wanted = lax.all_to_all(
        lax.all_to_all(
            requests.reshape(size_dp, size_tensor, capacity),
            "dp",
            split_axis=0,
            concat_axis=0,
            tiled=True,
        ),
        "tensor",
        split_axis=1,
        concat_axis=1,
        tiled=True,
    ).reshape(-1)
    found_rows = wanted >= 0
    picked = jnp.take(embed_table, jnp.where(found_rows, wanted, 0), axis=0)
    picked = jnp.where(found_rows[:, None], picked, jnp.zeros_like(picked))
    replies = lax.all_to_all(
        lax.all_to_all(
            picked.reshape(size_dp, size_tensor, capacity, -1),
            "dp",
            split_axis=0,
            concat_axis=0,
            tiled=True,
        ),
        "tensor",
        split_axis=1,
        concat_axis=1,
        tiled=True,
    )
    replies = replies.reshape(owners * capacity, -1)
    fetched = jnp.take(replies, jnp.minimum(slot_of, owners * capacity - 1), axis=0).astype(
        jnp.float32
    )
    fetched = fetched * token_live[:, None].astype(jnp.float32)
    return (fetched, (slot_of, wanted, found_rows, size_dp, size_tensor, capacity))


def table_gradient(grad_tokens, route_info, shard_rows):
    slot_of, wanted, found_rows, size_dp, size_tensor, capacity = route_info
    owners = size_dp * size_tensor
    width_model = grad_tokens.shape[1]
    outgoing = (
        jnp.zeros((owners * capacity, width_model), jnp.float32)
        .at[slot_of]
        .set(grad_tokens, mode="drop")
    )
    arrived = lax.all_to_all(
        lax.all_to_all(
            outgoing.reshape(size_dp, size_tensor, capacity, width_model).astype(jnp.bfloat16),
            "dp",
            split_axis=0,
            concat_axis=0,
            tiled=True,
        ),
        "tensor",
        split_axis=1,
        concat_axis=1,
        tiled=True,
    ).astype(jnp.float32)
    arrived = arrived.reshape(owners * capacity, width_model)
    target_rows = jnp.where(found_rows, wanted, shard_rows)
    summed = (
        jnp.zeros((shard_rows, width_model), jnp.float32).at[target_rows].add(arrived, mode="drop")
    )
    counted = (
        jnp.zeros((shard_rows,), jnp.float32)
        .at[target_rows]
        .add(jnp.ones(target_rows.shape, jnp.float32), mode="drop")
    )
    return summed / jnp.maximum(counted, 1.0)[:, None]


def on_device(
    src_ids,
    tgt_ids,
    src_segs,
    tgt_segs,
    embed_table,
    norm_gains,
    enc_qkv,
    enc_out,
    enc_up,
    enc_down,
    dec_qkv,
    dec_out,
    cross_q,
    cross_kv,
    cross_out,
    dec_up,
    dec_down,
    cotangent,
):
    local_len, batch_rows = src_ids.shape
    width_model = embed_table.shape[1]
    factor = 1.0 / math.sqrt(HEAD_DIM)
    offset = lax.axis_index("tensor") * local_len
    src_here = lax.dynamic_slice_in_dim(src_segs, offset, local_len, 0)
    tgt_here = lax.dynamic_slice_in_dim(tgt_segs, offset, local_len, 0)
    src_live = src_here >= 0
    tgt_live = tgt_here >= 0
    fetched, route_info = table_lookup(src_ids, tgt_ids, src_live, tgt_live, embed_table)
    half_tokens = local_len * batch_rows
    src_rows = fetched[:half_tokens].reshape(local_len, batch_rows, width_model)
    tgt_rows = fetched[half_tokens:].reshape(local_len, batch_rows, width_model)
    hidden, src_back = jax.vjp(embed_norm, src_rows, norm_gains[0])
    hidden, enc_attn = attention_forward(
        hidden, norm_gains[1], enc_qkv, enc_out, src_segs, False, factor
    )
    hidden, enc_ffn = ffn_forward(hidden, norm_gains[2], enc_up, enc_down)
    memory, memory_back = jax.vjp(layer_norm, hidden, norm_gains[3])
    memory_low = memory.astype(jnp.bfloat16)
    memory_full = gather_inputs(memory_low)
    dec_state, tgt_back = jax.vjp(embed_norm, tgt_rows, norm_gains[4])
    dec_state, dec_attn = attention_forward(
        dec_state, norm_gains[5], dec_qkv, dec_out, tgt_segs, True, factor
    )
    dec_state, dec_cross = cross_forward(
        dec_state,
        norm_gains[6],
        memory_full,
        cross_q,
        cross_kv,
        cross_out,
        tgt_segs,
        src_segs,
        factor,
    )
    dec_state, dec_ffn = ffn_forward(dec_state, norm_gains[7], dec_up, dec_down)
    final_norm, final_back = jax.vjp(layer_norm, dec_state, norm_gains[8])
    live_target = tgt_live[..., None].astype(jnp.float32)
    decoded = final_norm * live_target
    grad_state, gain_final = final_back(cotangent * live_target)
    grad_state, gain_dffn, dec_up_grad, dec_down_grad = ffn_backward(
        grad_state, dec_ffn, dec_up, dec_down
    )
    grad_state, gain_cross, grad_memory, cross_q_grad, cross_kv_grad, cross_out_grad = (
        cross_backward(
            grad_state,
            dec_cross,
            memory_low,
            cross_q,
            cross_kv,
            cross_out,
            tgt_segs,
            src_segs,
            factor,
        )
    )
    grad_state, gain_dattn, dec_qkv_grad, dec_out_grad = attention_backward(
        grad_state, dec_attn, dec_qkv, dec_out, tgt_segs, True, factor
    )
    grad_tgt_rows, gain_demb = tgt_back(grad_state)
    grad_hidden, gain_memory = memory_back(grad_memory)
    grad_hidden, gain_effn, enc_up_grad, enc_down_grad = ffn_backward(
        grad_hidden, enc_ffn, enc_up, enc_down
    )
    grad_hidden, gain_eattn, enc_qkv_grad, enc_out_grad = attention_backward(
        grad_hidden, enc_attn, enc_qkv, enc_out, src_segs, False, factor
    )
    grad_src_rows, gain_eemb = src_back(grad_hidden)
    grad_tokens = jnp.concatenate(
        [
            grad_src_rows.reshape(half_tokens, width_model),
            grad_tgt_rows.reshape(half_tokens, width_model),
        ]
    )
    table_grad = table_gradient(grad_tokens, route_info, embed_table.shape[0])
    gain_parts = jnp.stack(
        [
            gain_eemb,
            gain_eattn,
            gain_effn,
            gain_memory,
            gain_demb,
            gain_dattn,
            gain_cross,
            gain_dffn,
            gain_final,
        ]
    )
    gain_grad = lax.psum(gain_parts, ("dp", "tensor"))
    summed_grads = (
        lax.psum_scatter(
            enc_qkv_grad.astype(jnp.bfloat16), "dp", scatter_dimension=1, tiled=True
        ).astype(jnp.float32),
        lax.psum_scatter(
            enc_out_grad.astype(jnp.bfloat16), "dp", scatter_dimension=1, tiled=True
        ).astype(jnp.float32),
        lax.psum_scatter(
            enc_up_grad.astype(jnp.bfloat16), "dp", scatter_dimension=0, tiled=True
        ).astype(jnp.float32),
        lax.psum_scatter(
            enc_down_grad.astype(jnp.bfloat16), "dp", scatter_dimension=1, tiled=True
        ).astype(jnp.float32),
        lax.psum_scatter(
            dec_qkv_grad.astype(jnp.bfloat16), "dp", scatter_dimension=1, tiled=True
        ).astype(jnp.float32),
        lax.psum_scatter(
            dec_out_grad.astype(jnp.bfloat16), "dp", scatter_dimension=1, tiled=True
        ).astype(jnp.float32),
        lax.psum_scatter(
            cross_q_grad.astype(jnp.bfloat16), "dp", scatter_dimension=0, tiled=True
        ).astype(jnp.float32),
        lax.psum_scatter(
            cross_kv_grad.astype(jnp.bfloat16), "dp", scatter_dimension=1, tiled=True
        ).astype(jnp.float32),
        lax.psum_scatter(
            cross_out_grad.astype(jnp.bfloat16), "dp", scatter_dimension=1, tiled=True
        ).astype(jnp.float32),
        lax.psum_scatter(
            dec_up_grad.astype(jnp.bfloat16), "dp", scatter_dimension=0, tiled=True
        ).astype(jnp.float32),
        lax.psum_scatter(
            dec_down_grad.astype(jnp.bfloat16), "dp", scatter_dimension=1, tiled=True
        ).astype(jnp.float32),
    )
    return (
        decoded,
        table_grad,
        gain_grad,
        summed_grads[0],
        summed_grads[1],
        summed_grads[2],
        summed_grads[3],
        summed_grads[4],
        summed_grads[5],
        summed_grads[6],
        summed_grads[7],
        summed_grads[8],
        summed_grads[9],
        summed_grads[10],
    )


def solution(mesh):
    return jax.shard_map(
        on_device,
        mesh=mesh,
        in_specs=(
            P("tensor", "dp"),
            P("tensor", "dp"),
            P(None, "dp"),
            P(None, "dp"),
            P(("dp", "tensor"), None),
            P(),
            P(None, None, "tensor"),
            P("tensor", None),
            P(None, "tensor"),
            P("tensor", None),
            P(None, None, "tensor"),
            P("tensor", None),
            P(None, "tensor"),
            P(None, None, "tensor"),
            P("tensor", None),
            P(None, "tensor"),
            P("tensor", None),
            P("tensor", "dp", None),
        ),
        out_specs=(
            P("tensor", "dp", None),
            P(("dp", "tensor"), None),
            P(),
            P(None, "dp", "tensor"),
            P("tensor", "dp"),
            P("dp", "tensor"),
            P("tensor", "dp"),
            P(None, "dp", "tensor"),
            P("tensor", "dp"),
            P("dp", "tensor"),
            P(None, "dp", "tensor"),
            P("tensor", "dp"),
            P("dp", "tensor"),
            P("tensor", "dp"),
        ),
        check_vma=False,
    )
```

profile of v0, /device:TPU:0, one launch (start us, length us, event | category | flops | bytes accessed | tf_op | source)
XLA Modules:
  0.0 1835.5 jit_solution(764004514226483896)
XLA Ops:
  14.3 7.9 all_to_all.30
  22.2 12.2 all_to_all.31
  35.2 7.2 gather_fusion
  43.2 14.2 all_to_all.32
  58.9 3.5 all-to-all-start.3
  63.2 19.4 %all-to-all-done.3 = bf16[4,8,12,1024]{3,0,2,1:T(4,128)(2,1)S(1)} async-done(((bf16[4,8,12,1024]{3,0,2,1:T(4,128)(2,1)}), bf16[4,8,12,1024]{3,0,2,1:T(4,128)(2,1)S(1)}, u32[]{:S(2)}, u32[]{:S(2)}) %all-to-all-start.3) | async-done | bytes 786464 | tf_op jit(solution)/shard_map/all_to_all | solution.py:364
  92.8 3.8 fusion.78
  96.6 40.2 %all-gather.32.cloned.1.call-done = bf16[1024,1024]{1,0:T(8,128)(2,1)} async-done(((bf16[128,1024]{1,0:T(8,128)(2,1)}), bf16[1024,1024]{1,0:T(8,128)(2,1)}) %all-gather.32.cloned.1.call-update) | async-done | bytes 2097168 | tf_op jit(solution)/shard_map/all_gather | solution.py:150
  139.8 5.0 fusion.318
  144.8 3.6 fusion.317
  157.2 30.1 %all-gather.34.cloned.1.call-done = bf16[1024,1024]{1,0:T(8,128)(2,1)} async-done(((bf16[128,1024]{1,0:T(8,128)(2,1)}), bf16[1024,1024]{1,0:T(8,128)(2,1)}) %all-gather.34.cloned.1.call-update) | async-done | bytes 2097168 | tf_op jit(solution)/shard_map/all_gather | solution.py:150
  190.3 4.9 fusion.316
  195.2 3.6 fusion.315
  206.1 50.9 %reduce-scatter.23.cloned.1.call-done = bf16[128,1,1024]{2,0,1:T(8,128)(2,1)} async-done(((bf16[1024,1,1024]{2,0,1:T(8,128)(2,1)}), bf16[128,1,1024]{2,0,1:T(8,128)(2,1)}) %reduce-scatter.23.cloned.1.call-update) | async-done | bytes 262160 | tf_op jit(solution)/shard_map/reduce_scatter | solution.py:158
  257.0 70.0 %reduce-scatter.25.cloned.1.call-done = bf16[128,1,1024]{2,0,1:T(8,128)(2,1)} async-done(((bf16[1024,1,1024]{2,0,1:T(8,128)(2,1)}), bf16[128,1,1024]{2,0,1:T(8,128)(2,1)}) %reduce-scatter.25.cloned.1.call-update) | async-done | bytes 262160 | tf_op jit(solution)/shard_map/reduce_scatter | solution.py:158
  329.6 48.4 %all-gather.14.cloned.1.call-done = bf16[1024,1,1024]{2,0,1:T(8,128)(2,1)} async-done(((bf16[128,1,1024]{2,0,1:T(8,128)(2,1)}), bf16[1024,1,1024]{2,0,1:T(8,128)(2,1)}) %all-gather.14.cloned.1.call-update) | async-done | bytes 2097168 | tf_op jit(solution)/shard_map/all_gather | solution.py:150
  378.0 8.3 multiply_convert_fusion.7
  391.2 65.1 %reduce-scatter.27.cloned.1.call-done = bf16[128,1,1024]{2,0,1:T(8,128)(2,1)} async-done(((bf16[1024,1,1024]{2,0,1:T(8,128)(2,1)}), bf16[128,1,1024]{2,0,1:T(8,128)(2,1)}) %reduce-scatter.27.cloned.1.call-update) | async-done | bytes 262160 | tf_op jit(solution)/shard_map/reduce_scatter | solution.py:158
  460.0 47.3 %all-gather.18.cloned.1.call-done = bf16[1024,1,1024]{2,0,1:T(8,128)(2,1)} async-done(((bf16[128,1,1024]{2,0,1:T(8,128)(2,1)}), bf16[1024,1,1024]{2,0,1:T(8,128)(2,1)}) %all-gather.18.cloned.1.call-update) | async-done | bytes 2097168 | tf_op jit(solution)/shard_map/all_gather | solution.py:150
  509.8 48.0 %all-gather.16.cloned.1.call-done = bf16[1024,1,1024]{2,0,1:T(8,128)(2,1)} async-done(((bf16[128,1,1024]{2,0,1:T(8,128)(2,1)}), bf16[1024,1,1024]{2,0,1:T(8,128)(2,1)}) %all-gather.16.cloned.1.call-update) | async-done | bytes 2097168 | tf_op jit(solution)/shard_map/all_gather | solution.py:150
  560.3 4.8 fusion.320
  565.1 4.6 fusion.319
  576.3 66.2 %reduce-scatter.29.cloned.1.call-done = bf16[128,1,1024]{2,0,1:T(8,128)(2,1)} async-done(((bf16[1024,1,1024]{2,0,1:T(8,128)(2,1)}), bf16[128,1,1024]{2,0,1:T(8,128)(2,1)}) %reduce-scatter.29.cloned.1.call-update) | async-done | bytes 262160 | tf_op jit(solution)/shard_map/reduce_scatter | solution.py:158
  645.9 48.4 %all-gather.20.cloned.1.call-done = bf16[1024,1,1024]{2,0,1:T(8,128)(2,1)} async-done(((bf16[128,1,1024]{2,0,1:T(8,128)(2,1)}), bf16[1024,1,1024]{2,0,1:T(8,128)(2,1)}) %all-gather.20.cloned.1.call-update) | async-done | bytes 2097168 | tf_op jit(solution)/shard_map/all_gather | solution.py:150
  694.3 8.5 multiply_convert_fusion.6
  706.4 66.3 %reduce-scatter.31.cloned.1.call-done = bf16[128,1,1024]{2,0,1:T(8,128)(2,1)} async-done(((bf16[1024,1,1024]{2,0,1:T(8,128)(2,1)}), bf16[128,1,1024]{2,0,1:T(8,128)(2,1)}) %reduce-scatter.31.cloned.1.call-update) | async-done | bytes 262160 | tf_op jit(solution)/shard_map/reduce_scatter | solution.py:158
  778.8 48.2 %all-gather.22.cloned.1.call-done = bf16[1024,1,1024]{2,0,1:T(8,128)(2,1)} async-done(((bf16[128,1,1024]{2,0,1:T(8,128)(2,1)}), bf16[1024,1,1024]{2,0,1:T(8,128)(2,1)}) %all-gather.22.cloned.1.call-update) | async-done | bytes 2097168 | tf_op jit(solution)/shard_map/all_gather | solution.py:154
  827.0 5.0 add_convert_fusion.1
  835.7 66.1 %reduce-scatter.33.cloned.1.call-done = bf16[128,1,1024]{2,0,1:T(8,128)(2,1)} async-done(((bf16[1024,1,1024]{2,0,1:T(8,128)(2,1)}), bf16[128,1,1024]{2,0,1:T(8,128)(2,1)}) %reduce-scatter.33.cloned.1.call-update) | async-done | bytes 262160 | tf_op jit(solution)/shard_map/reduce_scatter | solution.py:167
  906.9 48.4 %all-gather.24.cloned.1.call-done = bf16[1024,1,1024]{2,0,1:T(8,128)(2,1)} async-done(((bf16[128,1,1024]{2,0,1:T(8,128)(2,1)}), bf16[1024,1,1024]{2,0,1:T(8,128)(2,1)}) %all-gather.24.cloned.1.call-update) | async-done | bytes 2097168 | tf_op jit(solution)/shard_map/all_gather | solution.py:154
  964.5 3.4 multiply_reduce_fusion.4
  968.7 4.2 multiply_convert_fusion.5
  989.0 59.2 %reduce-scatter.35.cloned.1.call-done = bf16[128,1,1024]{2,0,1:T(8,128)(2,1)} async-done(((bf16[1024,1,1024]{2,0,1:T(8,128)(2,1)}), bf16[128,1,1024]{2,0,1:T(8,128)(2,1)}) %reduce-scatter.35.cloned.1.call-update) | async-done | bytes 262160 | tf_op jit(solution)/shard_map/reduce_scatter | solution.py:167
  1052.1 66.3 %reduce-scatter.41.cloned.1.call-done = bf16[128,1,1024]{2,0,1:T(8,128)(2,1)} async-done(((bf16[1024,1,1024]{2,0,1:T(8,128)(2,1)}), bf16[128,1,1024]{2,0,1:T(8,128)(2,1)}) %reduce-scatter.41.cloned.1.call-update) | async-done | bytes 262160 | tf_op jit(solution)/shard_map/reduce_scatter | solution.py:167
  1121.8 47.6 %all-gather.26.cloned.1.call-done = bf16[1024,1,1024]{2,0,1:T(8,128)(2,1)} async-done(((bf16[128,1,1024]{2,0,1:T(8,128)(2,1)}), bf16[1024,1,1024]{2,0,1:T(8,128)(2,1)}) %all-gather.26.cloned.1.call-update) | async-done | bytes 2097168 | tf_op jit(solution)/shard_map/all_gather | solution.py:154
  1169.4 5.1 add_convert_fusion
  1178.2 41.5 %all-gather.30.cloned.1.call-done = bf16[1024,1,1024]{2,0,1:T(8,128)(2,1)} async-done(((bf16[128,1,1024]{2,0,1:T(8,128)(2,1)}), bf16[1024,1,1024]{2,0,1:T(8,128)(2,1)}) %all-gather.30.cloned.1.call-update) | async-done | bytes 2097168 | tf_op jit(solution)/shard_map/all_gather | solution.py:154
  1228.5 61.0 %reduce-scatter.37.cloned.1.call-done = bf16[128,1,1024]{2,0,1:T(8,128)(2,1)} async-done(((bf16[1024,1,1024]{2,0,1:T(8,128)(2,1)}), bf16[128,1,1024]{2,0,1:T(8,128)(2,1)}) %reduce-scatter.37.cloned.1.call-update) | async-done | bytes 262160 | tf_op jit(solution)/shard_map/reduce_scatter | solution.py:167
  1296.6 4.3 multiply_convert_fusion.1
  1309.6 3.8 fusion.87
  1313.7 27.7 %all-gather.28.cloned.1.call-done = bf16[1024,1,1024]{2,0,1:T(8,128)(2,1)} async-done(((bf16[128,1,1024]{2,0,1:T(8,128)(2,1)}), bf16[1024,1,1024]{2,0,1:T(8,128)(2,1)}) %all-gather.28.cloned.1.call-update) | async-done | bytes 2097168 | tf_op jit(solution)/shard_map/all_gather | solution.py:154
  1363.2 4.0 fusion.86
  1371.2 4.2 fusion.92
  1384.7 3.8 fusion.114
  1391.2 4.2 fusion.89
  1395.5 15.5 reduce-scatter.43.cloned.1.call-done
  1415.1 66.6 %reduce-scatter.39.cloned.1.call-done = bf16[128,1,1024]{2,0,1:T(8,128)(2,1)} async-done(((bf16[1024,1,1024]{2,0,1:T(8,128)(2,1)}), bf16[128,1,1024]{2,0,1:T(8,128)(2,1)}) %reduce-scatter.39.cloned.1.call-update) | async-done | bytes 262160 | tf_op jit(solution)/shard_map/reduce_scatter | solution.py:167
  1491.6 3.5 all-to-all-start.4
  1495.2 3.5 fusion.117
  1498.7 13.6 all-to-all-done.4
  1513.8 3.5 all-to-all-start.5
  1523.9 14.9 reduce-scatter.63.cloned.1.call-done
  1540.6 20.7 %reduce-scatter.61.cloned.1.call-done = bf16[128,256]{1,0:T(8,128)(2,1)} async-done(((bf16[128,1024]{1,0:T(8,128)(2,1)}), bf16[128,256]{1,0:T(8,128)(2,1)}) %reduce-scatter.61.cloned.1.call-update) | async-done | bytes 65552 | tf_op jit(solution)/shard_map/reduce_scatter | solution.py:554
  1562.8 21.0 %reduce-scatter.57.cloned.1.call-done = bf16[256,128]{1,0:T(8,128)(2,1)} async-done(((bf16[1024,128]{1,0:T(8,128)(2,1)}), bf16[256,128]{1,0:T(8,128)(2,1)}) %reduce-scatter.57.cloned.1.call-update) | async-done | bytes 65552 | tf_op jit(solution)/shard_map/reduce_scatter | solution.py:548
  1585.3 22.5 %reduce-scatter.59.cloned.1.call-done = bf16[2,256,128]{1,2,0:T(8,128)(2,1)} async-done(((bf16[2,1024,128]{1,2,0:T(8,128)(2,1)}), bf16[2,256,128]{1,2,0:T(8,128)(2,1)}) %reduce-scatter.59.cloned.1.call-update) | async-done | bytes 131088 | tf_op jit(solution)/shard_map/reduce_scatter | solution.py:551
  1609.6 21.0 %reduce-scatter.55.cloned.1.call-done = bf16[128,256]{1,0:T(8,128)(2,1)} async-done(((bf16[128,1024]{1,0:T(8,128)(2,1)}), bf16[128,256]{1,0:T(8,128)(2,1)}) %reduce-scatter.55.cloned.1.call-update) | async-done | bytes 65552 | tf_op jit(solution)/shard_map/reduce_scatter | solution.py:545
  1632.0 24.3 %reduce-scatter.53.cloned.1.call-done = bf16[3,256,128]{1,2,0:T(8,128)(2,1)} async-done(((bf16[3,1024,128]{1,2,0:T(8,128)(2,1)}), bf16[3,256,128]{1,2,0:T(8,128)(2,1)}) %reduce-scatter.53.cloned.1.call-update) | async-done | bytes 196624 | tf_op jit(solution)/shard_map/reduce_scatter | solution.py:542
  1658.2 25.6 %reduce-scatter.51.cloned.1.call-done = bf16[512,256]{1,0:T(8,128)(2,1)} async-done(((bf16[512,1024]{1,0:T(8,128)(2,1)}), bf16[512,256]{1,0:T(8,128)(2,1)}) %reduce-scatter.51.cloned.1.call-update) | async-done | bytes 262160 | tf_op jit(solution)/shard_map/reduce_scatter | solution.py:539
  1685.6 25.7 %reduce-scatter.49.cloned.1.call-done = bf16[256,512]{1,0:T(8,128)(2,1)} async-done(((bf16[1024,512]{1,0:T(8,128)(2,1)}), bf16[256,512]{1,0:T(8,128)(2,1)}) %reduce-scatter.49.cloned.1.call-update) | async-done | bytes 262160 | tf_op jit(solution)/shard_map/reduce_scatter | solution.py:536
  1713.1 20.8 %reduce-scatter.47.cloned.1.call-done = bf16[128,256]{1,0:T(8,128)(2,1)} async-done(((bf16[128,1024]{1,0:T(8,128)(2,1)}), bf16[128,256]{1,0:T(8,128)(2,1)}) %reduce-scatter.47.cloned.1.call-update) | async-done | bytes 65552 | tf_op jit(solution)/shard_map/reduce_scatter | solution.py:533
  1735.5 24.2 %reduce-scatter.45.cloned.1.call-done = bf16[3,256,128]{1,2,0:T(8,128)(2,1)} async-done(((bf16[3,1024,128]{1,2,0:T(8,128)(2,1)}), bf16[3,256,128]{1,2,0:T(8,128)(2,1)}) %reduce-scatter.45.cloned.1.call-update) | async-done | bytes 196624 | tf_op jit(solution)/shard_map/reduce_scatter | solution.py:530
  1761.5 40.4 %psum.7 = f32[9,1024]{1,0:T(8,128)} all-reduce(f32[9,1024]{1,0:T(8,128)S(1)} %stack.51), channel_id=1, replica_groups=mesh['dp'=4,'tensor'=8] {'dp','tensor'}, use_global_device_ids=true, to_apply=%region_81.82 | all-reduce | flops 9216 | bytes 73728 | tf_op jit(solution)/shard_map/psum | solution.py:528
  1804.6 11.7 scatter_custom_fusion.2
  1816.3 11.9 broadcast_divide_fusion
  (658 shorter events, 226.4 us)
Async XLA Ops:
  7.2 687.1 %copy-start = (bf16[1024,512]{1,0:T(8,128)(2,1)S(1)}, bf16[1024,512]{1,0:T(8,128)(2,1)}, u32[]{:S(2)}) copy-start(bf16[1024,512]{1,0:T(8,128)(2,1)} %param.33) | copy-start | bytes 3145732
  58.9 23.6 %all-to-all-start.3 = ((bf16[4,8,12,1024]{3,0,2,1:T(4,128)(2,1)}), bf16[4,8,12,1024]{3,0,2,1:T(4,128)(2,1)S(1)}, u32[]{:S(2)}, u32[]{:S(2)}) async-start(bf16[4,8,12,1024]{3,0,2,1:T(4,128)(2,1)} %copy.135), calls=%async_computation.3 | async-start | bytes 1572864 | tf_op jit(solution)/shard_map/all_to_all | solution.py:364
  62.5 74.3 %all-gather.32.cloned.1.call-start = ((), (), s32[]{:S(2)}) async-start(), calls=%async_computation.59 | async-start | bytes 2359296 | tf_op jit(solution)/shard_map/all_gather | solution.py:150
  63.2 263.8 %copy-start.95 = (f32[1,1024]{1,0:T(1,128)}, f32[1,1024]{1,0:T(1,128)S(1)}, u32[]{:S(2)}) copy-start(f32[1,1024]{1,0:T(1,128)S(1)} %get-tuple-element.180) | copy-start | bytes 12292
  63.2 263.8 %copy-start.97 = (f32[1,1024]{1,0:T(1,128)}, f32[1,1024]{1,0:T(1,128)S(1)}, u32[]{:S(2)}) copy-start(f32[1,1024]{1,0:T(1,128)S(1)} %get-tuple-element.182) | copy-start | bytes 12292
  86.2 240.7 %copy-start.2 = (f32[256,1024]{1,0:T(8,128)}, f32[256,1024]{1,0:T(8,128)S(1)}, u32[]{:S(2)}) copy-start(f32[256,1024]{1,0:T(8,128)S(1)} %convert_multiply_fusion) | copy-start | bytes 3145732
  86.4 240.6 %copy-start.104 = (f32[128]{0:T(128)}, f32[128]{0:T(128)S(1)}, u32[]{:S(2)}) copy-start(f32[128]{0:T(128)S(1)} %broadcast_multiply_fusion.6) | copy-start | bytes 1540
  86.4 240.6 %copy-start.106 = (f32[128]{0:T(128)}, f32[128]{0:T(128)S(1)}, u32[]{:S(2)}) copy-start(f32[128]{0:T(128)S(1)} %broadcast_multiply_fusion.8) | copy-start | bytes 1540
  86.7 240.3 %copy-start.110 = (f32[128]{0:T(128)}, f32[128]{0:T(128)S(1)}, u32[]{:S(2)}) copy-start(f32[128]{0:T(128)S(1)} %fusion.257) | copy-start | bytes 1540
  86.8 240.2 %copy-start.112 = (f32[128]{0:T(128)}, f32[128]{0:T(128)S(1)}, u32[]{:S(2)}) copy-start(f32[128]{0:T(128)S(1)} %fusion.255) | copy-start | bytes 1540
  89.2 98.1 %all-gather.34.cloned.1.call-start = ((), (), s32[]{:S(2)}) async-start(), calls=%async_computation.60 | async-start | bytes 2359296 | tf_op jit(solution)/shard_map/all_gather | solution.py:150
  92.5 164.5 %reduce-scatter.23.cloned.1.call-start = ((), (), s32[]{:S(2)}) async-start(), calls=%async_computation.28 | async-start | bytes 2359296 | tf_op jit(solution)/shard_map/reduce_scatter | solution.py:158
  155.6 171.4 %reduce-scatter.25.cloned.1.call-start = ((), (), s32[]{:S(2)}) async-start(), calls=%async_computation.29 | async-start | bytes 2359296 | tf_op jit(solution)/shard_map/reduce_scatter | solution.py:158
  206.0 172.0 %all-gather.14.cloned.1.call-start = ((), (), s32[]{:S(2)}) async-start(), calls=%async_computation.30 | async-start | bytes 2359296 | tf_op jit(solution)/shard_map/all_gather | solution.py:150
  329.6 126.7 %reduce-scatter.27.cloned.1.call-start = ((), (), s32[]{:S(2)}) async-start(), calls=%async_computation.31 | async-start | bytes 2359296 | tf_op jit(solution)/shard_map/reduce_scatter | solution.py:158
  390.0 117.3 %all-gather.18.cloned.1.call-start = ((), (), s32[]{:S(2)}) async-start(), calls=%async_computation.33 | async-start | bytes 2359296 | tf_op jit(solution)/shard_map/all_gather | solution.py:150
  391.2 116.2 %copy-start.59 = (bf16[1024,128]{1,0:T(8,128)(2,1)S(1)}, bf16[1024,128]{1,0:T(8,128)(2,1)}, u32[]{:S(2)}) copy-start(bf16[1024,128]{1,0:T(8,128)(2,1)} %param.30) | copy-start | bytes 786436
  391.2 166.6 %all-gather.16.cloned.1.call-start = ((), (), s32[]{:S(2)}) async-start(), calls=%async_computation.32 | async-start | bytes 2359296 | tf_op jit(solution)/shard_map/all_gather | solution.py:150
  458.5 184.0 %reduce-scatter.29.cloned.1.call-start = ((), (), s32[]{:S(2)}) async-start(), calls=%async_computation.34 | async-start | bytes 2359296 | tf_op jit(solution)/shard_map/reduce_scatter | solution.py:158
  576.3 118.0 %all-gather.20.cloned.1.call-start = ((), (), s32[]{:S(2)}) async-start(), calls=%async_computation.35 | async-start | bytes 2359296 | tf_op jit(solution)/shard_map/all_gather | solution.py:150
  645.8 127.0 %reduce-scatter.31.cloned.1.call-start = ((), (), s32[]{:S(2)}) async-start(), calls=%async_computation.36 | async-start | bytes 2359296 | tf_op jit(solution)/shard_map/reduce_scatter | solution.py:158
  706.4 120.6 %all-gather.22.cloned.1.call-start = ((), (), s32[]{:S(2)}) async-start(), calls=%async_computation.37 | async-start | bytes 2359296 | tf_op jit(solution)/shard_map/all_gather | solution.py:154
  778.5 123.3 %reduce-scatter.33.cloned.1.call-start = ((), (), s32[]{:S(2)}) async-start(), calls=%async_computation.38 | async-start | bytes 2359296 | tf_op jit(solution)/shard_map/reduce_scatter | solution.py:167
  835.7 119.7 %all-gather.24.cloned.1.call-start = ((), (), s32[]{:S(2)}) async-start(), calls=%async_computation.39 | async-start | bytes 2359296 | tf_op jit(solution)/shard_map/all_gather | solution.py:154
  906.8 214.0 %copy-start.20 = (f32[128,1,1024]{2,0,1:T(8,128)}, f32[128,1,1024]{2,0,1:T(8,128)S(1)}, u32[]{:S(2)}) copy-start(f32[128,1,1024]{2,0,1:T(8,128)S(1)} %get-tuple-element.121) | copy-start | bytes 1572868
  906.9 141.4 %reduce-scatter.35.cloned.1.call-start = ((), (), s32[]{:S(2)}) async-start(), calls=%async_computation.40 | async-start | bytes 2359296 | tf_op jit(solution)/shard_map/reduce_scatter | solution.py:167
  982.0 136.4 %reduce-scatter.41.cloned.1.call-start = ((), (), s32[]{:S(2)}) async-start(), calls=%async_computation.45 | async-start | bytes 2359296 | tf_op jit(solution)/shard_map/reduce_scatter | solution.py:167
  988.9 129.4 %copy-start.122 = (f32[128]{0:T(128)S(1)}, f32[128]{0:T(128)}, u32[]{:S(2)}) copy-start(f32[128]{0:T(128)} %copy-done.121) | copy-start | bytes 1540
  989.0 129.4 %copy-start.132 = (f32[128]{0:T(128)S(1)}, f32[128]{0:T(128)}, u32[]{:S(2)}) copy-start(f32[128]{0:T(128)} %copy-done.131) | copy-start | bytes 1540
  989.0 130.6 %copy-start.166 = (f32[128]{0:T(128)S(1)}, f32[128]{0:T(128)}, u32[]{:S(2)}) copy-start(f32[128]{0:T(128)} %copy-done.165) | copy-start | bytes 1540
  989.0 180.4 %all-gather.26.cloned.1.call-start = ((), (), s32[]{:S(2)}) async-start(), calls=%async_computation.41 | async-start | bytes 2359296 | tf_op jit(solution)/shard_map/all_gather | solution.py:154
  1050.7 241.3 %copy-start.14 = (f32[128,1,1024]{2,0,1:T(8,128)}, f32[128,1,1024]{2,0,1:T(8,128)S(1)}, u32[]{:S(2)}) copy-start(f32[128,1,1024]{2,0,1:T(8,128)S(1)} %get-tuple-element.115) | copy-start | bytes 1572868
  1050.7 241.2 %copy-start.135 = (f32[128]{0:T(128)}, f32[128]{0:T(128)S(1)}, u32[]{:S(2)}) copy-start(f32[128]{0:T(128)S(1)} %negate_multiply_fusion.8) | copy-start | bytes 1540
  1051.6 168.1 %all-gather.30.cloned.1.call-start = ((), (), s32[]{:S(2)}) async-start(), calls=%async_computation.46 | async-start | bytes 2359296 | tf_op jit(solution)/shard_map/all_gather | solution.py:154
  1121.8 167.7 %reduce-scatter.37.cloned.1.call-start = ((), (), s32[]{:S(2)}) async-start(), calls=%async_computation.42 | async-start | bytes 2359296 | tf_op jit(solution)/shard_map/reduce_scatter | solution.py:167
  1178.1 163.2 %all-gather.28.cloned.1.call-start = ((), (), s32[]{:S(2)}) async-start(), calls=%async_computation.43 | async-start | bytes 2359296 | tf_op jit(solution)/shard_map/all_gather | solution.py:154
  1292.9 118.1 %reduce-scatter.43.cloned.1.call-start = ((), (), s32[]{:S(2)}) async-start(), calls=%async_computation.47 | async-start | bytes 2359296 | tf_op jit(solution)/shard_map/reduce_scatter | solution.py:167
  1313.4 168.2 %reduce-scatter.39.cloned.1.call-start = ((), (), s32[]{:S(2)}) async-start(), calls=%async_computation.44 | async-start | bytes 2359296 | tf_op jit(solution)/shard_map/reduce_scatter | solution.py:167
  1367.2 154.9 %reduce-scatter.65.cloned.1.call-start = ((), (), s32[]{:S(2)}) async-start(), calls=%async_computation.58 | async-start | bytes 1310720 | tf_op jit(solution)/shard_map/reduce_scatter | solution.py:560
  1371.1 167.7 %reduce-scatter.63.cloned.1.call-start = ((), (), s32[]{:S(2)}) async-start(), calls=%async_computation.57 | async-start | bytes 1310720 | tf_op jit(solution)/shard_map/reduce_scatter | solution.py:557
  1375.4 185.9 %reduce-scatter.61.cloned.1.call-start = ((), (), s32[]{:S(2)}) async-start(), calls=%async_computation.56 | async-start | bytes 327680 | tf_op jit(solution)/shard_map/reduce_scatter | solution.py:554
  1378.4 205.4 %reduce-scatter.57.cloned.1.call-start = ((), (), s32[]{:S(2)}) async-start(), calls=%async_computation.54 | async-start | bytes 327680 | tf_op jit(solution)/shard_map/reduce_scatter | solution.py:548
  1380.0 227.9 %reduce-scatter.59.cloned.1.call-start = ((), (), s32[]{:S(2)}) async-start(), calls=%async_computation.55 | async-start | bytes 655360 | tf_op jit(solution)/shard_map/reduce_scatter | solution.py:551
  1383.4 247.1 %reduce-scatter.55.cloned.1.call-start = ((), (), s32[]{:S(2)}) async-start(), calls=%async_computation.53 | async-start | bytes 327680 | tf_op jit(solution)/shard_map/reduce_scatter | solution.py:545
  1384.6 271.7 %reduce-scatter.53.cloned.1.call-start = ((), (), s32[]{:S(2)}) async-start(), calls=%async_computation.52 | async-start | bytes 983040 | tf_op jit(solution)/shard_map/reduce_scatter | solution.py:542
  1388.5 295.3 %reduce-scatter.51.cloned.1.call-start = ((), (), s32[]{:S(2)}) async-start(), calls=%async_computation.51 | async-start | bytes 1310720 | tf_op jit(solution)/shard_map/reduce_scatter | solution.py:539
  1391.1 320.2 %reduce-scatter.49.cloned.1.call-start = ((), (), s32[]{:S(2)}) async-start(), calls=%async_computation.50 | async-start | bytes 1310720 | tf_op jit(solution)/shard_map/reduce_scatter | solution.py:536
  1395.4 86.3 %copy-start.10 = (f32[128,1024]{1,0:T(8,128)S(1)}, f32[128,1024]{1,0:T(8,128)}, u32[]{:S(2)}) copy-start(f32[128,1024]{1,0:T(8,128)} %copy-done.9) | copy-start | bytes 1572868
  1395.4 86.3 %copy-start.102 = (f32[1,1024]{1,0:T(1,128)S(1)}, f32[1,1024]{1,0:T(1,128)}, u32[]{:S(2)}) copy-start(f32[1,1024]{1,0:T(1,128)} %copy-done.101) | copy-start | bytes 12292
  1395.4 87.4 %copy-start.172 = (f32[128]{0:T(128)S(1)}, f32[128]{0:T(128)}, u32[]{:S(2)}) copy-start(f32[128]{0:T(128)} %copy-done.171) | copy-start | bytes 1540
  1395.4 87.4 %copy-start.126 = (f32[128]{0:T(128)S(1)}, f32[128]{0:T(128)}, u32[]{:S(2)}) copy-start(f32[128]{0:T(128)} %copy-done.125) | copy-start | bytes 1540
  1395.4 87.4 %copy-start.128 = (f32[128]{0:T(128)S(1)}, f32[128]{0:T(128)}, u32[]{:S(2)}) copy-start(f32[128]{0:T(128)} %copy-done.127) | copy-start | bytes 1540
  1395.4 338.5 %reduce-scatter.47.cloned.1.call-start = ((), (), s32[]{:S(2)}) async-start(), calls=%async_computation.49 | async-start | bytes 327680 | tf_op jit(solution)/shard_map/reduce_scatter | solution.py:533
  1412.1 72.5 %copy-start.3 = (f32[256,1024]{1,0:T(8,128)S(1)}, f32[256,1024]{1,0:T(8,128)}, u32[]{:S(2)}) copy-start(f32[256,1024]{1,0:T(8,128)} %copy-done.2) | copy-start | bytes 3145732
  1412.1 72.5 %copy-start.19 = (f32[128,1,1024]{2,0,1:T(8,128)S(1)}, f32[128,1,1024]{2,0,1:T(8,128)}, u32[]{:S(2)}) copy-start(f32[128,1,1024]{2,0,1:T(8,128)} %copy-done.18) | copy-start | bytes 1572868
  1412.1 72.5 %copy-start.21 = (f32[128,1,1024]{2,0,1:T(8,128)S(1)}, f32[128,1,1024]{2,0,1:T(8,128)}, u32[]{:S(2)}) copy-start(f32[128,1,1024]{2,0,1:T(8,128)} %copy-done.20) | copy-start | bytes 1572868
  1412.1 72.5 %copy-start.98 = (f32[1,1024]{1,0:T(1,128)S(1)}, f32[1,1024]{1,0:T(1,128)}, u32[]{:S(2)}) copy-start(f32[1,1024]{1,0:T(1,128)} %copy-done.97) | copy-start | bytes 12292
  1412.2 72.5 %copy-start.107 = (f32[128]{0:T(128)S(1)}, f32[128]{0:T(128)}, u32[]{:S(2)}) copy-start(f32[128]{0:T(128)} %copy-done.106) | copy-start | bytes 1540
  1412.2 72.5 %copy-start.154 = (f32[128]{0:T(128)S(1)}, f32[128]{0:T(128)}, u32[]{:S(2)}) copy-start(f32[128]{0:T(128)} %copy-done.153) | copy-start | bytes 1540
  1491.6 20.7 %all-to-all-start.4 = ((bf16[4,8,12,1024]{3,1,2,0:T(8,128)(2,1)}), bf16[4,8,12,1024]{3,1,2,0:T(8,128)(2,1)S(1)}, u32[]{:S(2)}, u32[]{:S(2)}) async-start(bf16[4,8,12,1024]{3,1,2,0:T(8,128)(2,1)} %copy.149), calls=%async_computation.15 | async-start | bytes 1572864 | tf_op jit(solution)/shard_map/all_to_all | solution.py:395
  1495.1 264.5 %reduce-scatter.45.cloned.1.call-start = ((), (), s32[]{:S(2)}) async-start(), calls=%async_computation.48 | async-start | bytes 983040 | tf_op jit(solution)/shard_map/reduce_scatter | solution.py:530
  1513.8 288.1 %all-to-all-start.5 = ((bf16[4,8,12,1024]{3,0,2,1:T(4,128)(2,1)}), bf16[4,8,12,1024]{3,0,2,1:T(4,128)(2,1)S(1)}, u32[]{:S(2)}, u32[]{:S(2)}) async-start(bf16[4,8,12,1024]{3,0,2,1:T(4,128)(2,1)} %copy.150), calls=%async_computation.16 | async-start | bytes 1572864 | tf_op jit(solution)/shard_map/all_to_all | solution.py:394
  1540.6 220.9 %copy-start.114 = (f32[1024]{0:T(1024)S(1)}, f32[1024]{0:T(1024)}, u32[]{:S(2)}) copy-start(f32[1024]{0:T(1024)} %get-tuple-element.88) | copy-start | bytes 12292
  1540.6 220.9 %copy-start.115 = (f32[1024]{0:T(1024)S(1)}, f32[1024]{0:T(1024)}, u32[]{:S(2)}) copy-start(f32[1024]{0:T(1024)} %get-tuple-element.97) | copy-start | bytes 12292
  (152 other events, 2293.8 us)
Sparse Core Ops, SparseCore 0:
  89.3 47.4 all-gather.31
  139.5 47.7 all-gather.33
  190.8 66.0 reduce-scatter.22
  260.4 66.5 reduce-scatter.24
  329.7 48.2 all-gather.13
  390.1 66.1 reduce-scatter.26
  459.0 48.2 all-gather.17
  510.0 47.7 all-gather.15
  576.4 66.0 reduce-scatter.28
  645.9 48.2 all-gather.19
  706.5 66.2 reduce-scatter.30
  778.6 48.2 all-gather.21
  835.8 66.0 reduce-scatter.32
  907.0 48.3 all-gather.23
  982.1 66.0 reduce-scatter.34
  1051.6 66.7 reduce-scatter.40
  1120.9 48.4 all-gather.25
  1171.9 47.7 all-gather.29
  1223.3 66.1 reduce-scatter.36
  1293.0 48.2 all-gather.27
  1344.9 66.0 reduce-scatter.42
  1415.1 66.5 reduce-scatter.38
  1484.2 29.1 reduce-scatter.64
  1515.9 22.8 reduce-scatter.62
  1541.2 20.0 reduce-scatter.60
  1563.8 19.9 reduce-scatter.56
  1586.1 21.6 reduce-scatter.58
  1610.4 20.0 reduce-scatter.54
  1633.1 23.2 reduce-scatter.52
  1658.9 24.8 reduce-scatter.50
  1686.3 24.9 reduce-scatter.48
  1713.9 19.9 reduce-scatter.46
  1736.3 23.2 reduce-scatter.44
where the time goes:
time: 1840 us
  waiting for transfers between devices  1380 us (75%)
  matrix products  187 us (10%)
  other arithmetic  102 us (6%)
  blocking collectives  74.6 us (4%)
  local copies, waits for them, and re-layouts  57.2 us (3%)
    reduce_scatter x6, waiting for transfers between devices, sum_inputs(): lax.psum_scatter(term_fn(jnp.int32(0), lax.axis_size('tensor') * row_coun...  335 us
    reduce_scatter x5, waiting for transfers between devices, sum_outputs(): lax.psum_scatter(term_fn(jnp.int32(0), lax.axis_size('tensor') * row_coun...  318 us
    all_gather x6, waiting for transfers between devices, gather_inputs(): return lax.all_gather(local_rows, 'tensor', axis=0, tiled=True)  262 us
    all_gather x5, waiting for transfers between devices, gather_grads(): return lax.all_gather(local_grad, 'tensor', axis=0, tiled=True)  213 us
    psum x1, blocking collectives, on_device(): gain_grad = lax.psum(gain_parts, ('dp', 'tensor'))  40.4 us
  transfers between devices with their start and end apart: 36, of which 34 were waited for; matrix products, arithmetic and copies ran while one was open for 10% of the time, Pallas kernels for 0%

commit v1 on v0

v1 whole, which is shorter than its diff:
```python
import math
from functools import partial

import jax
import jax.numpy as jnp
from jax import lax
from jax.experimental import pallas as pl
from jax.experimental.pallas import tpu as pltpu
from jax.sharding import PartitionSpec as P

HEAD_DIM = 64
FACTOR = 0.125

NORM_EPS = 1e-05
MASKED = -1e30
F32 = jnp.float32
BF16 = jnp.bfloat16
VMEM_LIMIT = 48 << 20


def layer_norm(values, gain_row):
    centre = jnp.mean(values, axis=-1, keepdims=True)
    shifted = values - centre
    spread = jnp.mean(shifted * shifted, axis=-1, keepdims=True)
    return shifted * lax.rsqrt(spread + NORM_EPS) * gain_row


def embed_norm(token_rows, gain_row):
    return layer_norm(token_rows * math.sqrt(token_rows.shape[-1]), gain_row)


def gelu_pair(pre_act):
    phi_big = 0.5 * (1.0 + lax.erf(pre_act * (1.0 / math.sqrt(2.0))))
    phi_small = jnp.exp(-0.5 * pre_act * pre_act) * (1.0 / math.sqrt(2.0 * math.pi))
    return pre_act * phi_big, phi_big + pre_act * phi_small


def dot(lhs, rhs, dims):
    return lax.dot_general(lhs, rhs, (dims, ((), ())), preferred_element_type=F32)


NN = ((1,), (0,))
NT = ((1,), (1,))
TN = ((0,), (0,))


def allowed_block(seg_query, seg_key, pos_query, pos_key, causal):
    allowed = (seg_key == seg_query) | (seg_query < 0)
    if causal:
        allowed = allowed & (pos_query >= pos_key)
    return allowed


def attn_fwd_kernel(q_ref, k_ref, v_ref, sq_ref, sk_ref, pq_ref, pk_ref, o_ref, st_ref, *, causal, heads):
    allowed = allowed_block(sq_ref[...], sk_ref[...], pq_ref[...], pk_ref[...], causal)
    for head in range(heads):
        cols = slice(head * HEAD_DIM, (head + 1) * HEAD_DIM)
        scores = dot(k_ref[:, cols], q_ref[:, cols], NT)
        scores = jnp.where(allowed, scores, MASKED)
        peak = jnp.max(scores, axis=0, keepdims=True)
        raised = jnp.exp(scores - peak)
        inverse = 1.0 / jnp.sum(raised, axis=0, keepdims=True)
        probs = (raised * inverse).astype(BF16)
        mixed = dot(v_ref[:, cols], probs, TN)
        o_ref[:, cols] = mixed.T.astype(BF16)
        st_ref[head : head + 1, :] = peak
        st_ref[heads + head : heads + head + 1, :] = inverse


def attn_bwd_kernel(
    q_ref, k_ref, v_ref, g_ref, sq_ref, sk_ref, pq_ref, pk_ref, st_ref, dq_ref, dk_ref, dv_ref, *, causal, heads
):
    @pl.when(pl.program_id(0) == 0)
    def _():
        dk_ref[...] = jnp.zeros_like(dk_ref)
        dv_ref[...] = jnp.zeros_like(dv_ref)

    allowed = allowed_block(sq_ref[...], sk_ref[...], pq_ref[...], pk_ref[...], causal)
    for head in range(heads):
        cols = slice(head * HEAD_DIM, (head + 1) * HEAD_DIM)
        queries, keys, values, grads = q_ref[:, cols], k_ref[:, cols], v_ref[:, cols], g_ref[:, cols]
        scores = jnp.where(allowed, dot(keys, queries, NT), MASKED)
        probs = jnp.exp(scores - st_ref[head : head + 1, :]) * st_ref[heads + head : heads + head + 1, :]
        grad_probs = dot(values, grads, NT)
        inner = jnp.sum(probs * grad_probs, axis=0, keepdims=True)
        grad_scores = (probs * (grad_probs - inner)).astype(BF16)
        dq_ref[:, cols] = (dot(keys, grad_scores, TN) * FACTOR).T.astype(BF16)
        dk_ref[:, cols] += dot(grad_scores, queries, NN)
        dv_ref[:, cols] += dot(probs.astype(BF16), grads, NN)


def mask_specs(step, keys_len):
    return [
        pl.BlockSpec((1, step), lambda i: (0, i)),
        pl.BlockSpec((keys_len, 1), lambda i: (0, 0)),
        pl.BlockSpec((1, step), lambda i: (0, i)),
        pl.BlockSpec((keys_len, 1), lambda i: (0, 0)),
    ]


def attend(queries, keys, values, marks, causal):
    length, width = queries.shape
    keys_len = keys.shape[0]
    heads = width // HEAD_DIM
    step = min(256, length)
    rows = pl.BlockSpec((step, width), lambda i: (i, 0))
    whole = pl.BlockSpec((keys_len, width), lambda i: (0, 0))
    return pl.pallas_call(
        partial(attn_fwd_kernel, causal=causal, heads=heads),
        grid=(length // step,),
        in_specs=[rows, whole, whole] + mask_specs(step, keys_len),
        out_specs=[rows, pl.BlockSpec((2 * heads, step), lambda i: (0, i))],
        out_shape=[
            jax.ShapeDtypeStruct((length, width), BF16),
            jax.ShapeDtypeStruct((2 * heads, length), F32),
        ],
        compiler_params=pltpu.CompilerParams(vmem_limit_bytes=VMEM_LIMIT),
        cost_estimate=pl.CostEstimate(
            flops=4 * length * keys_len * width, transcendentals=length * keys_len * heads,
            bytes_accessed=4 * (length + keys_len) * width
        ),
        name="attend",
    )(queries, keys, values, *marks)


def attend_back(queries, keys, values, grad_mixed, marks, stats, causal):
    length, width = queries.shape
    keys_len = keys.shape[0]
    heads = width // HEAD_DIM
    step = min(256, length)
    rows = pl.BlockSpec((step, width), lambda i: (i, 0))
    whole = pl.BlockSpec((keys_len, width), lambda i: (0, 0))
    return pl.pallas_call(
        partial(attn_bwd_kernel, causal=causal, heads=heads),
        grid=(length // step,),
        in_specs=[rows, whole, whole, rows]
        + mask_specs(step, keys_len)
        + [pl.BlockSpec((2 * heads, step), lambda i: (0, i))],
        out_specs=[rows, whole, whole],
        out_shape=[
            jax.ShapeDtypeStruct((length, width), BF16),
            jax.ShapeDtypeStruct((keys_len, width), F32),
            jax.ShapeDtypeStruct((keys_len, width), F32),
        ],
        compiler_params=pltpu.CompilerParams(vmem_limit_bytes=VMEM_LIMIT),
        cost_estimate=pl.CostEstimate(
            flops=10 * length * keys_len * width, transcendentals=length * keys_len * heads,
            bytes_accessed=10 * (length + keys_len) * width
        ),
        name="attend_back",
    )(queries, keys, values, grad_mixed, *marks, stats)


class Places:
    def __init__(self):
        self.dp_size = lax.axis_size("dp")
        self.tensor_size = lax.axis_size("tensor")
        self.group = self.tensor_size // 2
        self.dp_index = lax.axis_index("dp")
        tensor_index = lax.axis_index("tensor")
        self.core = self.dp_index % 2
        self.place = tensor_index % self.group

    def swap(self, value):
        pairs = []
        for dp_index in range(self.dp_size):
            for tensor_index in range(self.tensor_size):
                pair, core = divmod(dp_index, 2)
                side, place = divmod(tensor_index, self.group)
                pairs.append(
                    (
                        dp_index * self.tensor_size + tensor_index,
                        (2 * pair + side) * self.tensor_size + core * self.group + place,
                    )
                )
        return lax.ppermute(value, ("dp", "tensor"), pairs)

    def other_core(self, value):
        return lax.ppermute(value, "dp", [(d, d ^ 1) for d in range(self.dp_size)])

    def partner(self, value):
        return lax.ppermute(value, "tensor", [(t, t ^ self.group) for t in range(self.tensor_size)])

    def mate(self, value, offset):
        return lax.ppermute(value, "tensor", [(t, t ^ offset) for t in range(self.tensor_size)])

    def gather(self, block):
        if self.group == 4:
            half = block.shape[0] // 2
            low, high = block[:half], block[half:]
            low_1, high_2 = self.mate(low, 1), self.mate(high, 2)
            high_1, low_2 = self.mate(high, 1), self.mate(low, 2)
            high_3, low_3 = self.mate(high_2, 1), self.mate(low_1, 2)
            return jnp.concatenate([block, low_1, high_1, low_2, high_2, low_3, high_3])
        return jnp.concatenate([block] + [self.mate(block, o) for o in range(1, self.group)])

    def scatter_sum(self, value):
        length = value.shape[0] // self.group
        total = value[:length]
        for offset in range(1, self.group):
            sent = value[offset * length : (offset + 1) * length].astype(BF16)
            total = total + self.mate(sent, offset).astype(F32)
        return total

    def partner_weight(self, stacked):
        rows = stacked.shape[0] // self.dp_size
        share = lax.dynamic_slice_in_dim(stacked, self.dp_index * rows, rows, 0)
        return lax.all_gather(self.partner(share), "dp", axis=0, tiled=True)

    def sum_weight(self, own, other, axis):
        summed = lax.psum_scatter(
            jnp.stack([own.astype(BF16), other.astype(BF16)]), "dp", scatter_dimension=axis + 1, tiled=True
        )
        return summed[0].astype(F32) + self.partner(summed[1]).astype(F32)

    def marks(self, seg_row, seg_key_row):
        length = seg_row.shape[0] // self.tensor_size
        order = self.place ^ jnp.arange(self.group)
        own = self.core * self.group + order
        keys = jnp.concatenate([own, (1 - self.core) * self.group + order])

        def positions(blocks):
            return (blocks[:, None] * length + jnp.arange(length)[None, :]).reshape(-1)

        def segments(row, blocks):
            return jnp.take(row.reshape(-1, length), blocks, axis=0).reshape(-1)

        return (
            segments(seg_row, own)[None, :],
            segments(seg_key_row, keys)[:, None],
            positions(own)[None, :],
            positions(keys)[:, None],
        )


def project(gathered, weights):
    return [dot(gathered, weight, NN).astype(BF16) for weight in weights]


def add_up(terms):
    total = terms[0]
    for term in terms[1:]:
        total = total + term
    return total


def both_cores(places, first, second):
    width = first.shape[1]
    other = places.other_core(jnp.concatenate([first, second], axis=1))
    return jnp.concatenate([first, other[:, :width]]), jnp.concatenate([second, other[:, width:]])


def both_cores_sum(places, first, second):
    width, half = first.shape[1], first.shape[0] // 2
    sent = jnp.concatenate([first[half:].astype(BF16), second[half:].astype(BF16)], axis=1)
    other = places.other_core(sent).astype(F32)
    return (first[:half] + other[:, :width]).astype(BF16), (second[:half] + other[:, width:]).astype(BF16)


def attention_forward(places, hidden, gain_row, qkv, out_weight, marks, causal):
    normed, norm_back = jax.vjp(layer_norm, hidden, gain_row)
    gathered = places.gather(normed.astype(BF16))
    queries, keys, values = project(gathered, qkv)
    queries = queries * jnp.asarray(FACTOR, BF16)
    keys, values = both_cores(places, keys, values)
    mixed, stats = attend(queries, keys, values, marks, causal)
    update = places.scatter_sum(dot(mixed, out_weight, NN))
    return hidden + update, (norm_back, gathered, queries, keys, values, mixed, stats)


def attention_backward(places, grad_hidden, saved, qkv, out_weight, marks, causal):
    norm_back, gathered, queries, keys, values, mixed, stats = saved
    grad_full = places.gather(grad_hidden.astype(BF16))
    grad_mixed = dot(grad_full, out_weight, NT).astype(BF16)
    grad_q, grad_k, grad_v = attend_back(queries, keys, values, grad_mixed, marks, stats, causal)
    grad_k, grad_v = both_cores_sum(places, grad_k, grad_v)
    grads = [grad_q, grad_k, grad_v]
    grad_normed = places.scatter_sum(add_up([dot(g, w, NT) for g, w in zip(grads, qkv)]))
    grad_input, gain_grad = norm_back(grad_normed)
    out_grad = dot(mixed, grad_full, TN)
    qkv_grad = [dot(gathered, g, TN) for g in grads]
    return grad_hidden + grad_input, gain_grad, qkv_grad, out_grad


def cross_forward(places, state, gain_row, memory_full, query_weight, pair, out_weight, marks):
    normed, norm_back = jax.vjp(layer_norm, state, gain_row)
    gathered = places.gather(normed.astype(BF16))
    queries = project(gathered, [query_weight])[0] * jnp.asarray(FACTOR, BF16)
    keys, values = both_cores(places, *project(memory_full, pair))
    mixed, stats = attend(queries, keys, values, marks, False)
    update = places.scatter_sum(dot(mixed, out_weight, NN))
    return state + update, (norm_back, gathered, queries, keys, values, mixed, stats)


def cross_backward(places, grad_state, saved, memory_full, query_weight, pair, out_weight, marks):
    norm_back, gathered, queries, keys, values, mixed, stats = saved
    grad_full = places.gather(grad_state.astype(BF16))
    grad_mixed = dot(grad_full, out_weight, NT).astype(BF16)
    grad_q, grad_k, grad_v = attend_back(queries, keys, values, grad_mixed, marks, stats, False)
    grad_k, grad_v = both_cores_sum(places, grad_k, grad_v)
    grad_memory = places.scatter_sum(dot(grad_k, pair[0], NT) + dot(grad_v, pair[1], NT))
    grad_normed = places.scatter_sum(dot(grad_q, query_weight, NT))
    grad_input, gain_grad = norm_back(grad_normed)
    out_grad = dot(mixed, grad_full, TN)
    query_grad = dot(gathered, grad_q, TN)
    pair_grad = [dot(memory_full, g, TN) for g in (grad_k, grad_v)]
    return grad_state + grad_input, gain_grad, grad_memory, query_grad, pair_grad, out_grad


def ffn_forward(places, hidden, gain_row, ups, downs):
    normed, norm_back = jax.vjp(layer_norm, hidden, gain_row)
    gathered = places.gather(normed.astype(BF16))
    acts, slopes = [], []
    for up in ups:
        act, slope = gelu_pair(dot(gathered, up, NN))
        acts.append(act.astype(BF16))
        slopes.append(slope)
    update = places.scatter_sum(add_up([dot(a, w, NN) for a, w in zip(acts, downs)]))
    return hidden + update, (norm_back, gathered, acts, slopes)


def ffn_backward(places, grad_hidden, saved, ups, downs):
    norm_back, gathered, acts, slopes = saved
    grad_full = places.gather(grad_hidden.astype(BF16))
    grad_pre = [(s * dot(grad_full, w, NT)).astype(BF16) for s, w in zip(slopes, downs)]
    grad_normed = places.scatter_sum(add_up([dot(g, w, NT) for g, w in zip(grad_pre, ups)]))
    grad_input, gain_grad = norm_back(grad_normed)
    down_grads = [dot(a, grad_full, TN) for a in acts]
    up_grads = [dot(gathered, g, TN) for g in grad_pre]
    return grad_hidden + grad_input, gain_grad, up_grads, down_grads


def table_lookup(src_ids, tgt_ids, src_live, tgt_live, embed_table):
    token_ids = jnp.concatenate([src_ids.reshape(-1), tgt_ids.reshape(-1)])
    token_live = jnp.concatenate([src_live.reshape(-1), tgt_live.reshape(-1)])
    shard_rows = embed_table.shape[0]
    size_dp = lax.axis_size("dp")
    size_tensor = lax.axis_size("tensor")
    owners = size_dp * size_tensor
    capacity = max(2, 3 * token_ids.shape[0] // (2 * owners))
    owner_of = token_ids // shard_rows
    row_of = token_ids - owner_of * shard_rows
    owner_flags = ((owner_of[:, None] == jnp.arange(owners)[None, :]) & token_live[:, None]).astype(
        jnp.int32
    )
    earlier = jnp.cumsum(owner_flags, axis=0) - owner_flags
    ranking = jnp.sum(earlier * owner_flags, axis=1)
    slot_of = jnp.where(token_live, owner_of * capacity + ranking, owners * capacity)
    requests = jnp.full((owners * capacity,), -1, jnp.int32).at[slot_of].set(row_of, mode="drop")
    wanted = lax.all_to_all(
        lax.all_to_all(
            requests.reshape(size_dp, size_tensor, capacity),
            "dp",
            split_axis=0,
            concat_axis=0,
            tiled=True,
        ),
        "tensor",
        split_axis=1,
        concat_axis=1,
        tiled=True,
    ).reshape(-1)
    found_rows = wanted >= 0
    picked = jnp.take(embed_table, jnp.where(found_rows, wanted, 0), axis=0)
    picked = jnp.where(found_rows[:, None], picked, jnp.zeros_like(picked))
    replies = lax.all_to_all(
        lax.all_to_all(
            picked.reshape(size_dp, size_tensor, capacity, -1),
            "dp",
            split_axis=0,
            concat_axis=0,
            tiled=True,
        ),
        "tensor",
        split_axis=1,
        concat_axis=1,
        tiled=True,
    )
    replies = replies.reshape(owners * capacity, -1)
    fetched = jnp.take(replies, jnp.minimum(slot_of, owners * capacity - 1), axis=0).astype(
        jnp.float32
    )
    fetched = fetched * token_live[:, None].astype(jnp.float32)
    return (fetched, (slot_of, wanted, found_rows, size_dp, size_tensor, capacity))


def table_gradient(grad_tokens, route_info, shard_rows):
    slot_of, wanted, found_rows, size_dp, size_tensor, capacity = route_info
    owners = size_dp * size_tensor
    width_model = grad_tokens.shape[1]
    outgoing = (
        jnp.zeros((owners * capacity, width_model), jnp.float32)
        .at[slot_of]
        .set(grad_tokens, mode="drop")
    )
    arrived = lax.all_to_all(
        lax.all_to_all(
            outgoing.reshape(size_dp, size_tensor, capacity, width_model).astype(jnp.bfloat16),
            "dp",
            split_axis=0,
            concat_axis=0,
            tiled=True,
        ),
        "tensor",
        split_axis=1,
        concat_axis=1,
        tiled=True,
    ).astype(jnp.float32)
    arrived = arrived.reshape(owners * capacity, width_model)
    target_rows = jnp.where(found_rows, wanted, shard_rows)
    summed = (
        jnp.zeros((shard_rows, width_model), jnp.float32).at[target_rows].add(arrived, mode="drop")
    )
    counted = (
        jnp.zeros((shard_rows,), jnp.float32)
        .at[target_rows]
        .add(jnp.ones(target_rows.shape, jnp.float32), mode="drop")
    )
    return summed / jnp.maximum(counted, 1.0)[:, None]


def on_device(
    src_ids,
    tgt_ids,
    src_segs,
    tgt_segs,
    embed_table,
    norm_gains,
    enc_qkv,
    enc_out,
    enc_up,
    enc_down,
    dec_qkv,
    dec_out,
    cross_q,
    cross_kv,
    cross_out,
    dec_up,
    dec_down,
    cotangent,
):
    places = Places()
    local_len = src_ids.shape[0]
    width_model = embed_table.shape[1]
    moved = places.swap(
        jnp.concatenate([src_ids.reshape(-1), tgt_ids.reshape(-1), src_segs.reshape(-1), tgt_segs.reshape(-1)])
    )
    src_ids, tgt_ids = moved[:local_len], moved[local_len : 2 * local_len]
    src_row, tgt_row = jnp.split(moved[2 * local_len :], 2)
    offset = (places.core * places.group + places.place) * local_len
    src_live = lax.dynamic_slice_in_dim(src_row, offset, local_len, 0) >= 0
    tgt_live = lax.dynamic_slice_in_dim(tgt_row, offset, local_len, 0) >= 0
    enc_marks = places.marks(src_row, src_row)
    dec_marks = places.marks(tgt_row, tgt_row)
    cross_marks = places.marks(tgt_row, src_row)
    cotangent = places.swap(cotangent.reshape(local_len, width_model))

    shard = enc_qkv.shape[2]
    hidden_shard = enc_up.shape[1]
    narrow = [enc_qkv.reshape(-1, shard), dec_qkv.reshape(-1, shard), cross_q, cross_kv.reshape(-1, shard)]
    narrow_other = places.partner_weight(jnp.concatenate(narrow)).reshape(-1, width_model, shard)
    narrow_own = jnp.concatenate([enc_qkv, dec_qkv, cross_q[None], cross_kv])
    count = narrow_own.shape[0]
    wide = [jnp.concatenate([narrow_own[i], narrow_other[i]], axis=1) for i in range(count)]
    enc_qkv_both, dec_qkv_both, cross_q_both, cross_kv_both = wide[:3], wide[3:6], wide[6], wide[7:9]
    outs_other = places.partner_weight(jnp.concatenate([enc_out, dec_out, cross_out])).reshape(3, shard, -1)
    enc_out_both, dec_out_both, cross_out_both = [
        jnp.concatenate([own, outs_other[i]]) for i, own in enumerate([enc_out, dec_out, cross_out])
    ]
    enc_up_other = places.partner_weight(enc_up)
    enc_down_other = places.partner_weight(enc_down)
    dec_up_other = places.partner_weight(dec_up)
    dec_down_other = places.partner_weight(dec_down)
    enc_ups, enc_downs = [enc_up, enc_up_other], [enc_down, enc_down_other]
    dec_ups, dec_downs = [dec_up, dec_up_other], [dec_down, dec_down_other]

    fetched, route_info = table_lookup(src_ids, tgt_ids, src_live, tgt_live, embed_table)
    src_rows, tgt_rows = fetched[:local_len], fetched[local_len:]
    hidden, src_back = jax.vjp(embed_norm, src_rows, norm_gains[0])
    hidden, enc_attn = attention_forward(
        places, hidden, norm_gains[1], enc_qkv_both, enc_out_both, enc_marks, False
    )
    hidden, enc_ffn = ffn_forward(places, hidden, norm_gains[2], enc_ups, enc_downs)
    memory, memory_back = jax.vjp(layer_norm, hidden, norm_gains[3])
    memory_full = places.gather(memory.astype(BF16))
    state, tgt_back = jax.vjp(embed_norm, tgt_rows, norm_gains[4])
    state, dec_attn = attention_forward(
        places, state, norm_gains[5], dec_qkv_both, dec_out_both, dec_marks, True
    )
    state, dec_cross = cross_forward(
        places, state, norm_gains[6], memory_full, cross_q_both, cross_kv_both, cross_out_both, cross_marks
    )
    state, dec_ffn = ffn_forward(places, state, norm_gains[7], dec_ups, dec_downs)
    final_norm, final_back = jax.vjp(layer_norm, state, norm_gains[8])
    live_target = tgt_live[:, None].astype(F32)
    decoded = places.swap(final_norm * live_target)

    grad_state, gain_final = final_back(cotangent * live_target)
    grad_state, gain_dffn, dec_up_grad, dec_down_grad = ffn_backward(
        places, grad_state, dec_ffn, dec_ups, dec_downs
    )
    grad_state, gain_cross, grad_memory, cross_q_grad, cross_kv_grad, cross_out_grad = cross_backward(
        places, grad_state, dec_cross, memory_full, cross_q_both, cross_kv_both, cross_out_both, cross_marks
    )
    grad_state, gain_dattn, dec_qkv_grad, dec_out_grad = attention_backward(
        places, grad_state, dec_attn, dec_qkv_both, dec_out_both, dec_marks, True
    )
    grad_tgt_rows, gain_demb = tgt_back(grad_state)
    grad_hidden, gain_memory = memory_back(grad_memory)
    grad_hidden, gain_effn, enc_up_grad, enc_down_grad = ffn_backward(
        places, grad_hidden, enc_ffn, enc_ups, enc_downs
    )
    grad_hidden, gain_eattn, enc_qkv_grad, enc_out_grad = attention_backward(
        places, grad_hidden, enc_attn, enc_qkv_both, enc_out_both, enc_marks, False
    )
    grad_src_rows, gain_eemb = src_back(grad_hidden)
    grad_tokens = jnp.concatenate([grad_src_rows, grad_tgt_rows])
    table_grad = table_gradient(grad_tokens, route_info, embed_table.shape[0])
    gain_parts = jnp.stack(
        [
            gain_eemb,
            gain_eattn,
            gain_effn,
            gain_memory,
            gain_demb,
            gain_dattn,
            gain_cross,
            gain_dffn,
            gain_final,
        ]
    )
    gain_grad = lax.psum(gain_parts, ("dp", "tensor"))

    def narrow_sum(grads):
        grads = jnp.stack(grads)
        return places.sum_weight(grads[..., :shard], grads[..., shard:], 1)

    def out_sum(grad):
        return places.sum_weight(grad[:shard], grad[shard:], 1)

    return (
        decoded[:, None],
        table_grad,
        gain_grad,
        narrow_sum(enc_qkv_grad),
        out_sum(enc_out_grad),
        places.sum_weight(*enc_up_grad, 0),
        places.sum_weight(*enc_down_grad, 1),
        narrow_sum(dec_qkv_grad),
        out_sum(dec_out_grad),
        narrow_sum([cross_q_grad])[0],
        narrow_sum(cross_kv_grad),
        out_sum(cross_out_grad),
        places.sum_weight(*dec_up_grad, 0),
        places.sum_weight(*dec_down_grad, 1),
    )


def solution(mesh):
    return jax.shard_map(
        on_device,
        mesh=mesh,
        in_specs=(
            P("tensor", "dp"),
            P("tensor", "dp"),
            P(None, "dp"),
            P(None, "dp"),
            P(("dp", "tensor"), None),
            P(),
            P(None, None, "tensor"),
            P("tensor", None),
            P(None, "tensor"),
            P("tensor", None),
            P(None, None, "tensor"),
            P("tensor", None),
            P(None, "tensor"),
            P(None, None, "tensor"),
            P("tensor", None),
            P(None, "tensor"),
            P("tensor", None),
            P("tensor", "dp", None),
        ),
        out_specs=(
            P("tensor", "dp", None),
            P(("dp", "tensor"), None),
            P(),
            P(None, "dp", "tensor"),
            P("tensor", "dp"),
            P("dp", "tensor"),
            P("tensor", "dp"),
            P(None, "dp", "tensor"),
            P("tensor", "dp"),
            P("dp", "tensor"),
            P(None, "dp", "tensor"),
            P("tensor", "dp"),
            P("dp", "tensor"),
            P("tensor", "dp"),
        ),
        check_vma=False,
    )
```

time: 1840 us -> 843 us (0.46)
  waiting for transfers between devices: 1380 us -> 275 us
  starting transfers between devices: 13.8 us -> 181 us
  matrix products: 187 us -> 77 us
  Pallas kernels: 0 us -> 49.5 us
  local copies, waits for them, and re-layouts: 57.2 us -> 91.3 us
  blocking collectives: 74.6 us -> 48.6 us
    reduce_scatter x22 -> x11, waiting for transfers between devices: 874 us -> 0.06 us  [sum_weight(): lax.psum_scatter(jnp.stack([own.astype(BF16), other.astype(BF16)]), 'dp',...]
    all_gather x11 -> x5, waiting for transfers between devices: 476 us -> 0.01 us  [partner_weight(): return lax.all_gather(self.partner(share), 'dp', axis=0, tiled=True)]
    ppermute x0 -> x125, waiting for transfers between devices: none -> 246 us  [the longest x99 141 us: mate(): lax.ppermute(value, 'tensor', [(t, t ^ offset) for t in range(self.tensor...]
    ppermute x0 -> x125, starting transfers between devices: none -> 152 us  [the longest x99 108 us: mate(): lax.ppermute(value, 'tensor', [(t, t ^ offset) for t in range(self.tensor...]
    dot_general x60, matrix products: 153 us -> 77 us  [dot(): lax.dot_general(lhs, rhs, (dims, ((), ())), preferred_element_type=F32)]
    pallas_call x0 -> x6, Pallas kernels: none -> 49.5 us  [the longest x3 26.5 us: attend_back(): pl.pallas_call(partial(attn_bwd_kernel, causal=causal, heads=heads), grid...]
    all_to_all x3 -> x0, blocking collectives: 34.3 us -> none  [the longest x1 14.2 us: table_lookup(): lax.all_to_all(picked.reshape(size_dp, size_tensor, capacity, -1), 'dp',...]
    convert_element_type x29 -> x7, other arithmetic: 36.2 us -> 2.08 us  [the longest x3 1.47 us: both_cores_sum(): other = places.other_core(sent).astype(F32)]
  transfers between devices with their start and end apart: 36 -> 147, of which waited for: 34 -> 67; matrix products, arithmetic and copies ran while one was open for 10% -> 27% of each run, Pallas kernels for 0% -> 6%
where the time goes in v1:
time: 843 us; the launch traced here: 831 us
  waiting for transfers between devices  275 us (33%)
  starting transfers between devices  181 us (21%)
  other arithmetic  91.5 us (11%)
  local copies, waits for them, and re-layouts  91.3 us (11%)
  matrix products  77 us (9%)
  Pallas kernels  49.5 us (6%)
  blocking collectives  48.6 us (6%)
  between operations  18 us (2%)
    ppermute x99, waiting for transfers between devices, mate(): lax.ppermute(value, 'tensor', [(t, t ^ offset) for t in range(self.tensor...  141 us
    ppermute x99, starting transfers between devices, mate(): lax.ppermute(value, 'tensor', [(t, t ^ offset) for t in range(self.tensor...  108 us
    ppermute x17, waiting for transfers between devices, partner(): lax.ppermute(value, 'tensor', [(t, t ^ self.group) for t in range(self.te...  103 us
    dot_general x60, matrix products, dot(): lax.dot_general(lhs, rhs, (dims, ((), ())), preferred_element_type=F32)  77 us
    psum x1, blocking collectives, on_device(): gain_grad = lax.psum(gain_parts, ('dp', 'tensor'))  40.4 us
    ppermute x17, starting transfers between devices, partner(): lax.ppermute(value, 'tensor', [(t, t ^ self.group) for t in range(self.te...  39.5 us
    unnamed x447, local copies, waits for them, and re-layouts  33.6 us
    pallas_call x3, Pallas kernels, attend_back(): pl.pallas_call(partial(attn_bwd_kernel, causal=causal, heads=heads), grid...  26.5 us
  transfers between devices with their start and end apart: 147, of which 67 were waited for; matrix products, arithmetic and copies ran while one was open for 27% of the time, Pallas kernels for 6%

profile of v1, /device:TPU:0, one launch (start us, length us, event | category | flops | bytes accessed | tf_op | source)
XLA Modules:
  0.0 831.4 jit_solution(9388545031513899233)
XLA Ops:
  10.7 5.3 collective-permute-start.9
  18.7 3.0 collective-permute-start.35
  21.6 4.2 fusion.45
  28.1 44.6 %collective-permute-done.7 = bf16[2304,128]{1,0:T(8,128)(2,1)S(1)} collective-permute-done((bf16[2304,128]{1,0:T(8,128)(2,1)}, bf16[2304,128]{1,0:T(8,128)(2,1)S(1)}, u32[]{:S(2)}, u32[]{:S(2)}) %collective-permute-start.7) | collective-permute-done | bytes 589856 | tf_op jit(solution)/shard_map/ppermute | solution.py:182
  76.1 3.4 all-to-all-start
  79.4 3.9 all-to-all-done
  83.9 6.5 all-to-all-start.1
  90.4 6.6 all-to-all-done.1
  97.7 7.2 gather_fusion
  106.7 3.6 all-to-all-start.2
  113.4 8.6 %all-to-all-done.2 = bf16[4,8,12,1024]{3,1,2,0:T(8,128)(2,1)S(1)} async-done(((bf16[4,8,12,1024]{3,1,2,0:T(8,128)(2,1)}), bf16[4,8,12,1024]{3,1,2,0:T(8,128)(2,1)S(1)}, u32[]{:S(2)}, u32[]{:S(2)}) %all-to-all-start.2) | async-done | bytes 786464 | tf_op jit(solution)/shard_map/all_to_all | solution.py:367
  123.5 3.5 all-to-all-start.3
  131.0 8.2 all_gather.19
  140.3 6.9 all-to-all-done.3
  160.0 3.6 collective-permute-done.1
  168.0 3.2 collective-permute-done.19
  181.7 2.6 fusion.180
  192.7 7.4 attend.4
  206.5 7.8 attend.3
  222.7 5.5 collective-permute-done.10
  228.2 5.4 collective-permute-done.12
  233.5 3.9 collective-permute-done.11
  257.0 3.3 fusion.220
  260.3 3.0 multiply_convert_fusion.3
  266.2 3.0 fusion.210
  275.3 4.8 collective-permute-done.37
  289.2 3.0 collective-permute-start.42
  303.7 7.8 attend.5
  318.8 2.9 collective-permute-start.57
  321.7 4.5 collective-permute-done.47
  326.1 5.7 collective-permute-done.49
  331.8 3.6 collective-permute-done.48
  352.8 3.4 fusion.222
  360.0 3.0 fusion.212
  367.6 6.8 collective-permute-done.58
  374.4 4.6 collective-permute-done.60
  379.0 2.5 collective-permute-done.59
  392.8 4.3 collective-permute-done.67
  405.5 10.3 %collective-permute-done.69 = bf16[128,1024]{1,0:T(8,128)(2,1)S(1)} collective-permute-done((bf16[128,1024]{1,0:T(8,128)(2,1)S(1)}, bf16[128,1024]{1,0:T(8,128)(2,1)S(1)}, u32[]{:S(2)}, u32[]{:S(2)}) %collective-permute-start.69) | collective-permute-done | bytes 262176 | tf_op jit(solution)/shard_map/ppermute | solution.py:185
  427.8 2.8 collective-permute-done.76
  436.9 8.8 %attend_back.3 = (bf16[512,256]{1,0:T(8,128)(2,1)S(1)}, f32[1024,256]{1,0:T(8,128)S(1)}, f32[1024,256]{1,0:T(8,128)S(1)}) custom-call(bf16[512,256]{1,0:T(8,128)(2,1)S(1)} %copy-done.24, bf16[1024,256]{1,0:T(8,128)(2,1)S(1)} %copy-done.18, bf16[1024,256]{1,0:T(8,128)(2,1)S(1)} %copy-done.16, bf16[512,256]{1,0:T(8,128)(2,1)S(1)} %convolution_convert_fusion.14.g_ref, ...), custom_call_target="tpu_custom_call" | custom-call | flops 1342177280 | bytes 3932160 | tf_op jit(solution)/shard_map/attend_back/pallas_call | solution.py:133
  451.4 6.0 collective-permute-done.101
  477.3 6.3 collective-permute-done.79
  483.6 3.4 collective-permute-done.80
  495.7 2.7 collective-permute-done.86
  508.0 6.8 collective-permute-done.88
  548.8 8.8 %attend_back.5 = (bf16[512,256]{1,0:T(8,128)(2,1)S(1)}, f32[1024,256]{1,0:T(8,128)S(1)}, f32[1024,256]{1,0:T(8,128)S(1)}) custom-call(bf16[512,256]{1,0:T(8,128)(2,1)S(1)} %copy-done.22, bf16[1024,256]{1,0:T(8,128)(2,1)S(1)} %copy-done.14, bf16[1024,256]{1,0:T(8,128)(2,1)S(1)} %copy-done.12, bf16[512,256]{1,0:T(8,128)(2,1)S(1)} %convolution_convert_fusion.12.g_ref, ...), custom_call_target="tpu_custom_call" | custom-call | flops 1342177280 | bytes 3932160 | tf_op jit(solution)/shard_map/attend_back/pallas_call | solution.py:133
  570.1 8.8 %attend_back.4 = (bf16[512,256]{1,0:T(8,128)(2,1)S(1)}, f32[1024,256]{1,0:T(8,128)S(1)}, f32[1024,256]{1,0:T(8,128)S(1)}) custom-call(bf16[512,256]{1,0:T(8,128)(2,1)S(1)} %copy-done.20, bf16[1024,256]{1,0:T(8,128)(2,1)S(1)} %copy-done.10, bf16[1024,256]{1,0:T(8,128)(2,1)S(1)} %copy-done.8, bf16[512,256]{1,0:T(8,128)(2,1)S(1)} %convolution_convert_fusion.13.g_ref, ...), custom_call_target="tpu_custom_call" | custom-call | flops 1342177280 | bytes 3932160 | tf_op jit(solution)/shard_map/attend_back/pallas_call | solution.py:133
  588.4 3.6 scatter_custom_fusion.3
  596.1 12.0 %collective-permute-start.122 = (bf16[128,256]{1,0:T(8,128)(2,1)S(1)}, bf16[128,256]{1,0:T(8,128)(2,1)}, u32[]{:S(2)}, u32[]{:S(2)}) collective-permute-start(bf16[128,256]{1,0:T(8,128)(2,1)S(1)} %slice_bitcast_fusion.36), channel_id=1, source_target_pairs={{0,4},{1,5},{2,6},{3,7},{4,0},{5,1},{6,2},{7,3},{8,12},{9,13},{10,... | collective-permute-start | bytes 196616 | tf_op jit(solution)/shard_map/ppermute | solution.py:182
  629.9 2.8 collective-permute-start.119
  639.1 8.1 collective-permute-done.98
  651.9 40.4 %psum.7 = f32[9,1024]{1,0:T(8,128)} all-reduce(f32[9,1024]{1,0:T(8,128)S(1)} %stack.147), channel_id=1, replica_groups=mesh['dp'=4,'tensor'=8] {'dp','tensor'}, use_global_device_ids=true, to_apply=%region_52.55 | all-reduce | flops 9216 | bytes 73728 | tf_op jit(solution)/shard_map/psum | solution.py:532
  696.3 3.5 all-to-all-start.4
  704.7 2.9 collective-permute-done.115
  709.1 2.5 all-to-all-done.4
  713.0 6.1 all-to-all-start.5
  720.1 3.0 collective-permute-start.124
  725.0 32.3 %collective-permute-done.124 = bf16[512,256]{1,0:T(8,128)(2,1)S(1)} collective-permute-done((bf16[512,256]{1,0:T(8,128)(2,1)S(1)}, bf16[512,256]{1,0:T(8,128)(2,1)S(1)}, u32[]{:S(2)}, u32[]{:S(2)}) %collective-permute-start.124) | collective-permute-done | bytes 262176 | tf_op jit(solution)/shard_map/ppermute | solution.py:182
  765.5 11.7 %scatter_custom_fusion.2 = f32[4096,1024]{1,0:T(8,128)} fusion(s32[384]{0:T(512)} %get-tuple-element.141, f32[384,1024]{1,0:T(8,128)} %reshape.712, f32[]{:T(128)} %constant.175.clone.1), kind=kCustom, calls=%fused_computation.11 | custom fusion | flops 393216 | bytes 16777728 | tf_op jit(solution)/shard_map/scatter-add | solution.py:412
  777.2 12.0 %broadcast_divide_fusion = f32[4096,1024]{1,0:T(8,128)} fusion(f32[4096,1024]{1,0:T(8,128)} %scatter_custom_fusion.2, f32[4096]{0:T(1024)S(1)} %broadcast_maximum_fusion), kind=kLoop, calls=%fused_computation.10 | loop fusion | flops 4194304 | bytes 33570816 | tf_op jit(solution)/shard_map/div | solution.py:419
  791.1 3.0 collective-permute-start.117
  796.1 2.9 collective-permute-start.116
  799.1 20.8 %collective-permute-done.114 = bf16[3,256,128]{2,1,0:T(8,128)(2,1)S(1)} collective-permute-done((bf16[3,256,128]{2,1,0:T(8,128)(2,1)S(1)}, bf16[3,256,128]{2,1,0:T(8,128)(2,1)S(1)}, u32[]{:S(2)}, u32[]{:S(2)}) %collective-permute-start.114) | collective-permute-done | bytes 196640 | tf_op jit(solution)/shard_map/ppermute | solution.py:182
  (1021 shorter events, 359.8 us)
Async XLA Ops:
  7.2 174.5 %all-gather.6.cloned.1.call-start = ((), (), s32[]{:S(2)}) async-start(), calls=%async_computation.17 | async-start | bytes 2949120 | tf_op jit(solution)/shard_map/all_gather | solution.py:208
  8.1 19.1 %collective-permute-start = (s32[2304]{0:T(1024)S(1)}, s32[2304]{0:T(1024)S(1)}, u32[]{:S(2)}, u32[]{:S(2)}) collective-permute-start(s32[2304]{0:T(1024)S(1)} %pad_add_fusion), channel_id=1, source_target_pairs={{0,0},{1,1},{2,2},{3,3},{4,8},{5,9},{6,10},{7,11},{8,4},{9,5},{10,... | collective-permute-start | bytes 27656 | tf_op jit(solution)/shard_map/ppermute | solution.py:176
  10.7 120.3 %collective-permute-start.9 = (bf16[96,1024]{1,0:T(8,128)(2,1)}, bf16[96,1024]{1,0:T(8,128)(2,1)}, u32[]{:S(2)}, u32[]{:S(2)}) collective-permute-start(bf16[96,1024]{1,0:T(8,128)(2,1)} %fusion.97), channel_id=1, source_target_pairs={{0,4},{1,5},{2,6},{3,7},{4,0},{5,1},{6,2},{7,3},{8,12},{9,13},{10,... | collective-permute-start | bytes 589832 | tf_op jit(solution)/shard_map/ppermute | solution.py:182
  17.7 199.9 %collective-permute-start.36 = (bf16[128,1024]{1,0:T(8,128)(2,1)}, bf16[128,1024]{1,0:T(8,128)(2,1)}, u32[]{:S(2)}, u32[]{:S(2)}) collective-permute-start(bf16[128,1024]{1,0:T(8,128)(2,1)} %constant_dynamic-slice_fusion.2), channel_id=1, source_target_pairs={{0,4},{1,5},{2,6},{3,7},{4,0},{5,1},{6,2},{7,3},{8,12},{9,13},{10,... | collective-permute-start | bytes 786440 | tf_op jit(solution)/shard_map/ppermute | solution.py:182
  18.7 121.4 %collective-permute-start.35 = (bf16[256,512]{1,0:T(8,128)(2,1)S(1)}, bf16[256,512]{1,0:T(8,128)(2,1)}, u32[]{:S(2)}, u32[]{:S(2)}) collective-permute-start(bf16[256,512]{1,0:T(8,128)(2,1)S(1)} %constant_dynamic-slice_fusion.3), channel_id=1, source_target_pairs={{0,4},{1,5},{2,6},{3,7},{4,0},{5,1},{6,2},{7,3},{8,12},{9,13},{10,... | collective-permute-start | bytes 786440 | tf_op jit(solution)/shard_map/ppermute | solution.py:182
  25.9 46.9 %collective-permute-start.7 = (bf16[2304,128]{1,0:T(8,128)(2,1)}, bf16[2304,128]{1,0:T(8,128)(2,1)S(1)}, u32[]{:S(2)}, u32[]{:S(2)}) collective-permute-start(bf16[2304,128]{1,0:T(8,128)(2,1)} %fusion.45), channel_id=1, source_target_pairs={{0,4},{1,5},{2,6},{3,7},{4,0},{5,1},{6,2},{7,3},{8,12},{9,13},{10,... | collective-permute-start | bytes 1769480 | tf_op jit(solution)/shard_map/ppermute | solution.py:182
  83.9 13.1 %all-to-all-start.1 = ((s32[4,8,12]{2,0,1:T(4,128)}), s32[4,8,12]{2,0,1:T(4,128)S(1)}, u32[]{:S(2)}, u32[]{:S(2)}) async-start(s32[4,8,12]{2,0,1:T(4,128)} %copy.94), calls=%async_computation.1 | async-start | bytes 32768 | tf_op jit(solution)/shard_map/all_to_all | solution.py:350
  106.7 15.3 %all-to-all-start.2 = ((bf16[4,8,12,1024]{3,1,2,0:T(8,128)(2,1)}), bf16[4,8,12,1024]{3,1,2,0:T(8,128)(2,1)S(1)}, u32[]{:S(2)}, u32[]{:S(2)}) async-start(bf16[4,8,12,1024]{3,1,2,0:T(8,128)(2,1)} %copy.98), calls=%async_computation.2 | async-start | bytes 1572864 | tf_op jit(solution)/shard_map/all_to_all | solution.py:367
  123.5 23.8 %all-to-all-start.3 = ((bf16[4,8,12,1024]{3,0,2,1:T(4,128)(2,1)}), bf16[4,8,12,1024]{3,0,2,1:T(4,128)(2,1)S(1)}, u32[]{:S(2)}, u32[]{:S(2)}) async-start(bf16[4,8,12,1024]{3,0,2,1:T(4,128)(2,1)} %copy.99), calls=%async_computation.3 | async-start | bytes 1572864 | tf_op jit(solution)/shard_map/all_to_all | solution.py:366
  127.0 130.0 %all-gather.8.cloned.1.call-start = ((), (), s32[]{:S(2)}) async-start(), calls=%async_computation.18 | async-start | bytes 1310720 | tf_op jit(solution)/shard_map/all_gather | solution.py:208
  140.1 126.0 %all-gather.10.cloned.1.call-start = ((), (), s32[]{:S(2)}) async-start(), calls=%async_computation.19 | async-start | bytes 1310720 | tf_op jit(solution)/shard_map/all_gather | solution.py:208
  189.9 16.4 %collective-permute-start.8 = (bf16[512,512]{1,0:T(8,128)(2,1)S(1)}, bf16[512,512]{1,0:T(8,128)(2,1)S(1)}, u32[]{:S(2)}, u32[]{:S(2)}) collective-permute-start(bf16[512,512]{1,0:T(8,128)(2,1)S(1)} %pad_maximum_fusion.10), channel_id=1, source_target_pairs={{0,8},{8,0},{16,24},{24,16},{1,9},{9,1},{17,25},{25,17},{2,10},{10... | collective-permute-start | bytes 1572872 | tf_op jit(solution)/shard_map/ppermute | solution.py:179
  202.8 16.4 %collective-permute-start.26 = (bf16[128,1024]{1,0:T(8,128)(2,1)}, bf16[128,1024]{1,0:T(8,128)(2,1)}, u32[]{:S(2)}, u32[]{:S(2)}) collective-permute-start(bf16[128,1024]{1,0:T(8,128)(2,1)} %get-tuple-element.265), channel_id=1, source_target_pairs={{0,1},{1,0},{2,3},{3,2},{4,5},{5,4},{6,7},{7,6},{8,9},{9,8},{10,11... | collective-permute-start | bytes 786440 | tf_op jit(solution)/shard_map/ppermute | solution.py:185
  203.3 18.0 %collective-permute-start.28 = (bf16[128,1024]{1,0:T(8,128)(2,1)}, bf16[128,1024]{1,0:T(8,128)(2,1)}, u32[]{:S(2)}, u32[]{:S(2)}) collective-permute-start(bf16[128,1024]{1,0:T(8,128)(2,1)} %get-tuple-element.266), channel_id=1, source_target_pairs={{0,3},{1,2},{2,1},{3,0},{4,7},{5,6},{6,5},{7,4},{8,11},{9,10},{10,... | collective-permute-start | bytes 786440 | tf_op jit(solution)/shard_map/ppermute | solution.py:185
  204.9 17.8 %collective-permute-start.27 = (bf16[128,1024]{1,0:T(8,128)(2,1)}, bf16[128,1024]{1,0:T(8,128)(2,1)}, u32[]{:S(2)}, u32[]{:S(2)}) collective-permute-start(bf16[128,1024]{1,0:T(8,128)(2,1)} %get-tuple-element.267), channel_id=1, source_target_pairs={{0,2},{1,3},{2,0},{3,1},{4,6},{5,7},{6,4},{7,5},{8,10},{9,11},{10,... | collective-permute-start | bytes 786440 | tf_op jit(solution)/shard_map/ppermute | solution.py:185
  217.6 16.0 %collective-permute-start.12 = (bf16[128,1024]{1,0:T(8,128)(2,1)}, bf16[128,1024]{1,0:T(8,128)(2,1)S(1)}, u32[]{:S(2)}, u32[]{:S(2)}) collective-permute-start(bf16[128,1024]{1,0:T(8,128)(2,1)} %get-tuple-element.271), channel_id=1, source_target_pairs={{0,3},{1,2},{2,1},{3,0},{4,7},{5,6},{6,5},{7,4},{8,11},{9,10},{10,... | collective-permute-start | bytes 786440 | tf_op jit(solution)/shard_map/ppermute | solution.py:185
  219.2 18.2 %collective-permute-start.11 = (bf16[128,1024]{1,0:T(8,128)(2,1)}, bf16[128,1024]{1,0:T(8,128)(2,1)}, u32[]{:S(2)}, u32[]{:S(2)}) collective-permute-start(bf16[128,1024]{1,0:T(8,128)(2,1)} %get-tuple-element.272), channel_id=1, source_target_pairs={{0,2},{1,3},{2,0},{3,1},{4,6},{5,7},{6,4},{7,5},{8,10},{9,11},{10,... | collective-permute-start | bytes 786440 | tf_op jit(solution)/shard_map/ppermute | solution.py:185
  221.3 131.5 %all-gather.12.cloned.1.call-start = ((), (), s32[]{:S(2)}) async-start(), calls=%async_computation.20 | async-start | bytes 1310720 | tf_op jit(solution)/shard_map/all_gather | solution.py:208
  221.3 96.4 %collective-permute-start.56 = (bf16[256,512]{1,0:T(8,128)(2,1)}, bf16[256,512]{1,0:T(8,128)(2,1)}, u32[]{:S(2)}, u32[]{:S(2)}) collective-permute-start(bf16[256,512]{1,0:T(8,128)(2,1)} %constant_dynamic-slice_fusion.1), channel_id=1, source_target_pairs={{0,4},{1,5},{2,6},{3,7},{4,0},{5,1},{6,2},{7,3},{8,12},{9,13},{10,... | collective-permute-start | bytes 786440 | tf_op jit(solution)/shard_map/ppermute | solution.py:182
  248.5 24.4 %collective-permute-start.13 = (bf16[64,1024]{1,0:T(8,128)(2,1)}, bf16[64,1024]{1,0:T(8,128)(2,1)}, u32[]{:S(2)}, u32[]{:S(2)}) collective-permute-start(bf16[64,1024]{1,0:T(8,128)(2,1)} %get-tuple-element.318), channel_id=1, source_target_pairs={{0,1},{1,0},{2,3},{3,2},{4,5},{5,4},{6,7},{7,6},{8,9},{9,8},{10,11... | collective-permute-start | bytes 393224 | tf_op jit(solution)/shard_map/ppermute | solution.py:185
  272.9 19.3 %collective-permute-start.16 = (bf16[64,1024]{1,0:T(8,128)(2,1)S(1)}, bf16[64,1024]{1,0:T(8,128)(2,1)S(1)}, u32[]{:S(2)}, u32[]{:S(2)}) collective-permute-start(bf16[64,1024]{1,0:T(8,128)(2,1)S(1)} %copy-done.145), channel_id=1, source_target_pairs={{0,2},{1,3},{2,0},{3,1},{4,6},{5,7},{6,4},{7,5},{8,10},{9,11},{10,... | collective-permute-start | bytes 393224 | tf_op jit(solution)/shard_map/ppermute | solution.py:185
  314.3 11.9 %collective-permute-start.47 = (bf16[128,1024]{1,0:T(8,128)(2,1)}, bf16[128,1024]{1,0:T(8,128)(2,1)S(1)}, u32[]{:S(2)}, u32[]{:S(2)}) collective-permute-start(bf16[128,1024]{1,0:T(8,128)(2,1)} %get-tuple-element.257), channel_id=1, source_target_pairs={{0,1},{1,0},{2,3},{3,2},{4,5},{5,4},{6,7},{7,6},{8,9},{9,8},{10,11... | collective-permute-start | bytes 786440 | tf_op jit(solution)/shard_map/ppermute | solution.py:185
  315.9 15.9 %collective-permute-start.49 = (bf16[128,1024]{1,0:T(8,128)(2,1)}, bf16[128,1024]{1,0:T(8,128)(2,1)S(1)}, u32[]{:S(2)}, u32[]{:S(2)}) collective-permute-start(bf16[128,1024]{1,0:T(8,128)(2,1)} %get-tuple-element.258), channel_id=1, source_target_pairs={{0,3},{1,2},{2,1},{3,0},{4,7},{5,6},{6,5},{7,4},{8,11},{9,10},{10,... | collective-permute-start | bytes 786440 | tf_op jit(solution)/shard_map/ppermute | solution.py:185
  317.4 18.0 %collective-permute-start.48 = (bf16[128,1024]{1,0:T(8,128)(2,1)}, bf16[128,1024]{1,0:T(8,128)(2,1)}, u32[]{:S(2)}, u32[]{:S(2)}) collective-permute-start(bf16[128,1024]{1,0:T(8,128)(2,1)} %get-tuple-element.259), channel_id=1, source_target_pairs={{0,2},{1,3},{2,0},{3,1},{4,6},{5,7},{6,4},{7,5},{8,10},{9,11},{10,... | collective-permute-start | bytes 786440 | tf_op jit(solution)/shard_map/ppermute | solution.py:185
  317.8 42.2 %all-gather.14.cloned.1.call-start = ((), (), s32[]{:S(2)}) async-start(), calls=%async_computation.21 | async-start | bytes 1310720 | tf_op jit(solution)/shard_map/all_gather | solution.py:208
  318.8 21.8 %collective-permute-start.57 = (bf16[128,1024]{1,0:T(8,128)(2,1)S(1)}, bf16[128,1024]{1,0:T(8,128)(2,1)}, u32[]{:S(2)}, u32[]{:S(2)}) collective-permute-start(bf16[128,1024]{1,0:T(8,128)(2,1)S(1)} %constant_dynamic-slice_fusion), channel_id=1, source_target_pairs={{0,4},{1,5},{2,6},{3,7},{4,0},{5,1},{6,2},{7,3},{8,12},{9,13},{10,... | collective-permute-start | bytes 786440 | tf_op jit(solution)/shard_map/ppermute | solution.py:182
  340.6 254.6 %reduce-scatter.28.cloned.1.call-start = ((), (), s32[]{:S(2)}) async-start(), calls=%async_computation.30 | async-start | bytes 655360 | tf_op jit(solution)/shard_map/reduce_scatter | solution.py:211
  363.2 15.8 %collective-permute-start.60 = (bf16[128,1024]{1,0:T(8,128)(2,1)S(1)}, bf16[128,1024]{1,0:T(8,128)(2,1)S(1)}, u32[]{:S(2)}, u32[]{:S(2)}) collective-permute-start(bf16[128,1024]{1,0:T(8,128)(2,1)S(1)} %get-tuple-element.255), channel_id=1, source_target_pairs={{0,3},{1,2},{2,1},{3,0},{4,7},{5,6},{6,5},{7,4},{8,11},{9,10},{10,... | collective-permute-start | bytes 786440 | tf_op jit(solution)/shard_map/ppermute | solution.py:185
  365.0 16.5 %collective-permute-start.59 = (bf16[128,1024]{1,0:T(8,128)(2,1)S(1)}, bf16[128,1024]{1,0:T(8,128)(2,1)S(1)}, u32[]{:S(2)}, u32[]{:S(2)}) collective-permute-start(bf16[128,1024]{1,0:T(8,128)(2,1)S(1)} %get-tuple-element.256), channel_id=1, source_target_pairs={{0,2},{1,3},{2,0},{3,1},{4,6},{5,7},{6,4},{7,5},{8,10},{9,11},{10,... | collective-permute-start | bytes 786440 | tf_op jit(solution)/shard_map/ppermute | solution.py:185
  366.7 15.2 %collective-permute-start.62 = (f32[128,1024]{1,0:T(8,128)S(1)}, f32[128,1024]{1,0:T(8,128)S(1)}, u32[]{:S(2)}, u32[]{:S(2)}) collective-permute-start(f32[128,1024]{1,0:T(8,128)S(1)} %bitcast.333), channel_id=1, source_target_pairs={{0,0},{1,1},{2,2},{3,3},{4,8},{5,9},{6,10},{7,11},{8,4},{9,5},{10,... | collective-permute-start | bytes 1572872 | tf_op jit(solution)/shard_map/ppermute | solution.py:176
  402.0 13.8 %collective-permute-start.69 = (bf16[128,1024]{1,0:T(8,128)(2,1)S(1)}, bf16[128,1024]{1,0:T(8,128)(2,1)S(1)}, u32[]{:S(2)}, u32[]{:S(2)}) collective-permute-start(bf16[128,1024]{1,0:T(8,128)(2,1)S(1)} %get-tuple-element.251), channel_id=1, source_target_pairs={{0,1},{1,0},{2,3},{3,2},{4,5},{5,4},{6,7},{7,6},{8,9},{9,8},{10,11... | collective-permute-start | bytes 786440 | tf_op jit(solution)/shard_map/ppermute | solution.py:185
  402.8 13.0 %collective-permute-start.71 = (bf16[128,1024]{1,0:T(8,128)(2,1)S(1)}, bf16[128,1024]{1,0:T(8,128)(2,1)S(1)}, u32[]{:S(2)}, u32[]{:S(2)}) collective-permute-start(bf16[128,1024]{1,0:T(8,128)(2,1)S(1)} %get-tuple-element.252), channel_id=1, source_target_pairs={{0,3},{1,2},{2,1},{3,0},{4,7},{5,6},{6,5},{7,4},{8,11},{9,10},{10,... | collective-permute-start | bytes 786440 | tf_op jit(solution)/shard_map/ppermute | solution.py:185
  403.9 13.1 %collective-permute-start.70 = (bf16[128,1024]{1,0:T(8,128)(2,1)S(1)}, bf16[128,1024]{1,0:T(8,128)(2,1)S(1)}, u32[]{:S(2)}, u32[]{:S(2)}) collective-permute-start(bf16[128,1024]{1,0:T(8,128)(2,1)S(1)} %get-tuple-element.253), channel_id=1, source_target_pairs={{0,2},{1,3},{2,0},{3,1},{4,6},{5,7},{6,4},{7,5},{8,10},{9,11},{10,... | collective-permute-start | bytes 786440 | tf_op jit(solution)/shard_map/ppermute | solution.py:185
  432.6 175.6 %reduce-scatter.24.cloned.1.call-start = ((), (), s32[]{:S(2)}) async-start(), calls=%async_computation.28 | async-start | bytes 655360 | tf_op jit(solution)/shard_map/reduce_scatter | solution.py:211
  450.9 17.6 %collective-permute-start.78 = (bf16[512,512]{1,0:T(8,128)(2,1)}, bf16[512,512]{1,0:T(8,128)(2,1)}, u32[]{:S(2)}, u32[]{:S(2)}) collective-permute-start(bf16[512,512]{1,0:T(8,128)(2,1)} %pad_maximum_fusion.28), channel_id=1, source_target_pairs={{0,8},{8,0},{16,24},{24,16},{1,9},{9,1},{17,25},{25,17},{2,10},{10... | collective-permute-start | bytes 1572872 | tf_op jit(solution)/shard_map/ppermute | solution.py:179
  463.2 165.8 %reduce-scatter.22.cloned.1.call-start = ((), (), s32[]{:S(2)}) async-start(), calls=%async_computation.27 | async-start | bytes 655360 | tf_op jit(solution)/shard_map/reduce_scatter | solution.py:211
  463.5 11.8 %collective-permute-start.107 = (bf16[64,1024]{1,0:T(8,128)(2,1)}, bf16[64,1024]{1,0:T(8,128)(2,1)S(1)}, u32[]{:S(2)}, u32[]{:S(2)}) collective-permute-start(bf16[64,1024]{1,0:T(8,128)(2,1)} %get-tuple-element.303), channel_id=1, source_target_pairs={{0,2},{1,3},{2,0},{3,1},{4,6},{5,7},{6,4},{7,5},{8,10},{9,11},{10,... | collective-permute-start | bytes 393224 | tf_op jit(solution)/shard_map/ppermute | solution.py:185
  474.7 12.3 %collective-permute-start.80 = (bf16[128,1024]{1,0:T(8,128)(2,1)S(1)}, bf16[128,1024]{1,0:T(8,128)(2,1)S(1)}, u32[]{:S(2)}, u32[]{:S(2)}) collective-permute-start(bf16[128,1024]{1,0:T(8,128)(2,1)S(1)} %get-tuple-element.240), channel_id=1, source_target_pairs={{0,2},{1,3},{2,0},{3,1},{4,6},{5,7},{6,4},{7,5},{8,10},{9,11},{10,... | collective-permute-start | bytes 786440 | tf_op jit(solution)/shard_map/ppermute | solution.py:185
  475.3 14.3 %collective-permute-start.108 = (bf16[64,1024]{1,0:T(8,128)(2,1)}, bf16[64,1024]{1,0:T(8,128)(2,1)S(1)}, u32[]{:S(2)}, u32[]{:S(2)}) collective-permute-start(bf16[64,1024]{1,0:T(8,128)(2,1)} %collective-permute-done.104), channel_id=1, source_target_pairs={{0,2},{1,3},{2,0},{3,1},{4,6},{5,7},{6,4},{7,5},{8,10},{9,11},{10,... | collective-permute-start | bytes 393224 | tf_op jit(solution)/shard_map/ppermute | solution.py:185
  476.8 13.8 %collective-permute-start.109 = (bf16[64,1024]{1,0:T(8,128)(2,1)S(1)}, bf16[64,1024]{1,0:T(8,128)(2,1)S(1)}, u32[]{:S(2)}, u32[]{:S(2)}) collective-permute-start(bf16[64,1024]{1,0:T(8,128)(2,1)S(1)} %collective-permute-done.107), channel_id=1, source_target_pairs={{0,1},{1,0},{2,3},{3,2},{4,5},{5,4},{6,7},{7,6},{8,9},{9,8},{10,11... | collective-permute-start | bytes 393224 | tf_op jit(solution)/shard_map/ppermute | solution.py:185
  522.4 177.5 %reduce-scatter.14.cloned.1.call-start = ((), (), s32[]{:S(2)}) async-start(), calls=%async_computation.23 | async-start | bytes 655360 | tf_op jit(solution)/shard_map/reduce_scatter | solution.py:211
  530.9 171.9 %reduce-scatter.26.cloned.1.call-start = ((), (), s32[]{:S(2)}) async-start(), calls=%async_computation.29 | async-start | bytes 1310720 | tf_op jit(solution)/shard_map/reduce_scatter | solution.py:211
  535.9 183.3 %reduce-scatter.32.cloned.1.call-start = ((), (), s32[]{:S(2)}) async-start(), calls=%async_computation.32 | async-start | bytes 2621440 | tf_op jit(solution)/shard_map/reduce_scatter | solution.py:211
  541.6 181.6 %reduce-scatter.30.cloned.1.call-start = ((), (), s32[]{:S(2)}) async-start(), calls=%async_computation.31 | async-start | bytes 2621440 | tf_op jit(solution)/shard_map/reduce_scatter | solution.py:211
  546.1 215.6 %reduce-scatter.20.cloned.1.call-start = ((), (), s32[]{:S(2)}) async-start(), calls=%async_computation.26 | async-start | bytes 1966080 | tf_op jit(solution)/shard_map/reduce_scatter | solution.py:211
  562.9 227.1 %reduce-scatter.18.cloned.1.call-start = ((), (), s32[]{:S(2)}) async-start(), calls=%async_computation.25 | async-start | bytes 2621440 | tf_op jit(solution)/shard_map/reduce_scatter | solution.py:211
  567.4 226.6 %reduce-scatter.12.cloned.1.call-start = ((), (), s32[]{:S(2)}) async-start(), calls=%async_computation.22 | async-start | bytes 1966080 | tf_op jit(solution)/shard_map/reduce_scatter | solution.py:211
  586.5 208.6 %reduce-scatter.16.cloned.1.call-start = ((), (), s32[]{:S(2)}) async-start(), calls=%async_computation.24 | async-start | bytes 2621440 | tf_op jit(solution)/shard_map/reduce_scatter | solution.py:211
  596.1 25.2 %collective-permute-start.122 = (bf16[128,256]{1,0:T(8,128)(2,1)S(1)}, bf16[128,256]{1,0:T(8,128)(2,1)}, u32[]{:S(2)}, u32[]{:S(2)}) collective-permute-start(bf16[128,256]{1,0:T(8,128)(2,1)S(1)} %slice_bitcast_fusion.36), channel_id=1, source_target_pairs={{0,4},{1,5},{2,6},{3,7},{4,0},{5,1},{6,2},{7,3},{8,12},{9,13},{10,... | collective-permute-start | bytes 196616 | tf_op jit(solution)/shard_map/ppermute | solution.py:182
  609.8 13.9 %collective-permute-start.120 = (bf16[1,256,128]{2,1,0:T(8,128)(2,1)}, bf16[1,256,128]{2,1,0:T(8,128)(2,1)}, u32[]{:S(2)}, u32[]{:S(2)}) collective-permute-start(bf16[1,256,128]{2,1,0:T(8,128)(2,1)} %slice_bitcast_fusion.38), channel_id=1, source_target_pairs={{0,4},{1,5},{2,6},{3,7},{4,0},{5,1},{6,2},{7,3},{8,12},{9,13},{10,... | collective-permute-start | bytes 196616 | tf_op jit(solution)/shard_map/ppermute | solution.py:182
  612.2 13.4 %collective-permute-start.111 = (bf16[128,1024]{1,0:T(8,128)(2,1)S(1)}, bf16[128,1024]{1,0:T(8,128)(2,1)}, u32[]{:S(2)}, u32[]{:S(2)}) collective-permute-start(bf16[128,1024]{1,0:T(8,128)(2,1)S(1)} %get-tuple-element.243), channel_id=1, source_target_pairs={{0,1},{1,0},{2,3},{3,2},{4,5},{5,4},{6,7},{7,6},{8,9},{9,8},{10,11... | collective-permute-start | bytes 786440 | tf_op jit(solution)/shard_map/ppermute | solution.py:185
  613.5 12.0 %collective-permute-start.113 = (bf16[128,1024]{1,0:T(8,128)(2,1)S(1)}, bf16[128,1024]{1,0:T(8,128)(2,1)}, u32[]{:S(2)}, u32[]{:S(2)}) collective-permute-start(bf16[128,1024]{1,0:T(8,128)(2,1)S(1)} %get-tuple-element.244), channel_id=1, source_target_pairs={{0,3},{1,2},{2,1},{3,0},{4,7},{5,6},{6,5},{7,4},{8,11},{9,10},{10,... | collective-permute-start | bytes 786440 | tf_op jit(solution)/shard_map/ppermute | solution.py:185
  614.9 12.5 %collective-permute-start.112 = (bf16[128,1024]{1,0:T(8,128)(2,1)S(1)}, bf16[128,1024]{1,0:T(8,128)(2,1)}, u32[]{:S(2)}, u32[]{:S(2)}) collective-permute-start(bf16[128,1024]{1,0:T(8,128)(2,1)S(1)} %get-tuple-element.245), channel_id=1, source_target_pairs={{0,2},{1,3},{2,0},{3,1},{4,6},{5,7},{6,4},{7,5},{8,10},{9,11},{10,... | collective-permute-start | bytes 786440 | tf_op jit(solution)/shard_map/ppermute | solution.py:185
  634.8 12.4 %collective-permute-start.98 = (bf16[128,1024]{1,0:T(8,128)(2,1)S(1)}, bf16[128,1024]{1,0:T(8,128)(2,1)S(1)}, u32[]{:S(2)}, u32[]{:S(2)}) collective-permute-start(bf16[128,1024]{1,0:T(8,128)(2,1)S(1)} %get-tuple-element.230), channel_id=1, source_target_pairs={{0,1},{1,0},{2,3},{3,2},{4,5},{5,4},{6,7},{7,6},{8,9},{9,8},{10,11... | collective-permute-start | bytes 786440 | tf_op jit(solution)/shard_map/ppermute | solution.py:185
  636.5 12.0 %collective-permute-start.99 = (bf16[128,1024]{1,0:T(8,128)(2,1)S(1)}, bf16[128,1024]{1,0:T(8,128)(2,1)S(1)}, u32[]{:S(2)}, u32[]{:S(2)}) collective-permute-start(bf16[128,1024]{1,0:T(8,128)(2,1)S(1)} %get-tuple-element.232), channel_id=1, source_target_pairs={{0,2},{1,3},{2,0},{3,1},{4,6},{5,7},{6,4},{7,5},{8,10},{9,11},{10,... | collective-permute-start | bytes 786440 | tf_op jit(solution)/shard_map/ppermute | solution.py:185
  696.3 15.2 %all-to-all-start.4 = ((bf16[4,8,12,1024]{3,1,2,0:T(8,128)(2,1)}), bf16[4,8,12,1024]{3,1,2,0:T(8,128)(2,1)S(1)}, u32[]{:S(2)}, u32[]{:S(2)}) async-start(bf16[4,8,12,1024]{3,1,2,0:T(8,128)(2,1)} %copy.113), calls=%async_computation.4 | async-start | bytes 1572864 | tf_op jit(solution)/shard_map/all_to_all | solution.py:397
  703.8 20.5 %collective-permute-start.121 = (bf16[2,256,128]{2,1,0:T(8,128)(2,1)S(1)}, bf16[2,256,128]{2,1,0:T(8,128)(2,1)S(1)}, u32[]{:S(2)}, u32[]{:S(2)}) collective-permute-start(bf16[2,256,128]{2,1,0:T(8,128)(2,1)S(1)} %slice_bitcast_fusion.34), channel_id=1, source_target_pairs={{0,4},{1,5},{2,6},{3,7},{4,0},{5,1},{6,2},{7,3},{8,12},{9,13},{10,... | collective-permute-start | bytes 393224 | tf_op jit(solution)/shard_map/ppermute | solution.py:182
  713.0 49.7 %all-to-all-start.5 = ((bf16[4,8,12,1024]{3,0,2,1:T(4,128)(2,1)}), bf16[4,8,12,1024]{3,0,2,1:T(4,128)(2,1)S(1)}, u32[]{:S(2)}, u32[]{:S(2)}) async-start(bf16[4,8,12,1024]{3,0,2,1:T(4,128)(2,1)} %copy.114), calls=%async_computation.5 | async-start | bytes 1572864 | tf_op jit(solution)/shard_map/all_to_all | solution.py:396
  720.1 37.2 %collective-permute-start.124 = (bf16[512,256]{1,0:T(8,128)(2,1)S(1)}, bf16[512,256]{1,0:T(8,128)(2,1)S(1)}, u32[]{:S(2)}, u32[]{:S(2)}) collective-permute-start(bf16[512,256]{1,0:T(8,128)(2,1)S(1)} %slice_bitcast_fusion.6), channel_id=1, source_target_pairs={{0,4},{1,5},{2,6},{3,7},{4,0},{5,1},{6,2},{7,3},{8,12},{9,13},{10,... | collective-permute-start | bytes 786440 | tf_op jit(solution)/shard_map/ppermute | solution.py:182
  724.2 36.7 %collective-permute-start.123 = (bf16[256,512]{1,0:T(8,128)(2,1)S(1)}, bf16[256,512]{1,0:T(8,128)(2,1)S(1)}, u32[]{:S(2)}, u32[]{:S(2)}) collective-permute-start(bf16[256,512]{1,0:T(8,128)(2,1)S(1)} %slice_bitcast_fusion.8), channel_id=1, source_target_pairs={{0,4},{1,5},{2,6},{3,7},{4,0},{5,1},{6,2},{7,3},{8,12},{9,13},{10,... | collective-permute-start | bytes 786440 | tf_op jit(solution)/shard_map/ppermute | solution.py:182
  762.6 26.6 %collective-permute-start.118 = (bf16[3,256,128]{2,1,0:T(8,128)(2,1)S(1)}, bf16[3,256,128]{2,1,0:T(8,128)(2,1)S(1)}, u32[]{:S(2)}, u32[]{:S(2)}) collective-permute-start(bf16[3,256,128]{2,1,0:T(8,128)(2,1)S(1)} %slice_bitcast_fusion.30), channel_id=1, source_target_pairs={{0,4},{1,5},{2,6},{3,7},{4,0},{5,1},{6,2},{7,3},{8,12},{9,13},{10,... | collective-permute-start | bytes 589832 | tf_op jit(solution)/shard_map/ppermute | solution.py:182
  791.1 30.5 %collective-permute-start.117 = (bf16[512,256]{1,0:T(8,128)(2,1)S(1)}, bf16[512,256]{1,0:T(8,128)(2,1)S(1)}, u32[]{:S(2)}, u32[]{:S(2)}) collective-permute-start(bf16[512,256]{1,0:T(8,128)(2,1)S(1)} %slice_bitcast_fusion.16), channel_id=1, source_target_pairs={{0,4},{1,5},{2,6},{3,7},{4,0},{5,1},{6,2},{7,3},{8,12},{9,13},{10,... | collective-permute-start | bytes 786440 | tf_op jit(solution)/shard_map/ppermute | solution.py:182
  795.0 24.9 %collective-permute-start.114 = (bf16[3,256,128]{2,1,0:T(8,128)(2,1)S(1)}, bf16[3,256,128]{2,1,0:T(8,128)(2,1)S(1)}, u32[]{:S(2)}, u32[]{:S(2)}) collective-permute-start(bf16[3,256,128]{2,1,0:T(8,128)(2,1)S(1)} %slice_bitcast_fusion.32), channel_id=1, source_target_pairs={{0,4},{1,5},{2,6},{3,7},{4,0},{5,1},{6,2},{7,3},{8,12},{9,13},{10,... | collective-permute-start | bytes 589832 | tf_op jit(solution)/shard_map/ppermute | solution.py:182
  796.1 27.4 %collective-permute-start.116 = (bf16[256,512]{1,0:T(8,128)(2,1)S(1)}, bf16[256,512]{1,0:T(8,128)(2,1)S(1)}, u32[]{:S(2)}, u32[]{:S(2)}) collective-permute-start(bf16[256,512]{1,0:T(8,128)(2,1)S(1)} %slice_bitcast_fusion.18), channel_id=1, source_target_pairs={{0,4},{1,5},{2,6},{3,7},{4,0},{5,1},{6,2},{7,3},{8,12},{9,13},{10,... | collective-permute-start | bytes 786440 | tf_op jit(solution)/shard_map/ppermute | solution.py:182
  (278 other events, 2695.4 us)
Sparse Core Ops, SparseCore 0:
  73.7 26.1 all-gather.5
  140.2 17.6 all-gather.7
  221.4 14.6 all-gather.9
  317.9 16.1 all-gather.11
  340.7 16.6 all-gather.13
  432.7 19.5 reduce-scatter.27
  463.3 19.6 reduce-scatter.23
  522.5 18.8 reduce-scatter.21
  544.0 22.1 reduce-scatter.13
  568.6 24.9 reduce-scatter.25
  596.3 31.4 reduce-scatter.31
  630.2 31.9 reduce-scatter.29
  664.8 28.7 reduce-scatter.19
  696.0 31.4 reduce-scatter.17
  730.0 28.1 reduce-scatter.11
  760.7 31.4 reduce-scatter.15

commit v2 on v1

v2 whole, which is shorter than its diff:
```python
import math
from functools import partial

import jax
import jax.numpy as jnp
from jax import lax
from jax.experimental import pallas as pl
from jax.experimental.pallas import tpu as pltpu
from jax.sharding import PartitionSpec as P

HEAD_DIM = 64
FACTOR = 0.125

NORM_EPS = 1e-05
MASKED = -1e30
SEGMENTS = 8
F32 = jnp.float32
BF16 = jnp.bfloat16
VMEM_LIMIT = 48 << 20

NN = ((1,), (0,))
NT = ((1,), (1,))
TN = ((0,), (0,))


def dot(lhs, rhs, dims):
    return lax.dot_general(lhs, rhs, (dims, ((), ())), preferred_element_type=F32)


def call(kernel, name, outs, args, grid=(), in_specs=None, out_specs=None, scratch=(), flops=0, exps=0):
    out_shape = [jax.ShapeDtypeStruct(shape, dtype) for shape, dtype in outs]
    moved = sum(math.prod(a.shape) * a.dtype.itemsize for a in list(args) + out_shape)
    specs = {}
    if in_specs is not None:
        specs = dict(in_specs=in_specs, out_specs=out_specs)
    return pl.pallas_call(
        kernel,
        grid=grid,
        out_shape=out_shape,
        scratch_shapes=list(scratch),
        compiler_params=pltpu.CompilerParams(vmem_limit_bytes=VMEM_LIMIT),
        cost_estimate=pl.CostEstimate(flops=flops, transcendentals=exps, bytes_accessed=moved),
        name=name,
        **specs,
    )(*args)


def normal_form(values):
    shifted = values - jnp.mean(values, axis=-1, keepdims=True)
    scale = lax.rsqrt(jnp.mean(shifted * shifted, axis=-1, keepdims=True) + NORM_EPS)
    return shifted * scale, scale


def norm_grad(values, gain, grad):
    normed, scale = normal_form(values)
    inner = grad * gain
    drop = jnp.mean(inner, axis=-1, keepdims=True) + normed * jnp.mean(inner * normed, axis=-1, keepdims=True)
    return scale * (inner - drop), jnp.sum(grad * normed, axis=0, keepdims=True)


def sum_parts(refs):
    total = refs[0][...].astype(F32)
    for ref in refs[1:]:
        total = total + ref[...].astype(F32)
    return total


def fill(refs, value):
    at = 0
    for ref in refs:
        ref[...] = value[at : at + ref.shape[0]].astype(ref.dtype)
        at += ref.shape[0]


def load(refs, scratch):
    at = 0
    for ref in refs:
        scratch[at : at + ref.shape[0]] = ref[...]
        at += ref.shape[0]


def piece_outs(state, count):
    return [((state.shape[0] // count, state.shape[1]), BF16)] * count


def embed_kernel(picks_ref, replies_ref, gains_ref, e_ref, h_ref, t_ref, *out_refs, root):
    length = h_ref.shape[0]
    rows = dot(picks_ref[...], replies_ref[...], TN)
    e_ref[...] = rows.astype(BF16)
    for start, first, state_ref, outs in ((0, 0, h_ref, out_refs[:-1]), (length, 4, t_ref, out_refs[-1:])):
        state = normal_form(rows[start : start + length] * root)[0] * gains_ref[first : first + 1, :]
        state_ref[...] = state
        fill(outs, normal_form(state)[0] * gains_ref[first + 1 : first + 2, :])


def sum_norm_kernel(state_ref, gains_ref, *refs, index, group):
    state = state_ref[...] + sum_parts(refs[:group])
    refs[group][...] = state
    fill(refs[group + 1 :], normal_form(state)[0] * gains_ref[index : index + 1, :])


def sum_norm(state, parts, gains, index, count):
    new, *pieces = call(
        partial(sum_norm_kernel, index=index, group=len(parts)), "sum_norm",
        [(state.shape, F32)] + piece_outs(state, count), [state, gains, *parts], flops=12 * state.size,
    )
    return new, pieces


def final_kernel(state_ref, gains_ref, live_ref, cot_ref, *refs, index, group):
    state = state_ref[...] + sum_parts(refs[:group])
    dec_ref, grad_ref, dg_ref, *outs = refs[group:]
    gain = gains_ref[index : index + 1, :]
    live = live_ref[...]
    dec_ref[...] = (normal_form(state)[0] * gain * live).astype(BF16)
    grad, dg_ref[...] = norm_grad(state, gain, cot_ref[...].astype(F32) * live)
    grad_ref[...] = grad
    fill(outs, grad)


def final(state, parts, gains, live, cotangent, index, count):
    decoded, grad, gain_grad, *pieces = call(
        partial(final_kernel, index=index, group=len(parts)), "final",
        [(state.shape, BF16), (state.shape, F32), ((1, state.shape[1]), F32)] + piece_outs(state, count),
        [state, gains, live, cotangent, *parts], flops=40 * state.size,
    )
    return decoded, grad, pieces, gain_grad


def norm_back_kernel(state_ref, gains_ref, *refs, index, group, adds):
    grad, dg = norm_grad(state_ref[...], gains_ref[index : index + 1, :], sum_parts(refs[:group]))
    refs = refs[group:]
    if adds:
        grad = grad + refs[0][...]
        refs = refs[1:]
    refs[0][...] = grad
    refs[1][...] = dg
    fill(refs[2:], grad)


def norm_back(grad, parts, state, gains, index, count):
    new, gain_grad, *pieces = call(
        partial(norm_back_kernel, index=index, group=len(parts), adds=grad is not None), "norm_back",
        [(state.shape, F32), ((1, state.shape[1]), F32)] + piece_outs(state, count),
        [far(state), gains, *parts] + ([] if grad is None else [grad]), flops=20 * state.size,
    )
    return new, pieces, gain_grad


def embed_back_kernel(grad_ref, state_ref, rows_ref, gains_ref, *refs, index, root, group):
    e_ref, dg_ref, de_ref = refs[group:]
    grad, dg_ref[...] = norm_grad(state_ref[...], gains_ref[index + 1 : index + 2, :], sum_parts(refs[:group]))
    rows = rows_ref[...].astype(F32) * root
    grad, de_ref[...] = norm_grad(rows, gains_ref[index : index + 1, :], grad + grad_ref[...])
    e_ref[...] = (grad * root).astype(BF16)


def embed_back(grad, parts, state, rows, gains, index, root):
    width = state.shape[1]
    return call(
        partial(embed_back_kernel, index=index, root=root, group=len(parts)), "embed_back",
        [(state.shape, BF16), ((1, width), F32), ((1, width), F32)], [grad, far(state), far(rows), gains, *parts],
        flops=40 * state.size,
    )


def weight_specs(weights):
    operands, specs = [], []
    for weight in weights:
        for array, block, index in weight:
            operands.append(far(array))
            specs.append(pl.BlockSpec(block, lambda *_, index=index: index))
    return operands, specs


def flat(ref):
    return ref[...].reshape(-1, ref.shape[-1])


def after(value, *others):
    return lax.optimization_barrier((value, *others))[0]


def far(values):
    return jax.tree.map(lambda value: pltpu.with_memory_space_constraint(value, pltpu.HBM), values)


def whole(array):
    return pl.BlockSpec(array.shape, lambda *_, rank=len(array.shape): (0,) * rank)


def pair_cols(own_ref, other_ref):
    return jnp.concatenate([flat(own_ref), flat(other_ref)], axis=1)


def project_kernel(*refs, pieces, count, scaled):
    x_ref = refs[-1]
    load(refs[:pieces], x_ref)
    refs = refs[pieces:-1]
    values = x_ref[...]
    for i in range(count):
        made = dot(values, pair_cols(refs[2 * i], refs[2 * i + 1]), NN).astype(BF16)
        if scaled and i == 0:
            refs[2 * count][...] = made * jnp.asarray(FACTOR, BF16)
        else:
            out_ref = refs[-1]
            at = (i - int(scaled)) * made.shape[1]
            out_ref[:, at : at + made.shape[1]] = made


def rows_of(pieces):
    return sum(piece.shape[0] for piece in pieces), pieces[0].shape[1]


def project(pieces, weights, shard, scaled):
    length, width = rows_of(pieces)
    operands, specs = weight_specs(weights)
    others = len(weights) - int(scaled)
    outs = [((length, 2 * shard), BF16)] * int(scaled) + [((length, 2 * shard * others), BF16)] * int(others > 0)
    return call(
        partial(project_kernel, pieces=len(pieces), count=len(weights), scaled=scaled), "project", outs,
        [*pieces, *operands], grid=(1,), in_specs=[whole(piece) for piece in pieces] + specs,
        out_specs=[pl.BlockSpec(shape, lambda *_: (0, 0)) for shape, _ in outs],
        scratch=[pltpu.VMEM((length, width), BF16)], flops=4 * length * width * shard * len(weights),
    )


def block_outs(length, width, group):
    shape = (length // group, width)
    return [(shape, BF16)] * group, [pl.BlockSpec(shape, lambda *_: (0, 0))] * group


def unproject_kernel(x_ref, own_ref, other_ref, *out_refs):
    fill(out_refs, dot(x_ref[...], pair_cols(own_ref, other_ref), NT))


def unproject(values, weight, width, group):
    operands, specs = weight_specs([weight])
    outs, out_specs = block_outs(values.shape[0], width, group)
    return call(
        unproject_kernel, "unproject", outs, [values] + operands, grid=(1,), in_specs=[whole(values)] + specs,
        out_specs=out_specs, flops=2 * values.size * width,
    )


def unproject_keys_kernel(*refs, lead, group):
    if lead:
        dq_ref, refs = refs[0], refs[1:]
    mine_ref, theirs_ref = refs[0], refs[1]
    weights, sum_ref, out_refs = refs[2 : -group - 1], refs[-group - 1], refs[-group:]
    summed = (mine_ref[...] + theirs_ref[...].astype(F32)).astype(BF16)
    sum_ref[...] = summed
    span = summed.shape[1] // 2
    total = dot(summed[:, :span], pair_cols(*weights[-4:-2]), NT) + dot(summed[:, span:], pair_cols(*weights[-2:]), NT)
    if lead:
        total = total + dot(dq_ref[...], pair_cols(*weights[:2]), NT)
    fill(out_refs, total)


def unproject_keys(queries_grad, mine, theirs, weights, width, group):
    lead = queries_grad is not None
    operands, specs = weight_specs(weights)
    values = ([queries_grad] if lead else []) + [mine, theirs]
    outs, out_specs = block_outs(mine.shape[0], width, group)
    summed, *parts = call(
        partial(unproject_keys_kernel, lead=lead, group=group), "unproject_keys", [(theirs.shape, BF16)] + outs,
        values + operands, grid=(1,), in_specs=[whole(v) for v in values] + specs, out_specs=[whole(theirs)] + out_specs,
        flops=2 * mine.size * width * len(weights) // 2,
    )
    return parts, summed


def mask_block(sq_ref, sk_ref, pq_ref, base_ref, causal):
    seen = dot(sk_ref[...], sq_ref[...], TN)
    if causal:
        blocks = base_ref.shape[0]
        size = seen.shape[0] // blocks
        index = lax.broadcasted_iota(jnp.int32, (size, seen.shape[1]), 0)
        passed = pq_ref[...]
        seen = jnp.concatenate(
            [
                jnp.where(passed >= index + base_ref[b : b + 1, :], seen[b * size : (b + 1) * size], 0.0)
                for b in range(blocks)
            ]
        )
    return (1.0 - seen) * MASKED


def gather_keys(kv_ref, mine_ref, theirs_ref):
    half = mine_ref.shape[0]
    kv_ref[:half] = mine_ref[...]
    kv_ref[half:] = theirs_ref[...]


def attend_kernel(
    q_ref, mine_ref, theirs_ref, wo_ref, wo2_ref, sq_ref, sk_ref, pq_ref, pk_ref, o_ref, st_ref, *refs, causal, heads
):
    part_refs, kv_ref, part_ref = refs[:-2], refs[-2], refs[-1]

    @pl.when(pl.program_id(0) == 0)
    def _():
        gather_keys(kv_ref, mine_ref, theirs_ref)

    width = heads * HEAD_DIM
    hidden = mask_block(sq_ref, sk_ref, pq_ref, pk_ref, causal)
    for head in range(heads):
        lo, hi = head * HEAD_DIM, (head + 1) * HEAD_DIM
        scores = dot(kv_ref[:, lo:hi], q_ref[:, lo:hi], NT) + hidden
        peak = jnp.max(scores, axis=0, keepdims=True)
        raised = jnp.exp(scores - peak)
        inverse = 1.0 / jnp.sum(raised, axis=0, keepdims=True)
        probs = (raised * inverse).astype(BF16)
        mixed = dot(kv_ref[:, width + lo : width + hi], probs, TN)
        o_ref[:, lo:hi] = mixed.T.astype(BF16)
        st_ref[head : head + 1, :] = peak
        st_ref[heads + head : heads + head + 1, :] = inverse
    half = width // 2
    part = dot(o_ref[:, :half], flat(wo_ref), NN) + dot(o_ref[:, half:], flat(wo2_ref), NN)
    step = part.shape[0]
    part_ref[pl.ds(pl.program_id(0) * step, step)] = part.astype(BF16)

    @pl.when(pl.program_id(0) == pl.num_programs(0) - 1)
    def _():
        fill(part_refs, part_ref)


def mask_specs(step, keys_len, blocks):
    return [
        pl.BlockSpec((SEGMENTS, step), lambda i: (0, i)),
        pl.BlockSpec((SEGMENTS, keys_len), lambda i: (0, 0)),
        pl.BlockSpec((1, step), lambda i: (0, i)),
        pl.BlockSpec((blocks, step), lambda i: (0, 0)),
    ]


def attend(queries, mine, theirs, out_weight, marks, causal, model, group):
    length, width = queries.shape
    keys_len = 2 * length
    heads = width // HEAD_DIM
    step = min(256, length)
    rows = pl.BlockSpec((step, width), lambda i: (i, 0))
    operands, specs = weight_specs([out_weight])
    outs, out_specs = block_outs(length, model, group)
    mixed, stats, *parts = call(
        partial(attend_kernel, causal=causal, heads=heads), "attend",
        [((length, width), BF16), ((2 * heads, length), F32)] + outs,
        [queries, mine, theirs] + operands + list(marks), grid=(length // step,),
        in_specs=[rows, whole(mine), whole(theirs)] + specs + mask_specs(step, keys_len, marks[3].shape[0]),
        out_specs=[rows, pl.BlockSpec((2 * heads, step), lambda i: (0, i))] + out_specs,
        scratch=[pltpu.VMEM((keys_len, 2 * width), BF16), pltpu.VMEM((length, model), BF16)],
        flops=4 * length * keys_len * width, exps=length * keys_len * heads,
    )
    return parts, mixed, stats


def attend_back_kernel(
    wo_ref, wo2_ref, q_ref, mine_ref, theirs_ref, sq_ref, sk_ref, pq_ref, pk_ref, st_ref, *refs, causal, heads
):
    pieces, (dq_ref, dmine_ref, dtheirs_ref, kv_ref, dkv_ref, do_ref, g_ref) = refs[:-7], refs[-7:]
    width = heads * HEAD_DIM
    half = width // 2
    step = dq_ref.shape[0]

    @pl.when(pl.program_id(0) == 0)
    def _():
        gather_keys(kv_ref, mine_ref, theirs_ref)
        dkv_ref[...] = jnp.zeros_like(dkv_ref)
        load(pieces, g_ref)

    grad = g_ref[pl.ds(pl.program_id(0) * step, step)]
    do_ref[:, :half] = dot(grad, flat(wo_ref), NT).astype(BF16)
    do_ref[:, half:] = dot(grad, flat(wo2_ref), NT).astype(BF16)
    hidden = mask_block(sq_ref, sk_ref, pq_ref, pk_ref, causal)
    for head in range(heads):
        lo, hi = head * HEAD_DIM, (head + 1) * HEAD_DIM
        queries, grads = q_ref[:, lo:hi], do_ref[:, lo:hi]
        keys, values = kv_ref[:, lo:hi], kv_ref[:, width + lo : width + hi]
        scores = dot(keys, queries, NT) + hidden
        probs = jnp.exp(scores - st_ref[head : head + 1, :]) * st_ref[heads + head : heads + head + 1, :]
        grad_probs = dot(values, grads, NT)
        inner = jnp.sum(probs * grad_probs, axis=0, keepdims=True)
        grad_scores = (probs * (grad_probs - inner)).astype(BF16)
        dq_ref[:, lo:hi] = (dot(keys, grad_scores, TN) * FACTOR).T.astype(BF16)
        dkv_ref[:, lo:hi] += dot(grad_scores, queries, NN)
        dkv_ref[:, width + lo : width + hi] += dot(probs.astype(BF16), grads, NN)

    @pl.when(pl.program_id(0) == pl.num_programs(0) - 1)
    def _():
        keys_half = dmine_ref.shape[0]
        dmine_ref[...] = dkv_ref[:keys_half]
        dtheirs_ref[...] = dkv_ref[keys_half:].astype(BF16)


def attend_back(pieces, out_weight, queries, mine, theirs, marks, stats, causal):
    length, width = queries.shape
    model = pieces[0].shape[1]
    keys_len = 2 * length
    heads = width // HEAD_DIM
    step = min(256, length)
    rows = pl.BlockSpec((step, width), lambda i: (i, 0))
    operands, specs = weight_specs([out_weight])
    return call(
        partial(attend_back_kernel, causal=causal, heads=heads), "attend_back",
        [((length, width), BF16), ((length, 2 * width), F32), ((length, 2 * width), BF16)],
        operands + far([queries, mine, theirs, *marks, stats]) + [*pieces], grid=(length // step,),
        in_specs=specs
        + [rows, whole(mine), whole(theirs)]
        + mask_specs(step, keys_len, marks[3].shape[0])
        + [pl.BlockSpec((2 * heads, step), lambda i: (0, i))]
        + [whole(piece) for piece in pieces],
        out_specs=[rows, whole(mine), whole(mine)],
        scratch=[
            pltpu.VMEM((keys_len, 2 * width), BF16),
            pltpu.VMEM((keys_len, 2 * width), F32),
            pltpu.VMEM((step, width), BF16),
            pltpu.VMEM((length, model), BF16),
        ],
        flops=10 * length * keys_len * width, exps=length * keys_len * heads,
    )


def attend_grads_kernel(*refs, pieces):
    sources, (dq_ref, dkv_ref, o_ref, out_ref), scratch = refs[:-7], refs[-7:-3], refs[-3:]
    for i, count in enumerate(pieces):
        load(sources[:count], scratch[i])
        sources = sources[count:]
    xq_ref, g_ref = scratch[0], scratch[1]
    xkv_ref = scratch[2] if len(pieces) > 2 else xq_ref
    shard = out_ref.shape[2]
    for index, (cols_ref, at, rhs_ref) in enumerate(
        ((dq_ref, 0, xq_ref), (dkv_ref, 0, xkv_ref), (dkv_ref, 2 * shard, xkv_ref), (o_ref, 0, g_ref))
    ):
        both = dot(cols_ref[:, at : at + 2 * shard], rhs_ref[...], TN).astype(BF16)
        out_ref[0, index] = both[:shard]
        out_ref[1, index] = both[shard:]


def attend_grads(grad_q, grad_kv, mixed, *sources):
    length, model = rows_of(sources[0])
    shard = mixed.shape[1] // 2
    return call(
        partial(attend_grads_kernel, pieces=[len(source) for source in sources]), "attend_grads",
        [((2, 4, shard, model), BF16)], [piece for source in sources for piece in source] + [grad_q, grad_kv, far(mixed)],
        scratch=[pltpu.VMEM((length, model), BF16)] * 3, flops=16 * length * model * shard,
    )[0]


def gelu_pair(pre_act):
    phi_big = 0.5 * (1.0 + lax.erf(pre_act * (1.0 / math.sqrt(2.0))))
    phi_small = jnp.exp(-0.5 * pre_act * pre_act) * (1.0 / math.sqrt(2.0 * math.pi))
    return pre_act * phi_big, phi_big + pre_act * phi_small


def ffn_step(total, acc_ref, out_refs):
    step = pl.program_id(0)

    @pl.when(step == 0)
    def _():
        acc_ref[...] = total

    @pl.when(step > 0)
    def _():
        acc_ref[...] += total

    @pl.when(step == pl.num_programs(0) - 1)
    def _():
        fill(out_refs, acc_ref)


def ffn_kernel(up_ref, up2_ref, dn_ref, dn2_ref, *refs, pieces):
    sources, (act_ref, slope_ref), out_refs, (acc_ref, x_ref) = refs[:pieces], refs[pieces : pieces + 2], refs[pieces + 2 : -2], refs[-2:]

    @pl.when(pl.program_id(0) == 0)
    def _():
        load(sources, x_ref)

    total = None
    for side, (up, down) in enumerate(((up_ref, dn_ref), (up2_ref, dn2_ref))):
        act, slope = gelu_pair(dot(x_ref[...], up[...], NN))
        act = act.astype(BF16)
        act_ref[side] = act
        slope_ref[side] = slope
        term = dot(act, flat(down), NN)
        total = term if total is None else total + term
    ffn_step(total, acc_ref, out_refs)


def ffn_specs(pieces, ups, downs):
    length, model = rows_of(pieces)
    hidden = ups[0].shape[1]
    step = min(256, hidden)
    cols = pl.BlockSpec((model, step), lambda i: (0, i))
    rows = pl.BlockSpec((step, model), lambda i: (i, 0))
    other_rows = rows
    if downs[1].ndim == 3:
        share = hidden // downs[1].shape[0]
        other_rows = pl.BlockSpec((step // share, share, model), lambda i: (i, 0, 0))
    made = pl.BlockSpec((2, length, step), lambda i: (0, 0, i))
    scratch = [pltpu.VMEM((length, model), F32), pltpu.VMEM((length, model), BF16)]
    return length, model, hidden, step, [cols, cols, rows, other_rows], made, [whole(piece) for piece in pieces], scratch


def ffn(pieces, ups, downs, group):
    length, model, hidden, step, specs, made, piece_specs, scratch = ffn_specs(pieces, ups, downs)
    outs, out_specs = block_outs(length, model, group)
    acts, slopes, *parts = call(
        partial(ffn_kernel, pieces=len(pieces)), "ffn",
        [((2, length, hidden), BF16), ((2, length, hidden), F32)] + outs,
        [*far(ups), *far(downs), *pieces], grid=(hidden // step,), in_specs=specs + piece_specs,
        out_specs=[made, made] + out_specs, scratch=scratch, flops=8 * length * model * hidden, exps=4 * length * hidden,
    )
    return parts, acts, slopes


def ffn_back_kernel(up_ref, up2_ref, dn_ref, dn2_ref, slope_ref, *refs, pieces):
    sources, dz_ref, out_refs, (acc_ref, g_ref) = refs[:pieces], refs[pieces], refs[pieces + 1 : -2], refs[-2:]

    @pl.when(pl.program_id(0) == 0)
    def _():
        load(sources, g_ref)

    total = None
    for side, (up, down) in enumerate(((up_ref, dn_ref), (up2_ref, dn2_ref))):
        grad_pre = (slope_ref[side] * dot(g_ref[...], flat(down), NT)).astype(BF16)
        dz_ref[side] = grad_pre
        term = dot(grad_pre, up[...], NT)
        total = term if total is None else total + term
    ffn_step(total, acc_ref, out_refs)


def ffn_back(pieces, ups, downs, slopes, group):
    length, model, hidden, step, specs, made, piece_specs, scratch = ffn_specs(pieces, ups, downs)
    outs, out_specs = block_outs(length, model, group)
    grad_pre, *parts = call(
        partial(ffn_back_kernel, pieces=len(pieces)), "ffn_back", [((2, length, hidden), BF16)] + outs,
        [*far(ups), *far(downs), far(slopes), *pieces], grid=(hidden // step,), in_specs=specs + [made] + piece_specs,
        out_specs=[made] + out_specs, scratch=scratch, flops=8 * length * model * hidden,
    )
    return parts, grad_pre


def ffn_grads_kernel(dz_ref, act_ref, *refs):
    sources, (out_ref, x_ref, g_ref) = refs[:-3], refs[-3:]

    @pl.when((pl.program_id(0) == 0) & (pl.program_id(1) == 0))
    def _():
        load(sources[: len(sources) // 2], x_ref)
        load(sources[len(sources) // 2 :], g_ref)

    out_ref[0, 0] = dot(dz_ref[0], x_ref[...], TN).astype(BF16)
    out_ref[0, 1] = dot(act_ref[0], g_ref[...], TN).astype(BF16)


def ffn_grads(pieces, grads, grad_pre, acts):
    length, model = rows_of(pieces)
    hidden = acts.shape[2]
    step = min(256, hidden)
    made = pl.BlockSpec((1, length, step), lambda s, i: (s, 0, i))
    return call(
        ffn_grads_kernel, "ffn_grads", [((2, 2, hidden, model), BF16)], [grad_pre, far(acts), *far(pieces), *grads],
        grid=(2, hidden // step), in_specs=[made, made] + [whole(p) for p in (*pieces, *grads)],
        out_specs=[pl.BlockSpec((1, 2, step, model), lambda s, i: (s, 0, i, 0))],
        scratch=[pltpu.VMEM((length, model), BF16)] * 2, flops=8 * length * model * hidden,
    )[0]


class Places:
    def __init__(self):
        self.dp_size = lax.axis_size("dp")
        self.tensor_size = lax.axis_size("tensor")
        self.group = self.tensor_size // 2
        self.dp_index = lax.axis_index("dp")
        tensor_index = lax.axis_index("tensor")
        self.core = self.dp_index % 2
        self.place = tensor_index % self.group
        self.pieces = 2 if self.group == 4 else 1

    def swap(self, value):
        pairs = []
        for dp_index in range(self.dp_size):
            for tensor_index in range(self.tensor_size):
                pair, core = divmod(dp_index, 2)
                side, place = divmod(tensor_index, self.group)
                pairs.append(
                    (
                        dp_index * self.tensor_size + tensor_index,
                        (2 * pair + side) * self.tensor_size + core * self.group + place,
                    )
                )
        return lax.ppermute(value, ("dp", "tensor"), pairs)

    def other_core(self, value):
        return lax.ppermute(value, "dp", [(d, d ^ 1) for d in range(self.dp_size)])

    def partner(self, value):
        return lax.ppermute(value, "tensor", [(t, t ^ self.group) for t in range(self.tensor_size)])

    def mate(self, value, offset):
        return lax.ppermute(value, "tensor", [(t, t ^ offset) for t in range(self.tensor_size)])

    def gather(self, pieces):
        if self.pieces == 2:
            low, high = pieces
            low_1, high_2 = self.mate(low, 1), self.mate(high, 2)
            high_1, low_2 = self.mate(high, 1), self.mate(low, 2)
            high_3, low_3 = self.mate(high_2, 1), self.mate(low_1, 2)
            return [low, high, low_1, high_1, low_2, high_2, low_3, high_3]
        return list(pieces) + [self.mate(pieces[0], o) for o in range(1, self.group)]

    def gather_beside(self, block):
        return [block] + [self.mate(block, o) for o in range(1, self.group)]

    def scatter(self, parts):
        return [parts[0]] + [self.mate(parts[o], o) for o in range(1, self.group)]

    def share(self, stacked):
        rows = stacked.shape[0] // self.dp_size
        return lax.dynamic_slice_in_dim(stacked, self.dp_index * rows, rows, 0)

    def split(self, weights):
        rows = weights.shape[1] // self.dp_size
        return lax.dynamic_slice_in_dim(weights, self.dp_index * rows, rows, 1)

    def whole(self, share):
        return lax.all_gather(share, "dp", axis=0)

    def whole_rows(self, share):
        return lax.all_gather(share, "dp", axis=0, tiled=True)

    def sum_weights(self, grads):
        shape = grads.shape
        summed = lax.psum_scatter(grads.reshape(-1, shape[-1]), "dp", scatter_dimension=1, tiled=True)
        return summed.reshape(*shape[:-1], -1)

    def sum_weights_now(self, grads):
        if self.dp_size != 4:
            return self.sum_weights(grads)
        width = grads.shape[-1] // 4
        blocks = [grads[..., i * width : (i + 1) * width] for i in range(4)]
        first = self.core == 0

        def pick(if_first, low, high):
            return jnp.where(if_first, low, high)

        kept = jnp.concatenate([pick(first, *blocks[:2]), pick(first, *blocks[2:])], axis=-1)
        sent = jnp.concatenate([pick(first, *blocks[1::-1]), pick(first, *blocks[:1:-1])], axis=-1)
        kept = kept.astype(F32) + self.other_core(sent).astype(F32)
        low, high = kept[..., :width], kept[..., width:]
        first = self.dp_index < 2
        sent = pick(first, high, low).astype(BF16)
        received = lax.ppermute(sent, "dp", [(d, d ^ 2) for d in range(4)])
        return (pick(first, low, high) + received.astype(F32)).astype(BF16)

    def marks(self, seg_row, seg_key_row):
        kinds = jnp.arange(SEGMENTS)[:, None] - 1
        length = seg_row.shape[0] // self.tensor_size
        order = self.place ^ jnp.arange(self.group)
        blocks = jnp.concatenate([self.core * self.group + order, (1 - self.core) * self.group + order])
        own = jnp.take(seg_row.reshape(-1, length), blocks[: self.group], axis=0).reshape(1, -1)
        keys = jnp.take(seg_key_row.reshape(-1, length), blocks, axis=0).reshape(1, -1)
        positions = (blocks[: self.group, None] * length + jnp.arange(length)[None, :]).reshape(1, -1)
        return (
            ((own == kinds) | (own < 0)).astype(BF16),
            (keys == kinds).astype(BF16),
            positions,
            jnp.broadcast_to(blocks[:, None] * length, (blocks.shape[0], own.shape[1])),
        )


def route(places, token_ids, token_live, shard_rows):
    owners = places.dp_size * places.tensor_size
    tokens = token_ids.shape[0]
    capacity = max(2, 3 * tokens // (2 * owners))
    owner = token_ids // shard_rows
    row = token_ids - owner * shard_rows
    earlier = jnp.arange(tokens)[None, :] < jnp.arange(tokens)[:, None]
    same = (owner[:, None] == owner[None, :]) & token_live[None, :] & earlier
    ranking = jnp.sum(same.astype(jnp.int32), axis=1)
    slot = jnp.where(token_live, owner * capacity + ranking, -1)
    picks = jnp.arange(owners * capacity)[:, None] == slot[None, :]
    requests = jnp.sum(jnp.where(picks, row[None, :] + 1, 0), axis=1) - 1
    return picks.astype(BF16), requests.reshape(owners, capacity)


def to_owners(places, rows, capacity):
    owners = places.dp_size * places.tensor_size
    return lax.all_to_all(
        rows.reshape(owners, capacity, -1), ("dp", "tensor"), split_axis=0, concat_axis=0, tiled=True
    )


def send_back_kernel(picks_ref, e_ref, e2_ref, last_ref, *refs):
    gain_refs, out_ref, rows_ref = refs[:-2], refs[-2], refs[-1]
    length = e_ref.shape[0]
    rows_ref[...] = jnp.zeros_like(rows_ref)
    for i, ref in enumerate(gain_refs):
        rows_ref[i : i + 1] = ref[...]
    sent = dot(picks_ref[:, :length], e_ref[...], NN) + dot(picks_ref[:, length:], e2_ref[...], NN)
    out_ref[...] = (sent + dot(last_ref[...], rows_ref[...].astype(BF16), NN)).astype(BF16)


def send_back(picks, src_grad, tgt_grad, gains, capacity):
    owners = picks.shape[0] // capacity
    slots = jnp.arange(owners * (capacity + 1))
    owner, slot = slots // (capacity + 1), slots % (capacity + 1)
    wider = jnp.take(picks, jnp.minimum(owner * capacity + slot, picks.shape[0] - 1), axis=0)
    wider = jnp.where((slot < capacity)[:, None], wider, jnp.zeros_like(wider))
    rows = 16
    last = (slot == capacity)[:, None] & (owner[:, None] == jnp.arange(rows)[None, :])
    return call(
        send_back_kernel, "send_back", [((slots.shape[0], src_grad.shape[1]), BF16)],
        [wider, src_grad, tgt_grad, last.astype(BF16), *gains], scratch=[pltpu.VMEM((rows, src_grad.shape[1]), F32)],
        flops=2 * wider.size * src_grad.shape[1],
    )[0]


def on_device(
    src_ids,
    tgt_ids,
    src_segs,
    tgt_segs,
    embed_table,
    norm_gains,
    enc_qkv,
    enc_out,
    enc_up,
    enc_down,
    dec_qkv,
    dec_out,
    cross_q,
    cross_kv,
    cross_out,
    dec_up,
    dec_down,
    cotangent,
):
    places = Places()
    group = places.group
    local_len = src_ids.shape[0]
    shard_rows, model = embed_table.shape
    root = math.sqrt(model)
    shard = enc_qkv.shape[2]
    count = places.pieces

    tensor_at = lax.axis_index("tensor") * local_len
    rows_here = [src_segs.reshape(-1), tgt_segs.reshape(-1)]
    ids_here = jnp.concatenate([src_ids.reshape(-1), tgt_ids.reshape(-1)])
    live_here = jnp.concatenate([lax.dynamic_slice_in_dim(row, tensor_at, local_len, 0) for row in rows_here]) >= 0
    enc_in_share = places.partner(places.split(enc_qkv))
    requests = route(places, ids_here, live_here, shard_rows)[1]
    capacity = requests.shape[1]
    moved = places.swap(jnp.concatenate([ids_here] + rows_here))
    wanted = lax.all_to_all(requests, ("dp", "tensor"), split_axis=0, concat_axis=0, tiled=True)
    wanted = wanted.reshape(-1, 2, 2, group * capacity).swapaxes(1, 2).reshape(-1)
    wanted = after(wanted, moved, enc_in_share)
    found = wanted >= 0
    picked = jnp.take(embed_table, jnp.maximum(wanted, 0), axis=0)
    replies = to_owners(places, picked, capacity).reshape(picked.shape)
    outs_share = jnp.concatenate([places.share(weight) for weight in (enc_out, dec_out, cross_out)])
    outs_share = places.partner(after(outs_share, picked))
    replies = after(replies, outs_share)
    cross_share = jnp.concatenate([places.split(cross_q[None]), places.split(cross_kv)])

    token_ids = moved[: 2 * local_len]
    src_row, tgt_row = jnp.split(moved[2 * local_len :], 2)
    offset = (places.core * group + places.place) * local_len
    live = [lax.dynamic_slice_in_dim(row, offset, local_len, 0) >= 0 for row in (src_row, tgt_row)]
    picks = route(places, token_ids, jnp.concatenate(live), shard_rows)[0]
    enc_marks = places.marks(src_row, src_row)
    dec_marks = places.marks(tgt_row, tgt_row)
    cross_marks = places.marks(tgt_row, src_row)

    def narrow(own, own_index, other, other_index):
        if own.ndim == 2:
            own_part = (own, own.shape, (0, 0))
        else:
            own_part = (own, (1, *own.shape[1:]), (own_index, 0, 0))
        return own_part, (other, (other.shape[0], 1, *other.shape[2:]), (0, other_index, 0, 0))

    def wide(own, other, index):
        rows = own.shape[0] // places.dp_size
        return (own, own.shape, (0, 0)), (other, (other.shape[0], rows, model), (0, index, 0))

    def narrow_whole(share, start):
        share = after(share, start)
        return places.whole(jnp.concatenate([share, share]))

    enc_in_other = narrow_whole(enc_in_share, picked)
    enc_in = [narrow(enc_qkv, i, enc_in_other, i) for i in range(3)]

    token_shape = (local_len, model)
    embeds, h0, t0, *pieces = call(
        partial(embed_kernel, root=root), "embed",
        [((2 * local_len, model), BF16), (token_shape, F32), (token_shape, F32)] + [((local_len // count, model), BF16)] * count + [(token_shape, BF16)],
        [picks, replies, norm_gains],
    )
    a1, c1 = pieces[:-1], pieces[-1]
    down_rows = enc_down.shape[0] // places.dp_size
    out_rows = shard // places.dp_size
    outs_other = narrow_whole(outs_share, a1)
    dec_in_share = places.partner(after(places.split(dec_qkv), a1))
    a1 = places.gather(a1)
    c1 = places.gather_beside(after(c1, a1))
    out_rows = shard // places.dp_size
    if out_rows % 8:
        outs_other = [outs_other[:, i * out_rows : (i + 1) * out_rows] for i in range(3)]
        enc_o, dec_o, cross_o = [wide(own, other, 0) for own, other in zip((enc_out, dec_out, cross_out), outs_other)]
    else:
        enc_o, dec_o, cross_o = [wide(own, outs_other, i) for i, own in enumerate((enc_out, dec_out, cross_out))]
    enc_q, enc_mine = project(a1, enc_in, shard, True)
    dec_in_other = narrow_whole(dec_in_share, enc_mine)
    dec_in = [narrow(dec_qkv, i, dec_in_other, i) for i in range(3)]
    enc_theirs = places.other_core(enc_mine)
    parts, enc_mixed, enc_stats = attend(enc_q, enc_mine, enc_theirs, enc_o, enc_marks, False, model, group)
    enc_up_share = places.partner(after(places.share(enc_up), enc_mine))
    enc_down_share = places.partner(after(places.share(enc_down), enc_mine))
    own_parts = after(parts, enc_up_share, c1)
    enc_ups = [enc_up, places.whole_rows(after(enc_up_share, own_parts))]
    parts = places.scatter(own_parts)
    dec_q, dec_mine = project(after(c1, own_parts), dec_in, shard, True)
    dec_theirs = places.other_core(dec_mine)
    cross_share = places.partner(after(cross_share, dec_mine))
    cot_moved = places.swap(after(cotangent.reshape(token_shape).astype(BF16), dec_mine))
    dec_parts, dec_mixed, dec_stats = attend(
        after(dec_q, enc_down_share), dec_mine, dec_theirs, dec_o, dec_marks, True, model, group
    )
    enc_downs = [enc_down, places.whole_rows(after(enc_down_share, dec_q))]
    h1, own_b1 = sum_norm(h0, after(parts, dec_parts, cot_moved), norm_gains, 2, count)

    b1 = places.gather(own_b1)
    cross_other = narrow_whole(cross_share, own_b1)
    dec_parts = places.scatter(after(dec_parts, own_b1))
    t1, (own_c2,) = sum_norm(t0, after(dec_parts, b1), norm_gains, 6, 1)
    dec_up_share = places.partner(after(places.share(dec_up), own_c2))
    b1 = after(b1, own_c2)
    c2 = places.gather_beside(own_c2)
    own_parts, enc_acts, enc_slopes = ffn(b1, enc_ups, enc_downs, group)
    own_parts = after(own_parts, c2)
    cross_in = narrow(cross_q, 0, cross_other, 0)
    cross_mem = [narrow(cross_kv, i, cross_other, 1 + i) for i in range(2)]
    parts = places.scatter(own_parts)
    h2, own_memory = sum_norm(h1, parts, norm_gains, 3, count)
    dec_ups = [dec_up, places.whole_rows(after(dec_up_share, own_memory))]
    memory = places.gather(own_memory)
    cross_qs = project(after(c2, own_memory), [cross_in], shard, True)[0]
    cross_mine = project(after(memory, cross_qs), cross_mem, shard, False)[0]
    dec_down_share = places.partner(after(places.share(dec_down), cross_mine))
    cross_theirs = places.other_core(cross_mine)
    parts, cross_mixed, cross_stats = attend(
        cross_qs, cross_mine, cross_theirs, cross_o, cross_marks, False, model, group
    )
    dec_downs = [dec_down, places.whole_rows(after(dec_down_share, parts))]
    t2, own_f1 = sum_norm(t1, places.scatter(parts), norm_gains, 7, count)
    f1 = places.gather(own_f1)
    parts, dec_acts, dec_slopes = ffn(f1, dec_ups, dec_downs, group)
    decoded, grad_t, pieces, gain_final = final(
        t2, places.scatter(parts), norm_gains, live[1][:, None].astype(F32), cot_moved, 8, count
    )

    grad_full = places.gather(pieces)
    decoded = places.swap(after(decoded, grad_full))
    own_parts, grad_pre = ffn_back(grad_full, dec_ups, dec_downs, dec_slopes, group)
    dec_ffn_grads = ffn_grads(f1, after(grad_full, own_parts), grad_pre, dec_acts)
    parts = after(places.scatter(own_parts), dec_ffn_grads)
    grad_t, pieces, gain_dffn = norm_back(grad_t, parts, t2, norm_gains, 7, count)

    dec_ffn_sum = places.sum_weights(after(dec_ffn_grads, pieces))
    grad_full = after(places.gather(pieces), decoded)
    grad_q, mine, theirs = attend_back(
        grad_full, cross_o, cross_qs, cross_mine, cross_theirs, cross_marks, cross_stats, False
    )
    theirs = places.other_core(theirs)
    own_parts = unproject(grad_q, cross_in, model, group)
    own_mem_parts, grad_kv = unproject_keys(None, mine, after(theirs, own_parts), cross_mem, model, group)
    mem_parts = places.scatter(own_mem_parts)
    cross_grads = attend_grads(grad_q, grad_kv, cross_mixed, far(c2), after(grad_full, own_mem_parts), far(memory))
    grad_h, pieces_h, gain_memory = norm_back(None, after(mem_parts, cross_grads), h2, norm_gains, 3, count)
    cross_sum = places.sum_weights(after(cross_grads, pieces_h))

    enc_full = places.gather(pieces_h)
    parts = places.scatter(after(own_parts, enc_full))
    dec_ffn_other = places.partner(after(dec_ffn_sum[1], enc_full))
    own_parts, grad_pre = ffn_back(enc_full, enc_ups, enc_downs, enc_slopes, group)
    h_parts = places.scatter(own_parts)
    enc_ffn_grads = ffn_grads(b1, after(enc_full, own_parts), grad_pre, enc_acts)
    grad_t, pieces, gain_cross = norm_back(grad_t, after(parts, enc_ffn_grads, dec_ffn_sum), t1, norm_gains, 6, count)
    dec_full = places.gather(pieces)
    grad_h, pieces_h, gain_effn = norm_back(grad_h, after(h_parts, pieces), h1, norm_gains, 2, 1)
    hidden_full = places.gather_beside(pieces_h[0])
    dec_full = after(dec_full, pieces_h, dec_ffn_other)
    cross_sum_other = places.partner(after(cross_sum[1], dec_full))
    enc_ffn_sum = places.sum_weights(after(enc_ffn_grads, cross_sum, pieces_h))
    grad_q, mine, theirs = attend_back(dec_full, dec_o, dec_q, dec_mine, dec_theirs, dec_marks, dec_stats, True)
    theirs = places.other_core(theirs)
    own_parts, grad_kv = unproject_keys(grad_q, mine, theirs, dec_in, model, group)
    dec_parts = places.scatter(own_parts)
    dec_grads = attend_grads(grad_q, grad_kv, dec_mixed, far(c1), after(dec_full, own_parts))

    grad_full = after(hidden_full, dec_grads, cross_sum_other)
    enc_ffn_other = places.partner(after(enc_ffn_sum[1], grad_full))
    grad_q, mine, theirs = attend_back(grad_full, enc_o, enc_q, enc_mine, enc_theirs, enc_marks, enc_stats, False)
    theirs = places.other_core(theirs)
    dec_sum = places.sum_weights(after(dec_grads, enc_ffn_sum, grad_full))
    own_parts, grad_kv = unproject_keys(grad_q, mine, theirs, enc_in, model, group)
    parts = places.scatter(after(own_parts, enc_ffn_other))
    tgt_grad, gain_dattn, gain_demb = embed_back(
        grad_t, after(dec_parts, own_parts), t0, embeds[local_len:], norm_gains, 4, root
    )
    src_grad, gain_eattn, gain_eemb = embed_back(
        grad_h, after(parts, tgt_grad), h0, embeds[:local_len], norm_gains, 0, root
    )

    gains = [
        gain_eemb, gain_eattn, gain_effn, gain_memory, gain_demb, gain_dattn, gain_cross, gain_dffn, gain_final
    ]
    outgoing = send_back(picks, src_grad, tgt_grad, gains, capacity)
    arrived = to_owners(places, outgoing, capacity + 1)
    enc_grads = attend_grads(grad_q, grad_kv, enc_mixed, far(a1), after(grad_full, outgoing))
    enc_sum = places.sum_weights_now(enc_grads)
    dec_sum_other = places.partner(after(dec_sum[1], outgoing))
    enc_sum_other = places.partner(enc_sum[1])
    arrived = after(arrived, enc_sum)
    gain_sum = jnp.sum(arrived[:, capacity].astype(F32), axis=0)
    gain_grad = lax.all_to_all(
        jnp.broadcast_to(gain_sum[None], (arrived.shape[0], model)), ("dp", "tensor"), 0, 0, tiled=True
    )[: len(gains)]
    counts = jnp.sum(((wanted[:, None] == wanted[None, :]) & found[None, :]).astype(F32), axis=1)
    rows = arrived[:, :capacity].reshape(-1, model).astype(F32) / jnp.maximum(counts, 1.0)[:, None]
    target_rows = jnp.where(found, wanted, shard_rows)
    table_grad = jnp.zeros((shard_rows, model), F32).at[target_rows].add(rows, mode="drop")

    def finish(summed, other):
        return summed[0].astype(F32) + other.astype(F32)

    dec_ffn_sum = finish(dec_ffn_sum, dec_ffn_other)
    cross_sum = finish(cross_sum, cross_sum_other)
    enc_ffn_sum = finish(enc_ffn_sum, enc_ffn_other)
    dec_sum = finish(dec_sum, dec_sum_other)
    enc_sum = finish(enc_sum, enc_sum_other)

    def turned(grads):
        return jnp.swapaxes(grads, -1, -2)

    return (
        decoded.astype(F32)[:, None],
        table_grad,
        gain_grad,
        turned(enc_sum[:3]),
        enc_sum[3],
        turned(enc_ffn_sum[0]),
        enc_ffn_sum[1],
        turned(dec_sum[:3]),
        dec_sum[3],
        turned(cross_sum[0]),
        turned(cross_sum[1:3]),
        cross_sum[3],
        turned(dec_ffn_sum[0]),
        dec_ffn_sum[1],
    )


def solution(mesh):
    return jax.shard_map(
        on_device,
        mesh=mesh,
        in_specs=(
            P("tensor", "dp"),
            P("tensor", "dp"),
            P(None, "dp"),
            P(None, "dp"),
            P(("dp", "tensor"), None),
            P(),
            P(None, None, "tensor"),
            P("tensor", None),
            P(None, "tensor"),
            P("tensor", None),
            P(None, None, "tensor"),
            P("tensor", None),
            P(None, "tensor"),
            P(None, None, "tensor"),
            P("tensor", None),
            P(None, "tensor"),
            P("tensor", None),
            P("tensor", "dp", None),
        ),
        out_specs=(
            P("tensor", "dp", None),
            P(("dp", "tensor"), None),
            P(),
            P(None, "dp", "tensor"),
            P("tensor", "dp"),
            P("dp", "tensor"),
            P("tensor", "dp"),
            P(None, "dp", "tensor"),
            P("tensor", "dp"),
            P("dp", "tensor"),
            P(None, "dp", "tensor"),
            P("tensor", "dp"),
            P("dp", "tensor"),
            P("tensor", "dp"),
        ),
        check_vma=False,
    )
```

time: 843 us -> 640 us (0.76)
  Pallas kernels: 49.5 us -> 140 us
  matrix products: 77 us -> 0 us
  waiting for transfers between devices: 275 us -> 217 us
  other arithmetic: 91.5 us -> 34.1 us
  starting transfers between devices: 181 us -> 140 us
  blocking collectives: 48.6 us -> 12.5 us
  local copies, waits for them, and re-layouts: 91.3 us -> 70.5 us
    pallas_call x6 -> x36, Pallas kernels: 49.5 us -> 140 us  [call(): pl.pallas_call(kernel, grid=grid, out_shape=out_shape, scratch_shapes=lis...]
    dot_general x60 -> x0, matrix products: 77 us -> none  [dot(): lax.dot_general(lhs, rhs, (dims, ((), ())), preferred_element_type=F32)]
    ppermute x17 -> x13, waiting for transfers between devices: 103 us -> 48.4 us  [partner(): lax.ppermute(value, 'tensor', [(t, t ^ self.group) for t in range(self.te...]
    psum x1 -> x0, blocking collectives: 40.4 us -> none  [on_device(): gain_grad = lax.psum(gain_parts, ('dp', 'tensor'))]
    all_to_all x6 -> x3, starting transfers between devices: 26.7 us -> 9.88 us  [the longest x2 6.23 us: to_owners(): lax.all_to_all(rows.reshape(owners, capacity, -1), ('dp', 'tensor'), spli...]
    ppermute x0 -> x1, waiting for transfers between devices: none -> 15.4 us  [sum_weights_now(): received = lax.ppermute(sent, 'dp', [(d, d ^ 2) for d in range(4)])]
    ppermute x99 -> x90, waiting for transfers between devices: 141 us -> 126 us  [mate(): lax.ppermute(value, 'tensor', [(t, t ^ offset) for t in range(self.tensor...]
    another operation x16 -> x0, other arithmetic: 14.5 us -> none  [the longest x11 13.4 us: sum_weight(): jnp.stack([own.astype(BF16), other.astype(BF16)])]
  transfers between devices with their start and end apart: 147 -> 129, of which waited for: 67 -> 61; matrix products, arithmetic and copies ran while one was open for 27% -> 12% of each run, Pallas kernels for 6% -> 20%
where the time goes in v2:
time: 640 us; the launch traced here: 630 us
  waiting for transfers between devices  217 us (34%)
  starting transfers between devices  140 us (22%)
  Pallas kernels  140 us (22%)
  local copies, waits for them, and re-layouts  70.5 us (11%)
  other arithmetic  34.1 us (5%)
  between operations  16.4 us (3%)
  blocking collectives  12.5 us (2%)
    pallas_call x36, Pallas kernels, call(): pl.pallas_call(kernel, grid=grid, out_shape=out_shape, scratch_shapes=lis...  140 us
    ppermute x90, waiting for transfers between devices, mate(): lax.ppermute(value, 'tensor', [(t, t ^ offset) for t in range(self.tensor...  126 us
    ppermute x90, starting transfers between devices, mate(): lax.ppermute(value, 'tensor', [(t, t ^ offset) for t in range(self.tensor...  95.3 us
    ppermute x13, waiting for transfers between devices, partner(): lax.ppermute(value, 'tensor', [(t, t ^ self.group) for t in range(self.te...  48.4 us
    unnamed x277, local copies, waits for them, and re-layouts  29.6 us
    ppermute x13, starting transfers between devices, partner(): lax.ppermute(value, 'tensor', [(t, t ^ self.group) for t in range(self.te...  26.5 us
    all_to_all x2, waiting for transfers between devices, to_owners(): lax.all_to_all(rows.reshape(owners, capacity, -1), ('dp', 'tensor'), spli...  26.3 us
    ppermute x1, waiting for transfers between devices, sum_weights_now(): received = lax.ppermute(sent, 'dp', [(d, d ^ 2) for d in range(4)])  15.4 us
  transfers between devices with their start and end apart: 129, of which 61 were waited for; matrix products, arithmetic and copies ran while one was open for 12% of the time, Pallas kernels for 20%

profile of v2, /device:TPU:0, one launch (start us, length us, event | category | flops | bytes accessed | tf_op | source)
XLA Modules:
  0.0 629.8 jit_solution(1671119315969626602)
XLA Ops:
  9.6 5.4 collective-permute-start.1
  16.8 12.5 %all_to_all.22 = s32[32,1,12]{2,1,0:T(1,128)S(1)} all-to-all(s32[32,1,12]{2,1,0:T(1,128)S(1)} %bitcast.129), channel_id=1, replica_groups=mesh['dp'=4,'tensor'=8] {'dp','tensor'}, dimensions={0} | all-to-all | bytes 3072 | tf_op jit(solution)/shard_map/all_to_all | solution.py:753
  31.9 7.2 %gather_fusion = bf16[384,1024]{1,0:T(8,128)(2,1)S(1)} fusion(bf16[4096,1024]{1,0:T(8,128)(2,1)} %param.26, s32[1024]{0:T(1024)S(1)} %pad_clamp_fusion.3), kind=kCustom, calls=%fused_computation.4 | custom fusion | bytes 1574400 | tf_op jit(solution)/shard_map/jit(_take)/gather | solution.py:757
  41.3 2.8 all-to-all-start.1
  46.9 2.7 collective-permute-start.2
  49.6 26.3 %all-to-all-done.1 = bf16[32,12,1024]{2,1,0:T(8,128)(2,1)S(1)} async-done(((bf16[32,12,1024]{2,1,0:T(8,128)(2,1)}), bf16[32,12,1024]{2,1,0:T(8,128)(2,1)S(1)}, u32[]{:S(2)}, u32[]{:S(2)}) %all-to-all-start.1) | async-done | bytes 786464 | tf_op jit(solution)/shard_map/all_to_all | solution.py:687
  76.1 2.7 collective-permute-done.2
  84.9 2.4 collective-permute-done.3.refs_2_
  94.1 2.4 project.4
  96.7 3.3 collective-permute-done.14
  106.4 2.9 collective-permute-start.11
  111.9 8.9 %attend.3 = (bf16[512,256]{1,0:T(8,128)(2,1)S(1)}, f32[8,512]{1,0:T(8,128)S(1)}, bf16[128,1024]{1,0:T(8,128)(2,1)S(1)}, bf16[128,1024]{1,0:T(8,128)(2,1)S(1)}, b...) custom-call(bf16[512,256]{1,0:T(8,128)(2,1)S(1)} %get-tuple-element.303.q_ref, ...), custom_call_target="tpu_custom_call" | custom-call | flops 536870912 | bytes 4515840 | tf_op jit(solution)/shard_map/attend/pallas_call | solution.py:36
  123.6 3.6 collective-permute-done.11.refs_3_
  129.7 2.3 project.5
  132.1 11.7 %collective-permute-done.15 = bf16[128,1024]{1,0:T(8,128)(2,1)} collective-permute-done((bf16[128,1024]{1,0:T(8,128)(2,1)}, bf16[128,1024]{1,0:T(8,128)(2,1)}, u32[]{:S(2)}, u32[]{:S(2)}) %collective-permute-start.15) | collective-permute-done | bytes 262176 | tf_op jit(solution)/shard_map/ppermute | solution.py:596
  147.7 2.7 collective-permute-start.19
  151.1 3.5 collective-permute-start.36
  154.6 9.0 %attend.4 = (bf16[512,256]{1,0:T(8,128)(2,1)S(1)}, f32[8,512]{1,0:T(8,128)S(1)}, bf16[128,1024]{1,0:T(8,128)(2,1)S(1)}, bf16[128,1024]{1,0:T(8,128)(2,1)S(1)}, b...) custom-call(bf16[512,256]{1,0:T(8,128)(2,1)S(1)} %get-tuple-element.323.q_ref, ...), custom_call_target="tpu_custom_call" | custom-call | flops 536870912 | bytes 4515840 | tf_op jit(solution)/shard_map/attend/pallas_call | solution.py:36
  164.9 4.2 collective-permute-done.19.refs_3_
  182.5 10.8 %collective-permute-done.28.refs_6_ = bf16[64,1024]{1,0:T(8,128)(2,1)S(1)} collective-permute-done((bf16[64,1024]{1,0:T(8,128)(2,1)S(1)}, bf16[64,1024]{1,0:T(8,128)(2,1)S(1)}, u32[]{:S(2)}, u32[]{:S(2)}) %collective-permute-start.28) | collective-permute-done | bytes 131104 | tf_op jit(solution)/shard_map/ppermute | solution.py:599
  197.2 5.1 ffn.2
  211.2 2.4 collective-permute-start.47
  214.7 6.9 %collective-permute-done.34.refs_2_ = bf16[128,1024]{1,0:T(8,128)(2,1)S(1)} collective-permute-done((bf16[128,1024]{1,0:T(8,128)(2,1)S(1)}, bf16[128,1024]{1,0:T(8,128)(2,1)S(1)}, u32[]{:S(2)}, u32[]{:S(2)}) %collective-permute-start.34) | collective-permute-done | bytes 262176 | tf_op jit(solution)/shard_map/ppermute | solution.py:599
  221.5 2.5 collective-permute-done.35.refs_3_
  242.2 3.1 collective-permute-start.48
  245.4 9.1 %attend.5 = (bf16[512,256]{1,0:T(8,128)(2,1)S(1)}, f32[8,512]{1,0:T(8,128)S(1)}, bf16[128,1024]{1,0:T(8,128)(2,1)S(1)}, bf16[128,1024]{1,0:T(8,128)(2,1)S(1)}, b...) custom-call(bf16[512,256]{1,0:T(8,128)(2,1)S(1)} %project.6.q_ref, bf16[512,512]{1,0:T(8,128)(2,1)S(1)} %project.7.mine_ref, ...), custom_call_target="tpu_custom_call" | custom-call | flops 536870912 | bytes 4515840 | tf_op jit(solution)/shard_map/attend/pallas_call | solution.py:36
  261.7 4.8 collective-permute-done.44.refs_1_
  266.5 2.7 collective-permute-done.45.refs_2_
  269.2 4.1 collective-permute-done.46.refs_3_
  286.7 5.9 ffn.3
  298.7 4.5 collective-permute-done.55.refs_1_
  303.2 3.2 collective-permute-done.57.refs_3_
  315.3 2.7 collective-permute-done.62.refs_6_.refs_14_
  319.3 5.1 ffn_back.2
  328.0 6.1 ffn_grads.2
  345.2 3.7 collective-permute-done.70.refs_4_.refs_8_
  349.0 2.8 collective-permute-done.72.refs_6_.refs_10_
  351.8 11.6 %attend_back.3 = (bf16[512,256]{1,0:T(8,128)(2,1)S(1)}, f32[512,512]{1,0:T(8,128)S(1)}, bf16[512,512]{1,0:T(8,128)(2,1)S(1)}) custom-call(bf16[128,1024]{1,0:T(8,128)(2,1)} %wo_ref.9, bf16[4,192,1024]{2,1,0:T(8,128)(2,1)} %bitcast.141, bf16[512,256]{1,0:T(8,128)(2,1)} %copy-done.46, bf16[512,512]{1,0:T(8,128)(2,1)} %copy-done.37, ...), custom_call_target="tpu_custom_call" | custom-call | flops 1342177280 | bytes 6088704 | tf_op jit(solution)/shard_map/attend_back/pallas_call | solution.py:36
  373.4 4.2 attend_grads.3
  380.4 4.5 collective-permute-done.77.refs_3_
  397.7 2.6 collective-permute-done.83.refs_7_.refs_15_
  403.8 5.1 ffn_back.3
  412.5 6.1 ffn_grads.3
  420.1 2.3 collective-permute-done.86.refs_3_
  432.3 7.6 %collective-permute-done.96.refs_5_.refs_9_ = bf16[64,1024]{1,0:T(8,128)(2,1)S(1)} collective-permute-done((bf16[64,1024]{1,0:T(8,128)(2,1)S(1)}, bf16[64,1024]{1,0:T(8,128)(2,1)S(1)}, u32[]{:S(2)}, u32[]{:S(2)}) %collective-permute-start.96) | collective-permute-done | bytes 131104 | tf_op jit(solution)/shard_map/ppermute | solution.py:599
  444.9 3.7 collective-permute-done.99
  449.3 12.2 %attend_back.4 = (bf16[512,256]{1,0:T(8,128)(2,1)S(1)}, f32[512,512]{1,0:T(8,128)S(1)}, bf16[512,512]{1,0:T(8,128)(2,1)}) custom-call(bf16[128,1024]{1,0:T(8,128)(2,1)} %wo_ref.10, bf16[4,192,1024]{2,1,0:T(8,128)(2,1)} %bitcast.142, bf16[512,256]{1,0:T(8,128)(2,1)} %copy-done.103, bf16[512,512]{1,0:T(8,128)(2,1)} %copy-done.99, ...), custom_call_target="tpu_custom_call" | custom-call | flops 1342177280 | bytes 6088704 | tf_op jit(solution)/shard_map/attend_back/pallas_call | solution.py:36
  462.8 2.5 collective-permute-start.92
  467.5 2.6 gather_fusion.1
  470.1 2.5 unproject_keys.4
  474.9 4.0 attend_grads.4
  478.9 4.1 collective-permute-done.92.refs_3_.refs_11_
  483.0 12.7 %attend_back.5 = (bf16[512,256]{1,0:T(8,128)(2,1)S(1)}, f32[512,512]{1,0:T(8,128)S(1)}, bf16[512,512]{1,0:T(8,128)(2,1)}) custom-call(bf16[128,1024]{1,0:T(8,128)(2,1)} %wo_ref.11, bf16[4,192,1024]{2,1,0:T(8,128)(2,1)} %bitcast.143, bf16[512,256]{1,0:T(8,128)(2,1)} %copy-done.102, bf16[512,512]{1,0:T(8,128)(2,1)} %copy-done.96, bf16[512,512]{1,0:T(8,128)(2,1)} %copy-done.98, ...), custom_call_target="tpu_custom_call" | custom-call | flops 1342177280 | bytes 6088704 | tf_op jit(solution)/shard_map/attend_back/pallas_call | solution.py:36
  505.4 3.2 unproject_keys.5
  508.6 14.8 %collective-permute-done.103 = bf16[2,512,256]{2,1,0:T(8,128)(2,1)S(1)} collective-permute-done((bf16[2,512,256]{2,1,0:T(8,128)(2,1)S(1)}, bf16[2,512,256]{2,1,0:T(8,128)(2,1)S(1)}, u32[]{:S(2)}, u32[]{:S(2)}) %collective-permute-start.103) | collective-permute-done | bytes 524320 | tf_op jit(solution)/shard_map/ppermute | solution.py:596
  534.2 4.6 collective-permute-done.106.refs_3_
  541.7 2.9 attend_grads.5
  551.6 3.4 all-to-all-start.2
  565.2 15.4 %collective-permute-done.111 = bf16[2,4,128,256]{3,2,1,0:T(8,128)(2,1)} collective-permute-done((bf16[2,4,128,256]{3,2,1,0:T(8,128)(2,1)}, bf16[2,4,128,256]{3,2,1,0:T(8,128)(2,1)}, u32[]{:S(2)}, u32[]{:S(2)}) %collective-permute-start.111) | collective-permute-done | bytes 524320 | tf_op jit(solution)/shard_map/ppermute | solution.py:651
  582.6 3.1 collective-permute-start.112
  588.3 3.7 all-to-all-start.3
  592.0 11.9 %scatter_custom_fusion = f32[4096,1024]{1,0:T(8,128)} fusion(s32[384]{0:T(512)} %get-tuple-element.680, f32[]{:T(128)} %constant.151.clone.1, f32[384,1024]{1,0:T(8,128)} %reshape.598, f32[384]{0:T(512)S(1)} %broadcast_maximum_fusion), kind=kCustom, calls=%fused_computation.7 | custom fusion | flops 786432 | bytes 18352128 | tf_op jit(solution)/shard_map/scatter-add | solution.py:930
  605.9 2.9 collective-permute-start.113
  611.0 10.0 %collective-permute-done.113 = bf16[4,128,256]{2,1,0:T(8,128)(2,1)S(1)} collective-permute-done((bf16[4,128,256]{2,1,0:T(8,128)(2,1)S(1)}, bf16[4,128,256]{2,1,0:T(8,128)(2,1)S(1)}, u32[]{:S(2)}, u32[]{:S(2)}) %collective-permute-start.113) | collective-permute-done | bytes 262176 | tf_op jit(solution)/shard_map/ppermute | solution.py:596
  (626 shorter events, 247.4 us)
Async XLA Ops:
  7.2 86.9 %all-gather.21.cloned.1.call-start = ((), (), s32[]{:S(2)}) async-start(), calls=%async_computation.16 | async-start | bytes 1966080 | tf_op jit(solution)/shard_map/all_gather | solution.py:625
  7.9 22.8 %collective-permute-start = (s32[2304]{0:T(1024)S(1)}, s32[2304]{0:T(1024)S(1)}, u32[]{:S(2)}, u32[]{:S(2)}) collective-permute-start(s32[2304]{0:T(1024)S(1)} %pad_add_fusion), channel_id=1, source_target_pairs={{0,0},{1,1},{2,2},{3,3},{4,8},{5,9},{6,10},{7,11},{8,4},{9,5},{10,... | collective-permute-start | bytes 27656 | tf_op jit(solution)/shard_map/ppermute | solution.py:590
  9.6 21.1 %collective-permute-start.1 = (bf16[3,256,128]{2,1,0:T(8,128)(2,1)S(1)}, bf16[3,256,128]{2,1,0:T(8,128)(2,1)S(1)}, u32[]{:S(2)}, u32[]{:S(2)}) collective-permute-start(bf16[3,256,128]{2,1,0:T(8,128)(2,1)S(1)} %constant_dynamic-slice_fusion.9), channel_id=1, source_target_pairs={{0,4},{1,5},{2,6},{3,7},{4,0},{5,1},{6,2},{7,3},{8,12},{9,13},{10,... | collective-permute-start | bytes 589832 | tf_op jit(solution)/shard_map/ppermute | solution.py:596
  41.3 34.6 %all-to-all-start.1 = ((bf16[32,12,1024]{2,1,0:T(8,128)(2,1)}), bf16[32,12,1024]{2,1,0:T(8,128)(2,1)S(1)}, u32[]{:S(2)}, u32[]{:S(2)}) async-start(bf16[32,12,1024]{2,1,0:T(8,128)(2,1)} %broadcast_select_fusion), calls=%async_computation.1 | async-start | bytes 2097152 | tf_op jit(solution)/shard_map/all_to_all | solution.py:687
  44.1 66.6 %all-gather.23.cloned.1.call-start = ((), (), s32[]{:S(2)}) async-start(), calls=%async_computation.17 | async-start | bytes 1966080 | tf_op jit(solution)/shard_map/all_gather | solution.py:625
  46.9 31.9 %collective-permute-start.2 = (bf16[96,1024]{1,0:T(8,128)(2,1)S(1)}, bf16[96,1024]{1,0:T(8,128)(2,1)S(1)}, u32[]{:S(2)}, u32[]{:S(2)}) collective-permute-start(bf16[96,1024]{1,0:T(8,128)(2,1)S(1)} %pad_maximum_fusion.5), channel_id=1, source_target_pairs={{0,4},{1,5},{2,6},{3,7},{4,0},{5,1},{6,2},{7,3},{8,12},{9,13},{10,... | collective-permute-start | bytes 589832 | tf_op jit(solution)/shard_map/ppermute | solution.py:596
  80.7 48.9 %all-gather.25.cloned.1.call-start = ((), (), s32[]{:S(2)}) async-start(), calls=%async_computation.18 | async-start | bytes 1966080 | tf_op jit(solution)/shard_map/all_gather | solution.py:625
  101.8 95.4 %all-gather.13.cloned.1.call-start = ((), (), s32[]{:S(2)}) async-start(), calls=%async_computation.8 | async-start | bytes 1310720 | tf_op jit(solution)/shard_map/all_gather | solution.py:628
  106.3 17.3 %collective-permute-start.10 = (bf16[128,1024]{1,0:T(8,128)(2,1)S(1)}, bf16[128,1024]{1,0:T(8,128)(2,1)S(1)}, u32[]{:S(2)}, u32[]{:S(2)}) collective-permute-start(bf16[128,1024]{1,0:T(8,128)(2,1)S(1)} %get-tuple-element.315.refs_0_), channel_id=1, source_target_pairs={{0,2},{1,3},{2,0},{3,1},{4,6},{5,7},{6,4},{7,5},{8,10},{9,11},{10,... | collective-permute-start | bytes 786440 | tf_op jit(solution)/shard_map/ppermute | solution.py:599
  106.4 20.8 %collective-permute-start.11 = (bf16[128,1024]{1,0:T(8,128)(2,1)S(1)}, bf16[128,1024]{1,0:T(8,128)(2,1)S(1)}, u32[]{:S(2)}, u32[]{:S(2)}) collective-permute-start(bf16[128,1024]{1,0:T(8,128)(2,1)S(1)} %get-tuple-element.315.refs_0_), channel_id=1, source_target_pairs={{0,3},{1,2},{2,1},{3,0},{4,7},{5,6},{6,5},{7,4},{8,11},{9,10},{10,... | collective-permute-start | bytes 786440 | tf_op jit(solution)/shard_map/ppermute | solution.py:599
  109.3 17.9 %collective-permute-start.9 = (bf16[128,1024]{1,0:T(8,128)(2,1)S(1)}, bf16[128,1024]{1,0:T(8,128)(2,1)S(1)}, u32[]{:S(2)}, u32[]{:S(2)}) collective-permute-start(bf16[128,1024]{1,0:T(8,128)(2,1)S(1)} %get-tuple-element.315.refs_0_), channel_id=1, source_target_pairs={{0,1},{1,0},{2,3},{3,2},{4,5},{5,4},{6,7},{7,6},{8,9},{9,8},{10,11... | collective-permute-start | bytes 786440 | tf_op jit(solution)/shard_map/ppermute | solution.py:599
  109.9 17.3 %collective-permute-start.13 = (bf16[256,512]{1,0:T(8,128)(2,1)}, bf16[256,512]{1,0:T(8,128)(2,1)}, u32[]{:S(2)}, u32[]{:S(2)}) collective-permute-start(bf16[256,512]{1,0:T(8,128)(2,1)} %constant_dynamic-slice_fusion.5), channel_id=1, source_target_pairs={{0,4},{1,5},{2,6},{3,7},{4,0},{5,1},{6,2},{7,3},{8,12},{9,13},{10,... | collective-permute-start | bytes 786440 | tf_op jit(solution)/shard_map/ppermute | solution.py:596
  127.3 70.0 %all-gather.15.cloned.1.call-start = ((), (), s32[]{:S(2)}) async-start(), calls=%async_computation.9 | async-start | bytes 1310720 | tf_op jit(solution)/shard_map/all_gather | solution.py:628
  129.2 14.6 %collective-permute-start.15 = (bf16[128,1024]{1,0:T(8,128)(2,1)}, bf16[128,1024]{1,0:T(8,128)(2,1)}, u32[]{:S(2)}, u32[]{:S(2)}) collective-permute-start(bf16[128,1024]{1,0:T(8,128)(2,1)} %constant_dynamic-slice_fusion.3), channel_id=1, source_target_pairs={{0,4},{1,5},{2,6},{3,7},{4,0},{5,1},{6,2},{7,3},{8,12},{9,13},{10,... | collective-permute-start | bytes 786440 | tf_op jit(solution)/shard_map/ppermute | solution.py:596
  143.8 91.6 %all-gather.27.cloned.1.call-start = ((), (), s32[]{:S(2)}) async-start(), calls=%async_computation.19 | async-start | bytes 1966080 | tf_op jit(solution)/shard_map/all_gather | solution.py:625
  146.8 18.1 %collective-permute-start.17 = (bf16[128,1024]{1,0:T(8,128)(2,1)}, bf16[128,1024]{1,0:T(8,128)(2,1)S(1)}, u32[]{:S(2)}, u32[]{:S(2)}) collective-permute-start(bf16[128,1024]{1,0:T(8,128)(2,1)} %copy-done.109), channel_id=1, source_target_pairs={{0,1},{1,0},{2,3},{3,2},{4,5},{5,4},{6,7},{7,6},{8,9},{9,8},{10,11... | collective-permute-start | bytes 786440 | tf_op jit(solution)/shard_map/ppermute | solution.py:599
  147.7 17.2 %collective-permute-start.18 = (bf16[128,1024]{1,0:T(8,128)(2,1)}, bf16[128,1024]{1,0:T(8,128)(2,1)S(1)}, u32[]{:S(2)}, u32[]{:S(2)}) collective-permute-start(bf16[128,1024]{1,0:T(8,128)(2,1)} %copy-done.108), channel_id=1, source_target_pairs={{0,2},{1,3},{2,0},{3,1},{4,6},{5,7},{6,4},{7,5},{8,10},{9,11},{10,... | collective-permute-start | bytes 786440 | tf_op jit(solution)/shard_map/ppermute | solution.py:599
  147.7 21.4 %collective-permute-start.19 = (bf16[128,1024]{1,0:T(8,128)(2,1)}, bf16[128,1024]{1,0:T(8,128)(2,1)S(1)}, u32[]{:S(2)}, u32[]{:S(2)}) collective-permute-start(bf16[128,1024]{1,0:T(8,128)(2,1)} %copy-done.107), channel_id=1, source_target_pairs={{0,3},{1,2},{2,1},{3,0},{4,7},{5,6},{6,5},{7,4},{8,11},{9,10},{10,... | collective-permute-start | bytes 786440 | tf_op jit(solution)/shard_map/ppermute | solution.py:599
  150.4 18.7 %collective-permute-start.20 = (bf16[128,1024]{1,0:T(8,128)(2,1)S(1)}, bf16[128,1024]{1,0:T(8,128)(2,1)S(1)}, u32[]{:S(2)}, u32[]{:S(2)}) collective-permute-start(bf16[128,1024]{1,0:T(8,128)(2,1)S(1)} %bitcast.126), channel_id=1, source_target_pairs={{0,0},{1,1},{2,2},{3,3},{4,8},{5,9},{6,10},{7,11},{8,4},{9,5},{10,... | collective-permute-start | bytes 786440 | tf_op jit(solution)/shard_map/ppermute | solution.py:590
  151.1 19.1 %collective-permute-start.36 = (bf16[3,256,128]{2,1,0:T(8,128)(2,1)S(1)}, bf16[3,256,128]{2,1,0:T(8,128)(2,1)S(1)}, u32[]{:S(2)}, u32[]{:S(2)}) collective-permute-start(bf16[3,256,128]{2,1,0:T(8,128)(2,1)S(1)} %pad_maximum_fusion.6), channel_id=1, source_target_pairs={{0,4},{1,5},{2,6},{3,7},{4,0},{5,1},{6,2},{7,3},{8,12},{9,13},{10,... | collective-permute-start | bytes 589832 | tf_op jit(solution)/shard_map/ppermute | solution.py:596
  171.1 110.9 %all-gather.17.cloned.1.call-start = ((), (), s32[]{:S(2)}) async-start(), calls=%async_computation.10 | async-start | bytes 1310720 | tf_op jit(solution)/shard_map/all_gather | solution.py:628
  175.3 18.0 %collective-permute-start.21 = (bf16[128,1024]{1,0:T(8,128)(2,1)}, bf16[128,1024]{1,0:T(8,128)(2,1)S(1)}, u32[]{:S(2)}, u32[]{:S(2)}) collective-permute-start(bf16[128,1024]{1,0:T(8,128)(2,1)} %copy-done.112), channel_id=1, source_target_pairs={{0,1},{1,0},{2,3},{3,2},{4,5},{5,4},{6,7},{7,6},{8,9},{9,8},{10,11... | collective-permute-start | bytes 786440 | tf_op jit(solution)/shard_map/ppermute | solution.py:599
  177.6 15.7 %collective-permute-start.22 = (bf16[128,1024]{1,0:T(8,128)(2,1)}, bf16[128,1024]{1,0:T(8,128)(2,1)S(1)}, u32[]{:S(2)}, u32[]{:S(2)}) collective-permute-start(bf16[128,1024]{1,0:T(8,128)(2,1)} %copy-done.111), channel_id=1, source_target_pairs={{0,2},{1,3},{2,0},{3,1},{4,6},{5,7},{6,4},{7,5},{8,10},{9,11},{10,... | collective-permute-start | bytes 786440 | tf_op jit(solution)/shard_map/ppermute | solution.py:599
  178.3 15.0 %collective-permute-start.23 = (bf16[128,1024]{1,0:T(8,128)(2,1)}, bf16[128,1024]{1,0:T(8,128)(2,1)S(1)}, u32[]{:S(2)}, u32[]{:S(2)}) collective-permute-start(bf16[128,1024]{1,0:T(8,128)(2,1)} %copy-done.110), channel_id=1, source_target_pairs={{0,3},{1,2},{2,1},{3,0},{4,7},{5,6},{6,5},{7,4},{8,11},{9,10},{10,... | collective-permute-start | bytes 786440 | tf_op jit(solution)/shard_map/ppermute | solution.py:599
  180.5 12.8 %collective-permute-start.28 = (bf16[64,1024]{1,0:T(8,128)(2,1)S(1)}, bf16[64,1024]{1,0:T(8,128)(2,1)S(1)}, u32[]{:S(2)}, u32[]{:S(2)}) collective-permute-start(bf16[64,1024]{1,0:T(8,128)(2,1)S(1)} %collective-permute-done.24.refs_2_), channel_id=1, source_target_pairs={{0,2},{1,3},{2,0},{3,1},{4,6},{5,7},{6,4},{7,5},{8,10},{9,11},{10,... | collective-permute-start | bytes 393224 | tf_op jit(solution)/shard_map/ppermute | solution.py:599
  181.1 12.2 %collective-permute-start.29 = (bf16[64,1024]{1,0:T(8,128)(2,1)S(1)}, bf16[64,1024]{1,0:T(8,128)(2,1)S(1)}, u32[]{:S(2)}, u32[]{:S(2)}) collective-permute-start(bf16[64,1024]{1,0:T(8,128)(2,1)S(1)} %collective-permute-done.27.refs_5_), channel_id=1, source_target_pairs={{0,1},{1,0},{2,3},{3,2},{4,5},{5,4},{6,7},{7,6},{8,9},{9,8},{10,11... | collective-permute-start | bytes 393224 | tf_op jit(solution)/shard_map/ppermute | solution.py:599
  193.7 11.1 %collective-permute-start.30 = (bf16[128,1024]{1,0:T(8,128)(2,1)S(1)}, bf16[128,1024]{1,0:T(8,128)(2,1)S(1)}, u32[]{:S(2)}, u32[]{:S(2)}) collective-permute-start(bf16[128,1024]{1,0:T(8,128)(2,1)S(1)} %get-tuple-element.368.refs_0_), channel_id=1, source_target_pairs={{0,1},{1,0},{2,3},{3,2},{4,5},{5,4},{6,7},{7,6},{8,9},{9,8},{10,11... | collective-permute-start | bytes 786440 | tf_op jit(solution)/shard_map/ppermute | solution.py:599
  195.6 11.2 %collective-permute-start.32 = (bf16[128,1024]{1,0:T(8,128)(2,1)S(1)}, bf16[128,1024]{1,0:T(8,128)(2,1)S(1)}, u32[]{:S(2)}, u32[]{:S(2)}) collective-permute-start(bf16[128,1024]{1,0:T(8,128)(2,1)S(1)} %get-tuple-element.368.refs_0_), channel_id=1, source_target_pairs={{0,3},{1,2},{2,1},{3,0},{4,7},{5,6},{6,5},{7,4},{8,11},{9,10},{10,... | collective-permute-start | bytes 786440 | tf_op jit(solution)/shard_map/ppermute | solution.py:599
  208.4 13.1 %collective-permute-start.34 = (bf16[128,1024]{1,0:T(8,128)(2,1)S(1)}, bf16[128,1024]{1,0:T(8,128)(2,1)S(1)}, u32[]{:S(2)}, u32[]{:S(2)}) collective-permute-start(bf16[128,1024]{1,0:T(8,128)(2,1)S(1)} %get-tuple-element.364), channel_id=1, source_target_pairs={{0,2},{1,3},{2,0},{3,1},{4,6},{5,7},{6,4},{7,5},{8,10},{9,11},{10,... | collective-permute-start | bytes 786440 | tf_op jit(solution)/shard_map/ppermute | solution.py:599
  209.3 14.7 %collective-permute-start.35 = (bf16[128,1024]{1,0:T(8,128)(2,1)S(1)}, bf16[128,1024]{1,0:T(8,128)(2,1)S(1)}, u32[]{:S(2)}, u32[]{:S(2)}) collective-permute-start(bf16[128,1024]{1,0:T(8,128)(2,1)S(1)} %get-tuple-element.365), channel_id=1, source_target_pairs={{0,3},{1,2},{2,1},{3,0},{4,7},{5,6},{6,5},{7,4},{8,11},{9,10},{10,... | collective-permute-start | bytes 786440 | tf_op jit(solution)/shard_map/ppermute | solution.py:599
  211.2 14.0 %collective-permute-start.47 = (bf16[256,512]{1,0:T(8,128)(2,1)S(1)}, bf16[256,512]{1,0:T(8,128)(2,1)S(1)}, u32[]{:S(2)}, u32[]{:S(2)}) collective-permute-start(bf16[256,512]{1,0:T(8,128)(2,1)S(1)} %constant_dynamic-slice_fusion.1), channel_id=1, source_target_pairs={{0,4},{1,5},{2,6},{3,7},{4,0},{5,1},{6,2},{7,3},{8,12},{9,13},{10,... | collective-permute-start | bytes 786440 | tf_op jit(solution)/shard_map/ppermute | solution.py:596
  225.9 60.8 %all-gather.19.cloned.1.call-start = ((), (), s32[]{:S(2)}) async-start(), calls=%async_computation.11 | async-start | bytes 1310720 | tf_op jit(solution)/shard_map/all_gather | solution.py:628
  242.2 15.1 %collective-permute-start.48 = (bf16[128,1024]{1,0:T(8,128)(2,1)S(1)}, bf16[128,1024]{1,0:T(8,128)(2,1)S(1)}, u32[]{:S(2)}, u32[]{:S(2)}) collective-permute-start(bf16[128,1024]{1,0:T(8,128)(2,1)S(1)} %constant_dynamic-slice_fusion), channel_id=1, source_target_pairs={{0,4},{1,5},{2,6},{3,7},{4,0},{5,1},{6,2},{7,3},{8,12},{9,13},{10,... | collective-permute-start | bytes 786440 | tf_op jit(solution)/shard_map/ppermute | solution.py:596
  258.1 166.5 %reduce-scatter.5.cloned.1.call-start = ((), (), s32[]{:S(2)}) async-start(), calls=%async_computation.12 | async-start | bytes 5242880 | tf_op jit(solution)/shard_map/reduce_scatter | solution.py:632
  260.0 13.3 %collective-permute-start.46 = (bf16[128,1024]{1,0:T(8,128)(2,1)S(1)}, bf16[128,1024]{1,0:T(8,128)(2,1)S(1)}, u32[]{:S(2)}, u32[]{:S(2)}) collective-permute-start(bf16[128,1024]{1,0:T(8,128)(2,1)S(1)} %get-tuple-element.385), channel_id=1, source_target_pairs={{0,3},{1,2},{2,1},{3,0},{4,7},{5,6},{6,5},{7,4},{8,11},{9,10},{10,... | collective-permute-start | bytes 786440 | tf_op jit(solution)/shard_map/ppermute | solution.py:599
  336.7 128.6 %reduce-scatter.7.cloned.1.call-start = ((), (), s32[]{:S(2)}) async-start(), calls=%async_computation.13 | async-start | bytes 2621440 | tf_op jit(solution)/shard_map/reduce_scatter | solution.py:632
  372.0 13.0 %collective-permute-start.77 = (bf16[128,1024]{1,0:T(8,128)(2,1)S(1)}, bf16[128,1024]{1,0:T(8,128)(2,1)S(1)}, u32[]{:S(2)}, u32[]{:S(2)}) collective-permute-start(bf16[128,1024]{1,0:T(8,128)(2,1)S(1)} %get-tuple-element.445), channel_id=1, source_target_pairs={{0,3},{1,2},{2,1},{3,0},{4,7},{5,6},{6,5},{7,4},{8,11},{9,10},{10,... | collective-permute-start | bytes 786440 | tf_op jit(solution)/shard_map/ppermute | solution.py:599
  386.5 109.4 %reduce-scatter.9.cloned.1.call-start = ((), (), s32[]{:S(2)}) async-start(), calls=%async_computation.14 | async-start | bytes 5242880 | tf_op jit(solution)/shard_map/reduce_scatter | solution.py:632
  400.3 11.2 %collective-permute-start.87 = (bf16[128,1024]{1,0:T(8,128)(2,1)S(1)}, bf16[128,1024]{1,0:T(8,128)(2,1)S(1)}, u32[]{:S(2)}, u32[]{:S(2)}) collective-permute-start(bf16[128,1024]{1,0:T(8,128)(2,1)S(1)} %get-tuple-element.467), channel_id=1, source_target_pairs={{0,1},{1,0},{2,3},{3,2},{4,5},{5,4},{6,7},{7,6},{8,9},{9,8},{10,11... | collective-permute-start | bytes 786440 | tf_op jit(solution)/shard_map/ppermute | solution.py:599
  400.7 17.8 %collective-permute-start.88 = (bf16[128,1024]{1,0:T(8,128)(2,1)}, bf16[128,1024]{1,0:T(8,128)(2,1)S(1)}, u32[]{:S(2)}, u32[]{:S(2)}) collective-permute-start(bf16[128,1024]{1,0:T(8,128)(2,1)} %get-tuple-element.468), channel_id=1, source_target_pairs={{0,2},{1,3},{2,0},{3,1},{4,6},{5,7},{6,4},{7,5},{8,10},{9,11},{10,... | collective-permute-start | bytes 786440 | tf_op jit(solution)/shard_map/ppermute | solution.py:599
  402.9 15.7 %collective-permute-start.89 = (bf16[128,1024]{1,0:T(8,128)(2,1)}, bf16[128,1024]{1,0:T(8,128)(2,1)S(1)}, u32[]{:S(2)}, u32[]{:S(2)}) collective-permute-start(bf16[128,1024]{1,0:T(8,128)(2,1)} %get-tuple-element.469), channel_id=1, source_target_pairs={{0,3},{1,2},{2,1},{3,0},{4,7},{5,6},{6,5},{7,4},{8,11},{9,10},{10,... | collective-permute-start | bytes 786440 | tf_op jit(solution)/shard_map/ppermute | solution.py:599
  408.9 11.2 %collective-permute-start.84 = (bf16[128,1024]{1,0:T(8,128)(2,1)S(1)}, bf16[128,1024]{1,0:T(8,128)(2,1)S(1)}, u32[]{:S(2)}, u32[]{:S(2)}) collective-permute-start(bf16[128,1024]{1,0:T(8,128)(2,1)S(1)} %get-tuple-element.463), channel_id=1, source_target_pairs={{0,1},{1,0},{2,3},{3,2},{4,5},{5,4},{6,7},{7,6},{8,9},{9,8},{10,11... | collective-permute-start | bytes 786440 | tf_op jit(solution)/shard_map/ppermute | solution.py:599
  409.5 10.7 %collective-permute-start.85 = (bf16[128,1024]{1,0:T(8,128)(2,1)S(1)}, bf16[128,1024]{1,0:T(8,128)(2,1)S(1)}, u32[]{:S(2)}, u32[]{:S(2)}) collective-permute-start(bf16[128,1024]{1,0:T(8,128)(2,1)S(1)} %get-tuple-element.464), channel_id=1, source_target_pairs={{0,2},{1,3},{2,0},{3,1},{4,6},{5,7},{6,4},{7,5},{8,10},{9,11},{10,... | collective-permute-start | bytes 786440 | tf_op jit(solution)/shard_map/ppermute | solution.py:599
  411.5 11.0 %collective-permute-start.86 = (bf16[128,1024]{1,0:T(8,128)(2,1)S(1)}, bf16[128,1024]{1,0:T(8,128)(2,1)S(1)}, u32[]{:S(2)}, u32[]{:S(2)}) collective-permute-start(bf16[128,1024]{1,0:T(8,128)(2,1)S(1)} %get-tuple-element.465), channel_id=1, source_target_pairs={{0,3},{1,2},{2,1},{3,0},{4,7},{5,6},{6,5},{7,4},{8,11},{9,10},{10,... | collective-permute-start | bytes 786440 | tf_op jit(solution)/shard_map/ppermute | solution.py:599
  424.1 180.7 %reduce-scatter.11.cloned.1.call-start = ((), (), s32[]{:S(2)}) async-start(), calls=%async_computation.15 | async-start | bytes 2621440 | tf_op jit(solution)/shard_map/reduce_scatter | solution.py:632
  426.7 21.9 %collective-permute-start.99 = (bf16[2,512,256]{2,1,0:T(8,128)(2,1)S(1)}, bf16[2,512,256]{2,1,0:T(8,128)(2,1)S(1)}, u32[]{:S(2)}, u32[]{:S(2)}) collective-permute-start(bf16[2,512,256]{2,1,0:T(8,128)(2,1)S(1)} %bitcast.124), channel_id=1, source_target_pairs={{0,4},{1,5},{2,6},{3,7},{4,0},{5,1},{6,2},{7,3},{8,12},{9,13},{10,... | collective-permute-start | bytes 1572872 | tf_op jit(solution)/shard_map/ppermute | solution.py:596
  427.9 12.0 %collective-permute-start.96 = (bf16[64,1024]{1,0:T(8,128)(2,1)S(1)}, bf16[64,1024]{1,0:T(8,128)(2,1)S(1)}, u32[]{:S(2)}, u32[]{:S(2)}) collective-permute-start(bf16[64,1024]{1,0:T(8,128)(2,1)S(1)} %copy-done.73), channel_id=1, source_target_pairs={{0,2},{1,3},{2,0},{3,1},{4,6},{5,7},{6,4},{7,5},{8,10},{9,11},{10,... | collective-permute-start | bytes 393224 | tf_op jit(solution)/shard_map/ppermute | solution.py:599
  429.2 12.1 %collective-permute-start.94 = (bf16[64,1024]{1,0:T(8,128)(2,1)S(1)}, bf16[64,1024]{1,0:T(8,128)(2,1)S(1)}, u32[]{:S(2)}, u32[]{:S(2)}) collective-permute-start(bf16[64,1024]{1,0:T(8,128)(2,1)S(1)} %copy-done.73), channel_id=1, source_target_pairs={{0,1},{1,0},{2,3},{3,2},{4,5},{5,4},{6,7},{7,6},{8,9},{9,8},{10,11... | collective-permute-start | bytes 393224 | tf_op jit(solution)/shard_map/ppermute | solution.py:599
  429.5 11.9 %collective-permute-start.95 = (bf16[64,1024]{1,0:T(8,128)(2,1)S(1)}, bf16[64,1024]{1,0:T(8,128)(2,1)S(1)}, u32[]{:S(2)}, u32[]{:S(2)}) collective-permute-start(bf16[64,1024]{1,0:T(8,128)(2,1)S(1)} %copy-done.70), channel_id=1, source_target_pairs={{0,2},{1,3},{2,0},{3,1},{4,6},{5,7},{6,4},{7,5},{8,10},{9,11},{10,... | collective-permute-start | bytes 393224 | tf_op jit(solution)/shard_map/ppermute | solution.py:599
  431.6 11.1 %collective-permute-start.97 = (bf16[64,1024]{1,0:T(8,128)(2,1)S(1)}, bf16[64,1024]{1,0:T(8,128)(2,1)S(1)}, u32[]{:S(2)}, u32[]{:S(2)}) collective-permute-start(bf16[64,1024]{1,0:T(8,128)(2,1)S(1)} %collective-permute-done.93.refs_2_.refs_6_), channel_id=1, source_target_pairs={{0,2},{1,3},{2,0},{3,1},{4,6},{5,7},{6,4},{7,5},{8,10},{9,11},{10,... | collective-permute-start | bytes 393224 | tf_op jit(solution)/shard_map/ppermute | solution.py:599
  461.7 17.1 %collective-permute-start.90 = (bf16[128,1024]{1,0:T(8,128)(2,1)S(1)}, bf16[128,1024]{1,0:T(8,128)(2,1)}, u32[]{:S(2)}, u32[]{:S(2)}) collective-permute-start(bf16[128,1024]{1,0:T(8,128)(2,1)S(1)} %get-tuple-element.563.refs_0_.refs_8_), channel_id=1, source_target_pairs={{0,1},{1,0},{2,3},{3,2},{4,5},{5,4},{6,7},{7,6},{8,9},{9,8},{10,11... | collective-permute-start | bytes 786440 | tf_op jit(solution)/shard_map/ppermute | solution.py:599
  462.8 16.1 %collective-permute-start.91 = (bf16[128,1024]{1,0:T(8,128)(2,1)S(1)}, bf16[128,1024]{1,0:T(8,128)(2,1)}, u32[]{:S(2)}, u32[]{:S(2)}) collective-permute-start(bf16[128,1024]{1,0:T(8,128)(2,1)S(1)} %get-tuple-element.563.refs_0_.refs_8_), channel_id=1, source_target_pairs={{0,2},{1,3},{2,0},{3,1},{4,6},{5,7},{6,4},{7,5},{8,10},{9,11},{10,... | collective-permute-start | bytes 786440 | tf_op jit(solution)/shard_map/ppermute | solution.py:599
  462.8 20.2 %collective-permute-start.92 = (bf16[128,1024]{1,0:T(8,128)(2,1)S(1)}, bf16[128,1024]{1,0:T(8,128)(2,1)}, u32[]{:S(2)}, u32[]{:S(2)}) collective-permute-start(bf16[128,1024]{1,0:T(8,128)(2,1)S(1)} %get-tuple-element.563.refs_0_.refs_8_), channel_id=1, source_target_pairs={{0,3},{1,2},{2,1},{3,0},{4,7},{5,6},{6,5},{7,4},{8,11},{9,10},{10,... | collective-permute-start | bytes 786440 | tf_op jit(solution)/shard_map/ppermute | solution.py:599
  467.1 15.9 %collective-permute-start.101 = (bf16[4,128,256]{2,1,0:T(8,128)(2,1)}, bf16[4,128,256]{2,1,0:T(8,128)(2,1)}, u32[]{:S(2)}, u32[]{:S(2)}) collective-permute-start(bf16[4,128,256]{2,1,0:T(8,128)(2,1)} %bitcast.27), channel_id=1, source_target_pairs={{0,4},{1,5},{2,6},{3,7},{4,0},{5,1},{6,2},{7,3},{8,12},{9,13},{10,... | collective-permute-start | bytes 786440 | tf_op jit(solution)/shard_map/ppermute | solution.py:596
  498.0 25.4 %collective-permute-start.103 = (bf16[2,512,256]{2,1,0:T(8,128)(2,1)S(1)}, bf16[2,512,256]{2,1,0:T(8,128)(2,1)S(1)}, u32[]{:S(2)}, u32[]{:S(2)}) collective-permute-start(bf16[2,512,256]{2,1,0:T(8,128)(2,1)S(1)} %bitcast.125), channel_id=1, source_target_pairs={{0,4},{1,5},{2,6},{3,7},{4,0},{5,1},{6,2},{7,3},{8,12},{9,13},{10,... | collective-permute-start | bytes 1572872 | tf_op jit(solution)/shard_map/ppermute | solution.py:596
  500.0 24.9 %collective-permute-start.107 = (bf16[128,1024]{1,0:T(8,128)(2,1)}, bf16[128,1024]{1,0:T(8,128)(2,1)S(1)}, u32[]{:S(2)}, u32[]{:S(2)}) collective-permute-start(bf16[128,1024]{1,0:T(8,128)(2,1)} %copy-done.106), channel_id=1, source_target_pairs={{0,1},{1,0},{2,3},{3,2},{4,5},{5,4},{6,7},{7,6},{8,9},{9,8},{10,11... | collective-permute-start | bytes 786440 | tf_op jit(solution)/shard_map/ppermute | solution.py:599
  501.2 29.0 %collective-permute-start.108 = (bf16[128,1024]{1,0:T(8,128)(2,1)}, bf16[128,1024]{1,0:T(8,128)(2,1)}, u32[]{:S(2)}, u32[]{:S(2)}) collective-permute-start(bf16[128,1024]{1,0:T(8,128)(2,1)} %copy-done.105), channel_id=1, source_target_pairs={{0,2},{1,3},{2,0},{3,1},{4,6},{5,7},{6,4},{7,5},{8,10},{9,11},{10,... | collective-permute-start | bytes 786440 | tf_op jit(solution)/shard_map/ppermute | solution.py:599
  501.5 28.7 %collective-permute-start.109 = (bf16[128,1024]{1,0:T(8,128)(2,1)}, bf16[128,1024]{1,0:T(8,128)(2,1)}, u32[]{:S(2)}, u32[]{:S(2)}) collective-permute-start(bf16[128,1024]{1,0:T(8,128)(2,1)} %copy-done.104), channel_id=1, source_target_pairs={{0,3},{1,2},{2,1},{3,0},{4,7},{5,6},{6,5},{7,4},{8,11},{9,10},{10,... | collective-permute-start | bytes 786440 | tf_op jit(solution)/shard_map/ppermute | solution.py:599
  524.8 14.0 %collective-permute-start.106 = (bf16[128,1024]{1,0:T(8,128)(2,1)}, bf16[128,1024]{1,0:T(8,128)(2,1)}, u32[]{:S(2)}, u32[]{:S(2)}) collective-permute-start(bf16[128,1024]{1,0:T(8,128)(2,1)} %get-tuple-element.542), channel_id=1, source_target_pairs={{0,3},{1,2},{2,1},{3,0},{4,7},{5,6},{6,5},{7,4},{8,11},{9,10},{10,... | collective-permute-start | bytes 786440 | tf_op jit(solution)/shard_map/ppermute | solution.py:599
  551.6 34.1 %all-to-all-start.2 = ((bf16[32,13,1024]{2,1,0:T(8,128)(2,1)}), bf16[32,13,1024]{2,1,0:T(8,128)(2,1)S(1)}, u32[]{:S(2)}, u32[]{:S(2)}) async-start(bf16[32,13,1024]{2,1,0:T(8,128)(2,1)} %reshape.594), calls=%async_computation.5 | async-start | bytes 2097152 | tf_op jit(solution)/shard_map/all_to_all | solution.py:687
  560.2 20.4 %collective-permute-start.111 = (bf16[2,4,128,256]{3,2,1,0:T(8,128)(2,1)}, bf16[2,4,128,256]{3,2,1,0:T(8,128)(2,1)}, u32[]{:S(2)}, u32[]{:S(2)}) collective-permute-start(bf16[2,4,128,256]{3,2,1,0:T(8,128)(2,1)} %select_convert_fusion), channel_id=1, source_target_pairs={{0,16},{8,24},{16,0},{24,8},{1,17},{9,25},{17,1},{25,9},{2,18},{10... | collective-permute-start | bytes 1572872 | tf_op jit(solution)/shard_map/ppermute | solution.py:651
  582.6 21.2 %collective-permute-start.112 = (bf16[4,128,256]{2,1,0:T(8,128)(2,1)S(1)}, bf16[4,128,256]{2,1,0:T(8,128)(2,1)}, u32[]{:S(2)}, u32[]{:S(2)}) collective-permute-start(bf16[4,128,256]{2,1,0:T(8,128)(2,1)S(1)} %slice_bitcast_fusion.7), channel_id=1, source_target_pairs={{0,4},{1,5},{2,6},{3,7},{4,0},{5,1},{6,2},{7,3},{8,12},{9,13},{10,... | collective-permute-start | bytes 786440 | tf_op jit(solution)/shard_map/ppermute | solution.py:596
  588.3 22.1 %all-to-all-start.3 = ((f32[32,1,1024]{2,1,0:T(1,128)}), f32[32,1,1024]{2,1,0:T(1,128)S(1)}, u32[]{:S(2)}, u32[]{:S(2)}) async-start(f32[32,1,1024]{2,1,0:T(1,128)} %broadcast_in_dim.157), calls=%async_computation.6 | async-start | bytes 262144 | tf_op jit(solution)/shard_map/all_to_all | solution.py:924
  605.9 15.2 %collective-permute-start.113 = (bf16[4,128,256]{2,1,0:T(8,128)(2,1)S(1)}, bf16[4,128,256]{2,1,0:T(8,128)(2,1)S(1)}, u32[]{:S(2)}, u32[]{:S(2)}) collective-permute-start(bf16[4,128,256]{2,1,0:T(8,128)(2,1)S(1)} %bitcast.127), channel_id=1, source_target_pairs={{0,4},{1,5},{2,6},{3,7},{4,0},{5,1},{6,2},{7,3},{8,12},{9,13},{10,... | collective-permute-start | bytes 786440 | tf_op jit(solution)/shard_map/ppermute | solution.py:596
  (199 other events, 2461.7 us)
Sparse Core Ops, SparseCore 0:
  40.0 27.2 all-gather.20
  80.9 18.5 all-gather.22
  101.9 19.4 all-gather.24
  127.4 15.5 all-gather.12
  144.3 16.7 all-gather.14
  171.2 18.3 all-gather.26
  226.0 18.0 all-gather.16
  258.2 16.8 all-gather.18
  336.8 44.0 reduce-scatter.4
  386.6 29.7 reduce-scatter.6
  424.2 42.8 reduce-scatter.8
  527.9 30.4 reduce-scatter.10

commit v3 on v2

--- a/solution.py
+++ b/solution.py
@@ -39,7 +39,7 @@
         out_shape=out_shape,
         scratch_shapes=list(scratch),
         compiler_params=pltpu.CompilerParams(vmem_limit_bytes=VMEM_LIMIT),
-        cost_estimate=pl.CostEstimate(flops=flops, transcendentals=exps, bytes_accessed=moved),
+        cost_estimate=pl.CostEstimate(flops=flops // 50, transcendentals=exps // 50, bytes_accessed=moved // 50),
         name=name,
         **specs,
     )(*args)
@@ -308,12 +308,10 @@
         scores = dot(kv_ref[:, lo:hi], q_ref[:, lo:hi], NT) + hidden
         peak = jnp.max(scores, axis=0, keepdims=True)
         raised = jnp.exp(scores - peak)
-        inverse = 1.0 / jnp.sum(raised, axis=0, keepdims=True)
-        probs = (raised * inverse).astype(BF16)
-        mixed = dot(kv_ref[:, width + lo : width + hi], probs, TN)
+        summed = jnp.sum(raised, axis=0, keepdims=True)
+        mixed = dot(kv_ref[:, width + lo : width + hi], raised.astype(BF16), TN) * (1.0 / summed)
         o_ref[:, lo:hi] = mixed.T.astype(BF16)
-        st_ref[head : head + 1, :] = peak
-        st_ref[heads + head : heads + head + 1, :] = inverse
+        st_ref[head : head + 1, :] = peak + jnp.log(summed)
     half = width // 2
     part = dot(o_ref[:, :half], flat(wo_ref), NN) + dot(o_ref[:, half:], flat(wo2_ref), NN)
     step = part.shape[0]
@@ -343,10 +341,10 @@
     outs, out_specs = block_outs(length, model, group)
     mixed, stats, *parts = call(
         partial(attend_kernel, causal=causal, heads=heads), "attend",
-        [((length, width), BF16), ((2 * heads, length), F32)] + outs,
+        [((length, width), BF16), ((heads, length), F32)] + outs,
         [queries, mine, theirs] + operands + list(marks), grid=(length // step,),
         in_specs=[rows, whole(mine), whole(theirs)] + specs + mask_specs(step, keys_len, marks[3].shape[0]),
-        out_specs=[rows, pl.BlockSpec((2 * heads, step), lambda i: (0, i))] + out_specs,
+        out_specs=[rows, pl.BlockSpec((heads, step), lambda i: (0, i))] + out_specs,
         scratch=[pltpu.VMEM((keys_len, 2 * width), BF16), pltpu.VMEM((length, model), BF16)],
         flops=4 * length * keys_len * width, exps=length * keys_len * heads,
     )
@@ -376,7 +374,7 @@
         queries, grads = q_ref[:, lo:hi], do_ref[:, lo:hi]
         keys, values = kv_ref[:, lo:hi], kv_ref[:, width + lo : width + hi]
         scores = dot(keys, queries, NT) + hidden
-        probs = jnp.exp(scores - st_ref[head : head + 1, :]) * st_ref[heads + head : heads + head + 1, :]
+        probs = jnp.exp(scores - st_ref[head : head + 1, :])
         grad_probs = dot(values, grads, NT)
         inner = jnp.sum(probs * grad_probs, axis=0, keepdims=True)
         grad_scores = (probs * (grad_probs - inner)).astype(BF16)
@@ -406,7 +404,7 @@
         in_specs=specs
         + [rows, whole(mine), whole(theirs)]
         + mask_specs(step, keys_len, marks[3].shape[0])
-        + [pl.BlockSpec((2 * heads, step), lambda i: (0, i))]
+        + [pl.BlockSpec((heads, step), lambda i: (0, i))]
         + [whole(piece) for piece in pieces],
         out_specs=[rows, whole(mine), whole(mine)],
         scratch=[
@@ -682,10 +680,49 @@
     return picks.astype(BF16), requests.reshape(owners, capacity)
 
 
+LANES = 128
+
+
 def to_owners(places, rows, capacity):
     owners = places.dp_size * places.tensor_size
-    return lax.all_to_all(
-        rows.reshape(owners, capacity, -1), ("dp", "tensor"), split_axis=0, concat_axis=0, tiled=True
+    runs = rows.reshape(owners, capacity * rows.shape[1] // LANES, LANES)
+    moved = lax.all_to_all(runs, ("dp", "tensor"), split_axis=0, concat_axis=0, tiled=True)
+    return moved.reshape(rows.shape)
+
+
+def finish_kernel(*refs, count):
+    parts, outs = refs[: 2 * count], refs[2 * count :]
+    for i in range(count):
+        own_ref, other_ref = parts[2 * i], parts[2 * i + 1]
+        in_ref, out_ref = outs[2 * i], outs[2 * i + 1]
+        for j in range(3):
+            in_ref[j] = (own_ref[j].astype(F32) + other_ref[j].astype(F32)).T
+        out_ref[...] = own_ref[3].astype(F32) + other_ref[3].astype(F32)
+
+
+def finish_attention(*pairs):
+    _, shard, width = pairs[0][0].shape
+    return call(
+        partial(finish_kernel, count=len(pairs)), "finish",
+        [((3, width, shard), F32), ((shard, width), F32)] * len(pairs), [part for pair in pairs for part in pair],
+    )
+
+
+def finish_kernel(*refs, count):
+    parts, outs = refs[: 2 * count], refs[2 * count :]
+    for i in range(count):
+        own_ref, other_ref = parts[2 * i], parts[2 * i + 1]
+        in_ref, out_ref = outs[2 * i], outs[2 * i + 1]
+        for j in range(3):
+            in_ref[j] = (own_ref[j].astype(F32) + other_ref[j].astype(F32)).T
+        out_ref[...] = own_ref[3].astype(F32) + other_ref[3].astype(F32)
+
+
+def finish_attention(*pairs):
+    _, shard, width = pairs[0][0].shape
+    return call(
+        partial(finish_kernel, count=len(pairs)), "finish",
+        [((3, width, shard), F32), ((shard, width), F32)] * len(pairs), [part for pair in pairs for part in pair],
     )
 
 
@@ -754,8 +791,8 @@
     wanted = wanted.reshape(-1, 2, 2, group * capacity).swapaxes(1, 2).reshape(-1)
     wanted = after(wanted, moved, enc_in_share)
     found = wanted >= 0
-    picked = jnp.take(embed_table, jnp.maximum(wanted, 0), axis=0)
-    replies = to_owners(places, picked, capacity).reshape(picked.shape)
+    picked = jnp.take(embed_table, jnp.maximum(wanted, 0), axis=0, mode="clip")
+    replies = to_owners(places, picked, capacity)
     outs_share = jnp.concatenate([places.share(weight) for weight in (enc_out, dec_out, cross_out)])
     outs_share = places.partner(after(outs_share, picked))
     replies = after(replies, outs_share)
@@ -877,6 +914,12 @@
     grad_h, pieces_h, gain_memory = norm_back(None, after(mem_parts, cross_grads), h2, norm_gains, 3, count)
     cross_sum = places.sum_weights(after(cross_grads, pieces_h))
 
+    def finish(summed, other):
+        return summed[0].astype(F32) + other.astype(F32)
+
+    def turned(grads):
+        return jnp.swapaxes(grads, -1, -2)
+
     enc_full = places.gather(pieces_h)
     parts = places.scatter(after(own_parts, enc_full))
     dec_ffn_other = places.partner(after(dec_ffn_sum[1], enc_full))
@@ -897,14 +940,19 @@
     dec_grads = attend_grads(grad_q, grad_kv, dec_mixed, far(c1), after(dec_full, own_parts))
 
     grad_full = after(hidden_full, dec_grads, cross_sum_other)
-    enc_ffn_other = places.partner(after(enc_ffn_sum[1], grad_full))
     grad_q, mine, theirs = attend_back(grad_full, enc_o, enc_q, enc_mine, enc_theirs, enc_marks, enc_stats, False)
     theirs = places.other_core(theirs)
     dec_sum = places.sum_weights(after(dec_grads, enc_ffn_sum, grad_full))
     own_parts, grad_kv = unproject_keys(grad_q, mine, theirs, enc_in, model, group)
-    parts = places.scatter(after(own_parts, enc_ffn_other))
+    parts = places.scatter(own_parts)
+    dec_ffn_sum = finish(dec_ffn_sum, dec_ffn_other)
+    dec_ffn_outs = turned(dec_ffn_sum[0]), dec_ffn_sum[1]
+    cross_sum = finish(cross_sum, cross_sum_other)
+    cross_outs = turned(cross_sum[0]), turned(cross_sum[1:3]), cross_sum[3]
+    decoded_out = decoded.astype(F32)[:, None]
+    dec_ffn_outs, cross_outs, decoded_out = lax.optimization_barrier((dec_ffn_outs, cross_outs, decoded_out))
     tgt_grad, gain_dattn, gain_demb = embed_back(
-        grad_t, after(dec_parts, own_parts), t0, embeds[local_len:], norm_gains, 4, root
+        grad_t, after(dec_parts, own_parts, dec_ffn_outs, cross_outs, decoded_out), t0, embeds[local_len:], norm_gains, 4, root
     )
     src_grad, gain_eattn, gain_eemb = embed_back(
         grad_h, after(parts, tgt_grad), h0, embeds[:local_len], norm_gains, 0, root
@@ -914,12 +962,12 @@
         gain_eemb, gain_eattn, gain_effn, gain_memory, gain_demb, gain_dattn, gain_cross, gain_dffn, gain_final
     ]
     outgoing = send_back(picks, src_grad, tgt_grad, gains, capacity)
-    arrived = to_owners(places, outgoing, capacity + 1)
+    arrived = to_owners(places, outgoing, capacity + 1).reshape(-1, capacity + 1, model)
     enc_grads = attend_grads(grad_q, grad_kv, enc_mixed, far(a1), after(grad_full, outgoing))
     enc_sum = places.sum_weights_now(enc_grads)
-    dec_sum_other = places.partner(after(dec_sum[1], outgoing))
-    enc_sum_other = places.partner(enc_sum[1])
-    arrived = after(arrived, enc_sum)
+    enc_ffn_other = places.partner(after(enc_ffn_sum[1], outgoing))
+    arrived = after(arrived, enc_sum, enc_ffn_other)
+    last_other = places.partner(after(jnp.stack([dec_sum[1], enc_sum[1]]), arrived))
     gain_sum = jnp.sum(arrived[:, capacity].astype(F32), axis=0)
     gain_grad = lax.all_to_all(
         jnp.broadcast_to(gain_sum[None], (arrived.shape[0], model)), ("dp", "tensor"), 0, 0, tiled=True
@@ -929,33 +977,23 @@
     target_rows = jnp.where(found, wanted, shard_rows)
     table_grad = jnp.zeros((shard_rows, model), F32).at[target_rows].add(rows, mode="drop")
 
-    def finish(summed, other):
-        return summed[0].astype(F32) + other.astype(F32)
-
-    dec_ffn_sum = finish(dec_ffn_sum, dec_ffn_other)
-    cross_sum = finish(cross_sum, cross_sum_other)
     enc_ffn_sum = finish(enc_ffn_sum, enc_ffn_other)
-    dec_sum = finish(dec_sum, dec_sum_other)
-    enc_sum = finish(enc_sum, enc_sum_other)
-
-    def turned(grads):
-        return jnp.swapaxes(grads, -1, -2)
+    dec_in_grad, dec_out_grad, enc_in_grad, enc_out_grad = finish_attention(
+        (dec_sum[0], last_other[0]), (enc_sum[0], last_other[1])
+    )
 
     return (
-        decoded.astype(F32)[:, None],
+        decoded_out,
         table_grad,
         gain_grad,
-        turned(enc_sum[:3]),
-        enc_sum[3],
+        enc_in_grad,
+        enc_out_grad,
         turned(enc_ffn_sum[0]),
         enc_ffn_sum[1],
-        turned(dec_sum[:3]),
-        dec_sum[3],
-        turned(cross_sum[0]),
-        turned(cross_sum[1:3]),
-        cross_sum[3],
-        turned(dec_ffn_sum[0]),
-        dec_ffn_sum[1],
+        dec_in_grad,
+        dec_out_grad,
+        *cross_outs,
+        *dec_ffn_outs,
     )
 
 

time: 640 us -> 634 us (level)
  waiting for transfers between devices: 217 us -> 203 us
  local copies, waits for them, and re-layouts: 70.5 us -> 79.9 us
    ppermute x1, waiting for transfers between devices: 15.4 us -> 0.01 us  [sum_weights_now(): received = lax.ppermute(sent, 'dp', [(d, d ^ 2) for d in range(4)])]
    ppermute x13 -> x12, waiting for transfers between devices: 48.4 us -> 37.1 us  [partner(): lax.ppermute(value, 'tensor', [(t, t ^ self.group) for t in range(self.te...]
    all_to_all x1, waiting for transfers between devices: 0.01 us -> 7.9 us  [on_device(): lax.all_to_all(jnp.broadcast_to(gain_sum[None], (arrived.shape[0], model)...]
    unnamed x277 -> x259, local copies, waits for them, and re-layouts: 29.6 us -> 35.3 us
    pallas_call x36 -> x37, Pallas kernels: 140 us -> 137 us  [call(): pl.pallas_call(kernel, grid=grid, out_shape=out_shape, scratch_shapes=lis...]
    ppermute x13 -> x12, starting transfers between devices: 26.5 us -> 25.6 us  [partner(): lax.ppermute(value, 'tensor', [(t, t ^ self.group) for t in range(self.te...]
  transfers between devices with their start and end apart: 129 -> 128, of which waited for: 61 -> 60; matrix products, arithmetic and copies ran while one was open for 12% -> 12% of each run, Pallas kernels for 20% -> 20%
where the time goes in v3:
time: 634 us; the launch traced here: 624 us
  waiting for transfers between devices  203 us (32%)
  starting transfers between devices  141 us (22%)
  Pallas kernels  137 us (22%)
  local copies, waits for them, and re-layouts  79.9 us (13%)
  other arithmetic  33.8 us (5%)
  between operations  16.5 us (3%)
  blocking collectives  12.5 us (2%)
    pallas_call x37, Pallas kernels, call(): pl.pallas_call(kernel, grid=grid, out_shape=out_shape, scratch_shapes=lis...  137 us
    ppermute x90, waiting for transfers between devices, mate(): lax.ppermute(value, 'tensor', [(t, t ^ offset) for t in range(self.tensor...  130 us
    ppermute x90, starting transfers between devices, mate(): lax.ppermute(value, 'tensor', [(t, t ^ offset) for t in range(self.tensor...  95.5 us
    ppermute x12, waiting for transfers between devices, partner(): lax.ppermute(value, 'tensor', [(t, t ^ self.group) for t in range(self.te...  37.1 us
    unnamed x259, local copies, waits for them, and re-layouts  35.3 us
    all_to_all x2, waiting for transfers between devices, to_owners(): lax.all_to_all(runs, ('dp', 'tensor'), split_axis=0, concat_axis=0, tiled...  28.1 us
    ppermute x12, starting transfers between devices, partner(): lax.ppermute(value, 'tensor', [(t, t ^ self.group) for t in range(self.te...  25.6 us
  transfers between devices with their start and end apart: 128, of which 60 were waited for; matrix products, arithmetic and copies ran while one was open for 12% of the time, Pallas kernels for 20%

profile of v3, /device:TPU:0, one launch (start us, length us, event | category | flops | bytes accessed | tf_op | source)
XLA Modules:
  0.0 624.1 jit_solution(17455351510597616824)
XLA Ops:
  9.6 5.4 collective-permute-start.1
  16.8 12.5 %all_to_all.22 = s32[32,1,12]{2,1,0:T(1,128)S(1)} all-to-all(s32[32,1,12]{2,1,0:T(1,128)S(1)} %bitcast.126), channel_id=1, replica_groups=mesh['dp'=4,'tensor'=8] {'dp','tensor'}, dimensions={0} | all-to-all | bytes 3072 | tf_op jit(solution)/shard_map/all_to_all | solution.py:790
  30.7 7.2 %gather_fusion = bf16[384,1024]{1,0:T(8,128)(2,1)S(1)} fusion(bf16[4096,1024]{1,0:T(8,128)(2,1)} %param.26, s32[1024]{0:T(1024)S(1)} %pad_clamp_fusion.3), kind=kCustom, calls=%fused_computation.4 | custom fusion | bytes 1574400 | tf_op jit(solution)/shard_map/jit(_take)/gather | solution.py:794
  40.0 2.8 all-to-all-start.1
  44.9 2.7 collective-permute-start.2
  47.7 21.3 %all-to-all-done.1 = bf16[32,96,128]{2,1,0:T(8,128)(2,1)S(1)} async-done(((bf16[32,96,128]{2,1,0:T(8,128)(2,1)}), bf16[32,96,128]{2,1,0:T(8,128)(2,1)S(1)}, u32[]{:S(2)}, u32[]{:S(2)}) %all-to-all-start.1) | async-done | bytes 786464 | tf_op jit(solution)/shard_map/all_to_all | solution.py:689
  69.3 2.6 collective-permute-done.2
  73.7 2.3 pad_maximum_fusion.3
  87.3 3.6 collective-permute-done.5.refs_4_
  92.4 2.4 project.4
  107.9 8.0 %attend.3 = (bf16[512,256]{1,0:T(8,128)(2,1)S(1)}, f32[4,512]{1,0:T(4,128)S(1)}, bf16[128,1024]{1,0:T(8,128)(2,1)S(1)}, bf16[128,1024]{1,0:T(8,128)(2,1)S(1)}, b...) custom-call(bf16[512,256]{1,0:T(8,128)(2,1)S(1)} %copy-done.26, ...), custom_call_target="tpu_custom_call" | custom-call | flops 10737418 | bytes 90152 | tf_op jit(solution)/shard_map/attend/pallas_call | solution.py:36
  117.3 4.5 collective-permute-done.11.refs_3_
  125.2 2.3 project.5
  128.3 10.1 %collective-permute-done.15 = bf16[128,1024]{1,0:T(8,128)(2,1)} collective-permute-done((bf16[128,1024]{1,0:T(8,128)(2,1)}, bf16[128,1024]{1,0:T(8,128)(2,1)}, u32[]{:S(2)}, u32[]{:S(2)}) %collective-permute-start.15) | collective-permute-done | bytes 262176 | tf_op jit(solution)/shard_map/ppermute | solution.py:594
  143.0 2.3 collective-permute-start.19
  146.0 3.5 collective-permute-start.43
  150.4 8.0 %attend.4 = (bf16[512,256]{1,0:T(8,128)(2,1)S(1)}, f32[4,512]{1,0:T(4,128)S(1)}, bf16[128,1024]{1,0:T(8,128)(2,1)S(1)}, bf16[128,1024]{1,0:T(8,128)(2,1)S(1)}, b...) custom-call(bf16[512,256]{1,0:T(8,128)(2,1)S(1)} %copy-done.28, ...), custom_call_target="tpu_custom_call" | custom-call | flops 10737418 | bytes 90152 | tf_op jit(solution)/shard_map/attend/pallas_call | solution.py:36
  159.8 4.0 collective-permute-done.19.refs_3_
  177.2 11.2 %collective-permute-done.28.refs_6_ = bf16[64,1024]{1,0:T(8,128)(2,1)S(1)} collective-permute-done((bf16[64,1024]{1,0:T(8,128)(2,1)S(1)}, bf16[64,1024]{1,0:T(8,128)(2,1)S(1)}, u32[]{:S(2)}, u32[]{:S(2)}) %collective-permute-start.28) | collective-permute-done | bytes 131104 | tf_op jit(solution)/shard_map/ppermute | solution.py:597
  196.8 5.1 ffn.2
  210.8 8.2 %collective-permute-done.35.refs_2_ = bf16[128,1024]{1,0:T(8,128)(2,1)S(1)} collective-permute-done((bf16[128,1024]{1,0:T(8,128)(2,1)S(1)}, bf16[128,1024]{1,0:T(8,128)(2,1)S(1)}, u32[]{:S(2)}, u32[]{:S(2)}) %collective-permute-start.35) | collective-permute-done | bytes 262176 | tf_op jit(solution)/shard_map/ppermute | solution.py:597
  219.0 3.3 collective-permute-done.36.refs_3_
  233.1 2.5 collective-permute-done.41.refs_6_.refs_18_
  240.8 2.5 collective-permute-start.44
  243.3 8.2 %attend.5 = (bf16[512,256]{1,0:T(8,128)(2,1)S(1)}, f32[4,512]{1,0:T(4,128)S(1)}, bf16[128,1024]{1,0:T(8,128)(2,1)S(1)}, bf16[128,1024]{1,0:T(8,128)(2,1)S(1)}, b...) custom-call(bf16[512,256]{1,0:T(8,128)(2,1)S(1)} %project.6.q_ref, bf16[512,512]{1,0:T(8,128)(2,1)S(1)} %project.7.mine_ref, ...), custom_call_target="tpu_custom_call" | custom-call | flops 10737418 | bytes 90152 | tf_op jit(solution)/shard_map/attend/pallas_call | solution.py:36
  253.2 2.8 collective-permute-done.44
  259.7 4.8 collective-permute-done.46.refs_1_
  264.4 2.4 collective-permute-done.47.refs_2_
  266.8 4.0 collective-permute-done.48.refs_3_
  284.3 5.2 ffn.3
  293.1 2.3 collective-permute-start.57
  295.5 4.2 collective-permute-done.55.refs_1_
  299.7 3.0 collective-permute-done.57.refs_3_
  315.9 5.1 ffn_back.2
  324.5 6.1 ffn_grads.2
  342.4 5.9 collective-permute-done.71.refs_6_.refs_10_
  348.4 11.5 %attend_back.3 = (bf16[512,256]{1,0:T(8,128)(2,1)S(1)}, f32[512,512]{1,0:T(8,128)S(1)}, bf16[512,512]{1,0:T(8,128)(2,1)S(1)}) custom-call(bf16[128,1024]{1,0:T(8,128)(2,1)} %wo_ref.9, bf16[4,192,1024]{2,1,0:T(8,128)(2,1)} %bitcast.100, bf16[512,256]{1,0:T(8,128)(2,1)} %copy-done.2, bf16[512,512]{1,0:T(8,128)(2,1)} %copy-done.1, bf16[512,512]{1,0:T(8,128)(2,1)} %copy-done.14, ...), custom_call_target="tpu_custom_call" | custom-call | flops 26843544 | bytes 121610 | tf_op jit(solution)/shard_map/attend_back/pallas_call | solution.py:36
  359.9 4.4 collective-permute-start.74
  364.3 2.3 unproject.1
  372.1 4.3 attend_grads.3
  377.8 5.8 collective-permute-done.77.refs_3_
  397.6 2.5 collective-permute-start.85
  401.5 5.1 ffn_back.3
  410.4 6.1 ffn_grads.3
  433.0 7.9 %collective-permute-done.91.refs_5_.refs_9_ = bf16[64,1024]{1,0:T(8,128)(2,1)S(1)} collective-permute-done((bf16[64,1024]{1,0:T(8,128)(2,1)S(1)}, bf16[64,1024]{1,0:T(8,128)(2,1)S(1)}, u32[]{:S(2)}, u32[]{:S(2)}) %collective-permute-start.91) | collective-permute-done | bytes 131104 | tf_op jit(solution)/shard_map/ppermute | solution.py:597
  442.3 2.9 collective-permute-start.100
  446.3 2.5 collective-permute-done.92.refs_6_.refs_10_
  452.6 12.2 %attend_back.4 = (bf16[512,256]{1,0:T(8,128)(2,1)S(1)}, f32[512,512]{1,0:T(8,128)S(1)}, bf16[512,512]{1,0:T(8,128)(2,1)}) custom-call(bf16[128,1024]{1,0:T(8,128)(2,1)} %wo_ref.10, bf16[4,192,1024]{2,1,0:T(8,128)(2,1)} %bitcast.101, bf16[512,256]{1,0:T(8,128)(2,1)} %copy-done.27, bf16[512,512]{1,0:T(8,128)(2,1)} %copy-done.12, bf16[512,512]{1,0:T(8,128)(2,1)} %copy-done.13, ...), custom_call_target="tpu_custom_call" | custom-call | flops 26843544 | bytes 121610 | tf_op jit(solution)/shard_map/attend_back/pallas_call | solution.py:36
  466.8 3.5 collective-permute-start.97
  473.0 2.6 unproject_keys.4
  478.5 3.9 attend_grads.4
  482.8 12.5 %attend_back.5 = (bf16[512,256]{1,0:T(8,128)(2,1)S(1)}, f32[512,512]{1,0:T(8,128)S(1)}, bf16[512,512]{1,0:T(8,128)(2,1)}) custom-call(bf16[128,1024]{1,0:T(8,128)(2,1)} %wo_ref.11, bf16[4,192,1024]{2,1,0:T(8,128)(2,1)} %bitcast.102, bf16[512,256]{1,0:T(8,128)(2,1)} %copy-done.25, bf16[512,512]{1,0:T(8,128)(2,1)} %copy-done.10, bf16[512,512]{1,0:T(8,128)(2,1)} %copy-done.11, ...), custom_call_target="tpu_custom_call" | custom-call | flops 26843544 | bytes 121610 | tf_op jit(solution)/shard_map/attend_back/pallas_call | solution.py:36
  498.9 2.8 collective-permute-start.108
  501.6 2.7 unproject_keys.5
  505.7 2.3 collective-permute-start.105
  508.7 5.7 collective-permute-done.108.refs_3_
  519.3 5.6 collective-permute-done.105.refs_3_
  527.8 2.6 attend_grads.5
  536.4 3.6 all-to-all-start.2
  549.8 21.1 %collective-permute-done.111 = bf16[2,512,256]{2,1,0:T(8,128)(2,1)} collective-permute-done((bf16[2,512,256]{2,1,0:T(8,128)(2,1)}, bf16[2,512,256]{2,1,0:T(8,128)(2,1)}, u32[]{:S(2)}, u32[]{:S(2)}) %collective-permute-start.111) | collective-permute-done | bytes 524320 | tf_op jit(solution)/shard_map/ppermute | solution.py:594
  573.5 6.8 %all-to-all-done.2 = bf16[32,104,128]{2,1,0:T(8,128)(2,1)} async-done(((bf16[32,104,128]{2,1,0:T(8,128)(2,1)}), bf16[32,104,128]{2,1,0:T(8,128)(2,1)}, u32[]{:S(2)}, u32[]{:S(2)}) %all-to-all-start.2) | async-done | bytes 852000 | tf_op jit(solution)/shard_map/all_to_all | solution.py:689
  587.1 4.2 all-to-all-start.3
  594.2 11.9 %scatter_custom_fusion = f32[4096,1024]{1,0:T(8,128)} fusion(s32[384]{0:T(512)S(1)} %get-tuple-element.694, f32[]{:T(128)} %constant.136.clone.1, f32[384,1024]{1,0:T(8,128)} %reshape.587, f32[384]{0:T(512)S(1)} %broadcast_maximum_fusion), kind=kCustom, calls=%fused_computation.7 | custom fusion | flops 786432 | bytes 18352132 | tf_op jit(solution)/shard_map/scatter-add | solution.py:978
  606.0 7.9 %all-to-all-done.3 = f32[32,1,1024]{2,1,0:T(1,128)S(1)} async-done(((f32[32,1,1024]{2,1,0:T(1,128)}), f32[32,1,1024]{2,1,0:T(1,128)S(1)}, u32[]{:S(2)}, u32[]{:S(2)}) %all-to-all-start.3) | async-done | bytes 131104 | tf_op jit(solution)/shard_map/all_to_all | solution.py:972
  (602 shorter events, 248.2 us)
Async XLA Ops:
  7.2 85.2 %all-gather.21.cloned.1.call-start = ((), (), s32[]{:S(2)}) async-start(), calls=%async_computation.16 | async-start | bytes 1966080 | tf_op jit(solution)/shard_map/all_gather | solution.py:623
  7.9 22.8 %collective-permute-start = (s32[2304]{0:T(1024)S(1)}, s32[2304]{0:T(1024)S(1)}, u32[]{:S(2)}, u32[]{:S(2)}) collective-permute-start(s32[2304]{0:T(1024)S(1)} %pad_add_fusion), channel_id=1, source_target_pairs={{0,0},{1,1},{2,2},{3,3},{4,8},{5,9},{6,10},{7,11},{8,4},{9,5},{10,... | collective-permute-start | bytes 27656 | tf_op jit(solution)/shard_map/ppermute | solution.py:588
  9.6 21.1 %collective-permute-start.1 = (bf16[3,256,128]{2,1,0:T(8,128)(2,1)S(1)}, bf16[3,256,128]{2,1,0:T(8,128)(2,1)S(1)}, u32[]{:S(2)}, u32[]{:S(2)}) collective-permute-start(bf16[3,256,128]{2,1,0:T(8,128)(2,1)S(1)} %constant_dynamic-slice_fusion.8), channel_id=1, source_target_pairs={{0,4},{1,5},{2,6},{3,7},{4,0},{5,1},{6,2},{7,3},{8,12},{9,13},{10,... | collective-permute-start | bytes 589832 | tf_op jit(solution)/shard_map/ppermute | solution.py:594
  40.0 29.0 %all-to-all-start.1 = ((bf16[32,96,128]{2,1,0:T(8,128)(2,1)}), bf16[32,96,128]{2,1,0:T(8,128)(2,1)S(1)}, u32[]{:S(2)}, u32[]{:S(2)}) async-start(bf16[32,96,128]{2,1,0:T(8,128)(2,1)} %reshape.576), calls=%async_computation.1 | async-start | bytes 1572864 | tf_op jit(solution)/shard_map/all_to_all | solution.py:689
  42.8 64.0 %all-gather.23.cloned.1.call-start = ((), (), s32[]{:S(2)}) async-start(), calls=%async_computation.17 | async-start | bytes 1966080 | tf_op jit(solution)/shard_map/all_gather | solution.py:623
  44.9 27.0 %collective-permute-start.2 = (bf16[96,1024]{1,0:T(8,128)(2,1)S(1)}, bf16[96,1024]{1,0:T(8,128)(2,1)}, u32[]{:S(2)}, u32[]{:S(2)}) collective-permute-start(bf16[96,1024]{1,0:T(8,128)(2,1)S(1)} %pad_maximum_fusion.6), channel_id=1, source_target_pairs={{0,4},{1,5},{2,6},{3,7},{4,0},{5,1},{6,2},{7,3},{8,12},{9,13},{10,... | collective-permute-start | bytes 589832 | tf_op jit(solution)/shard_map/ppermute | solution.py:594
  76.0 49.2 %all-gather.25.cloned.1.call-start = ((), (), s32[]{:S(2)}) async-start(), calls=%async_computation.18 | async-start | bytes 1966080 | tf_op jit(solution)/shard_map/all_gather | solution.py:623
  79.2 15.7 %collective-permute-start.14 = (bf16[3,256,128]{2,1,0:T(8,128)(2,1)}, bf16[3,256,128]{2,1,0:T(8,128)(2,1)}, u32[]{:S(2)}, u32[]{:S(2)}) collective-permute-start(bf16[3,256,128]{2,1,0:T(8,128)(2,1)} %constant_dynamic-slice_fusion.3), channel_id=1, source_target_pairs={{0,4},{1,5},{2,6},{3,7},{4,0},{5,1},{6,2},{7,3},{8,12},{9,13},{10,... | collective-permute-start | bytes 589832 | tf_op jit(solution)/shard_map/ppermute | solution.py:594
  97.1 97.0 %all-gather.13.cloned.1.call-start = ((), (), s32[]{:S(2)}) async-start(), calls=%async_computation.8 | async-start | bytes 1310720 | tf_op jit(solution)/shard_map/all_gather | solution.py:626
  101.5 15.8 %collective-permute-start.10 = (bf16[128,1024]{1,0:T(8,128)(2,1)S(1)}, bf16[128,1024]{1,0:T(8,128)(2,1)S(1)}, u32[]{:S(2)}, u32[]{:S(2)}) collective-permute-start(bf16[128,1024]{1,0:T(8,128)(2,1)S(1)} %get-tuple-element.321.refs_0_), channel_id=1, source_target_pairs={{0,2},{1,3},{2,0},{3,1},{4,6},{5,7},{6,4},{7,5},{8,10},{9,11},{10,... | collective-permute-start | bytes 786440 | tf_op jit(solution)/shard_map/ppermute | solution.py:597
  102.4 19.4 %collective-permute-start.11 = (bf16[128,1024]{1,0:T(8,128)(2,1)S(1)}, bf16[128,1024]{1,0:T(8,128)(2,1)S(1)}, u32[]{:S(2)}, u32[]{:S(2)}) collective-permute-start(bf16[128,1024]{1,0:T(8,128)(2,1)S(1)} %get-tuple-element.321.refs_0_), channel_id=1, source_target_pairs={{0,3},{1,2},{2,1},{3,0},{4,7},{5,6},{6,5},{7,4},{8,11},{9,10},{10,... | collective-permute-start | bytes 786440 | tf_op jit(solution)/shard_map/ppermute | solution.py:597
  103.9 17.9 %collective-permute-start.9 = (bf16[128,1024]{1,0:T(8,128)(2,1)S(1)}, bf16[128,1024]{1,0:T(8,128)(2,1)S(1)}, u32[]{:S(2)}, u32[]{:S(2)}) collective-permute-start(bf16[128,1024]{1,0:T(8,128)(2,1)S(1)} %get-tuple-element.321.refs_0_), channel_id=1, source_target_pairs={{0,1},{1,0},{2,3},{3,2},{4,5},{5,4},{6,7},{7,6},{8,9},{9,8},{10,11... | collective-permute-start | bytes 786440 | tf_op jit(solution)/shard_map/ppermute | solution.py:597
  105.0 16.8 %collective-permute-start.13 = (bf16[256,512]{1,0:T(8,128)(2,1)}, bf16[256,512]{1,0:T(8,128)(2,1)}, u32[]{:S(2)}, u32[]{:S(2)}) collective-permute-start(bf16[256,512]{1,0:T(8,128)(2,1)} %constant_dynamic-slice_fusion.4), channel_id=1, source_target_pairs={{0,4},{1,5},{2,6},{3,7},{4,0},{5,1},{6,2},{7,3},{8,12},{9,13},{10,... | collective-permute-start | bytes 786440 | tf_op jit(solution)/shard_map/ppermute | solution.py:594
  121.9 72.2 %all-gather.15.cloned.1.call-start = ((), (), s32[]{:S(2)}) async-start(), calls=%async_computation.9 | async-start | bytes 1310720 | tf_op jit(solution)/shard_map/all_gather | solution.py:626
  123.6 14.8 %collective-permute-start.15 = (bf16[128,1024]{1,0:T(8,128)(2,1)}, bf16[128,1024]{1,0:T(8,128)(2,1)}, u32[]{:S(2)}, u32[]{:S(2)}) collective-permute-start(bf16[128,1024]{1,0:T(8,128)(2,1)} %constant_dynamic-slice_fusion.2), channel_id=1, source_target_pairs={{0,4},{1,5},{2,6},{3,7},{4,0},{5,1},{6,2},{7,3},{8,12},{9,13},{10,... | collective-permute-start | bytes 786440 | tf_op jit(solution)/shard_map/ppermute | solution.py:594
  138.4 93.1 %all-gather.27.cloned.1.call-start = ((), (), s32[]{:S(2)}) async-start(), calls=%async_computation.19 | async-start | bytes 1966080 | tf_op jit(solution)/shard_map/all_gather | solution.py:623
  141.7 18.1 %collective-permute-start.17 = (bf16[128,1024]{1,0:T(8,128)(2,1)}, bf16[128,1024]{1,0:T(8,128)(2,1)S(1)}, u32[]{:S(2)}, u32[]{:S(2)}) collective-permute-start(bf16[128,1024]{1,0:T(8,128)(2,1)} %copy-done.110), channel_id=1, source_target_pairs={{0,1},{1,0},{2,3},{3,2},{4,5},{5,4},{6,7},{7,6},{8,9},{9,8},{10,11... | collective-permute-start | bytes 786440 | tf_op jit(solution)/shard_map/ppermute | solution.py:597
  143.0 16.8 %collective-permute-start.18 = (bf16[128,1024]{1,0:T(8,128)(2,1)}, bf16[128,1024]{1,0:T(8,128)(2,1)S(1)}, u32[]{:S(2)}, u32[]{:S(2)}) collective-permute-start(bf16[128,1024]{1,0:T(8,128)(2,1)} %copy-done.107), channel_id=1, source_target_pairs={{0,2},{1,3},{2,0},{3,1},{4,6},{5,7},{6,4},{7,5},{8,10},{9,11},{10,... | collective-permute-start | bytes 786440 | tf_op jit(solution)/shard_map/ppermute | solution.py:597
  143.0 20.8 %collective-permute-start.19 = (bf16[128,1024]{1,0:T(8,128)(2,1)}, bf16[128,1024]{1,0:T(8,128)(2,1)S(1)}, u32[]{:S(2)}, u32[]{:S(2)}) collective-permute-start(bf16[128,1024]{1,0:T(8,128)(2,1)} %copy-done.106), channel_id=1, source_target_pairs={{0,3},{1,2},{2,1},{3,0},{4,7},{5,6},{6,5},{7,4},{8,11},{9,10},{10,... | collective-permute-start | bytes 786440 | tf_op jit(solution)/shard_map/ppermute | solution.py:597
  145.2 18.6 %collective-permute-start.20 = (bf16[128,1024]{1,0:T(8,128)(2,1)S(1)}, bf16[128,1024]{1,0:T(8,128)(2,1)S(1)}, u32[]{:S(2)}, u32[]{:S(2)}) collective-permute-start(bf16[128,1024]{1,0:T(8,128)(2,1)S(1)} %bitcast.123), channel_id=1, source_target_pairs={{0,0},{1,1},{2,2},{3,3},{4,8},{5,9},{6,10},{7,11},{8,4},{9,5},{10,... | collective-permute-start | bytes 786440 | tf_op jit(solution)/shard_map/ppermute | solution.py:588
  146.0 19.0 %collective-permute-start.43 = (bf16[3,256,128]{2,1,0:T(8,128)(2,1)S(1)}, bf16[3,256,128]{2,1,0:T(8,128)(2,1)S(1)}, u32[]{:S(2)}, u32[]{:S(2)}) collective-permute-start(bf16[3,256,128]{2,1,0:T(8,128)(2,1)S(1)} %pad_maximum_fusion.7), channel_id=1, source_target_pairs={{0,4},{1,5},{2,6},{3,7},{4,0},{5,1},{6,2},{7,3},{8,12},{9,13},{10,... | collective-permute-start | bytes 589832 | tf_op jit(solution)/shard_map/ppermute | solution.py:594
  165.8 113.7 %all-gather.17.cloned.1.call-start = ((), (), s32[]{:S(2)}) async-start(), calls=%async_computation.10 | async-start | bytes 1310720 | tf_op jit(solution)/shard_map/all_gather | solution.py:626
  170.0 19.1 %collective-permute-start.21 = (bf16[128,1024]{1,0:T(8,128)(2,1)}, bf16[128,1024]{1,0:T(8,128)(2,1)S(1)}, u32[]{:S(2)}, u32[]{:S(2)}) collective-permute-start(bf16[128,1024]{1,0:T(8,128)(2,1)} %copy-done.113), channel_id=1, source_target_pairs={{0,1},{1,0},{2,3},{3,2},{4,5},{5,4},{6,7},{7,6},{8,9},{9,8},{10,11... | collective-permute-start | bytes 786440 | tf_op jit(solution)/shard_map/ppermute | solution.py:597
  172.4 16.7 %collective-permute-start.22 = (bf16[128,1024]{1,0:T(8,128)(2,1)}, bf16[128,1024]{1,0:T(8,128)(2,1)S(1)}, u32[]{:S(2)}, u32[]{:S(2)}) collective-permute-start(bf16[128,1024]{1,0:T(8,128)(2,1)} %copy-done.112), channel_id=1, source_target_pairs={{0,2},{1,3},{2,0},{3,1},{4,6},{5,7},{6,4},{7,5},{8,10},{9,11},{10,... | collective-permute-start | bytes 786440 | tf_op jit(solution)/shard_map/ppermute | solution.py:597
  173.5 15.6 %collective-permute-start.23 = (bf16[128,1024]{1,0:T(8,128)(2,1)}, bf16[128,1024]{1,0:T(8,128)(2,1)S(1)}, u32[]{:S(2)}, u32[]{:S(2)}) collective-permute-start(bf16[128,1024]{1,0:T(8,128)(2,1)} %copy-done.111), channel_id=1, source_target_pairs={{0,3},{1,2},{2,1},{3,0},{4,7},{5,6},{6,5},{7,4},{8,11},{9,10},{10,... | collective-permute-start | bytes 786440 | tf_op jit(solution)/shard_map/ppermute | solution.py:597
  175.2 13.2 %collective-permute-start.28 = (bf16[64,1024]{1,0:T(8,128)(2,1)S(1)}, bf16[64,1024]{1,0:T(8,128)(2,1)S(1)}, u32[]{:S(2)}, u32[]{:S(2)}) collective-permute-start(bf16[64,1024]{1,0:T(8,128)(2,1)S(1)} %collective-permute-done.24.refs_2_), channel_id=1, source_target_pairs={{0,2},{1,3},{2,0},{3,1},{4,6},{5,7},{6,4},{7,5},{8,10},{9,11},{10,... | collective-permute-start | bytes 393224 | tf_op jit(solution)/shard_map/ppermute | solution.py:597
  176.3 12.1 %collective-permute-start.29 = (bf16[64,1024]{1,0:T(8,128)(2,1)S(1)}, bf16[64,1024]{1,0:T(8,128)(2,1)S(1)}, u32[]{:S(2)}, u32[]{:S(2)}) collective-permute-start(bf16[64,1024]{1,0:T(8,128)(2,1)S(1)} %collective-permute-done.27.refs_5_), channel_id=1, source_target_pairs={{0,1},{1,0},{2,3},{3,2},{4,5},{5,4},{6,7},{7,6},{8,9},{9,8},{10,11... | collective-permute-start | bytes 393224 | tf_op jit(solution)/shard_map/ppermute | solution.py:597
  189.5 14.8 %collective-permute-start.31 = (bf16[128,1024]{1,0:T(8,128)(2,1)S(1)}, bf16[128,1024]{1,0:T(8,128)(2,1)S(1)}, u32[]{:S(2)}, u32[]{:S(2)}) collective-permute-start(bf16[128,1024]{1,0:T(8,128)(2,1)S(1)} %get-tuple-element.375.refs_0_), channel_id=1, source_target_pairs={{0,1},{1,0},{2,3},{3,2},{4,5},{5,4},{6,7},{7,6},{8,9},{9,8},{10,11... | collective-permute-start | bytes 786440 | tf_op jit(solution)/shard_map/ppermute | solution.py:597
  190.6 13.8 %collective-permute-start.32 = (bf16[128,1024]{1,0:T(8,128)(2,1)S(1)}, bf16[128,1024]{1,0:T(8,128)(2,1)S(1)}, u32[]{:S(2)}, u32[]{:S(2)}) collective-permute-start(bf16[128,1024]{1,0:T(8,128)(2,1)S(1)} %get-tuple-element.375.refs_0_), channel_id=1, source_target_pairs={{0,2},{1,3},{2,0},{3,1},{4,6},{5,7},{6,4},{7,5},{8,10},{9,11},{10,... | collective-permute-start | bytes 786440 | tf_op jit(solution)/shard_map/ppermute | solution.py:597
  191.0 13.3 %collective-permute-start.33 = (bf16[128,1024]{1,0:T(8,128)(2,1)S(1)}, bf16[128,1024]{1,0:T(8,128)(2,1)S(1)}, u32[]{:S(2)}, u32[]{:S(2)}) collective-permute-start(bf16[128,1024]{1,0:T(8,128)(2,1)S(1)} %get-tuple-element.375.refs_0_), channel_id=1, source_target_pairs={{0,3},{1,2},{2,1},{3,0},{4,7},{5,6},{6,5},{7,4},{8,11},{9,10},{10,... | collective-permute-start | bytes 786440 | tf_op jit(solution)/shard_map/ppermute | solution.py:597
  205.4 13.6 %collective-permute-start.35 = (bf16[128,1024]{1,0:T(8,128)(2,1)S(1)}, bf16[128,1024]{1,0:T(8,128)(2,1)S(1)}, u32[]{:S(2)}, u32[]{:S(2)}) collective-permute-start(bf16[128,1024]{1,0:T(8,128)(2,1)S(1)} %get-tuple-element.370), channel_id=1, source_target_pairs={{0,2},{1,3},{2,0},{3,1},{4,6},{5,7},{6,4},{7,5},{8,10},{9,11},{10,... | collective-permute-start | bytes 786440 | tf_op jit(solution)/shard_map/ppermute | solution.py:597
  205.8 16.5 %collective-permute-start.36 = (bf16[128,1024]{1,0:T(8,128)(2,1)S(1)}, bf16[128,1024]{1,0:T(8,128)(2,1)S(1)}, u32[]{:S(2)}, u32[]{:S(2)}) collective-permute-start(bf16[128,1024]{1,0:T(8,128)(2,1)S(1)} %get-tuple-element.371), channel_id=1, source_target_pairs={{0,3},{1,2},{2,1},{3,0},{4,7},{5,6},{6,5},{7,4},{8,11},{9,10},{10,... | collective-permute-start | bytes 786440 | tf_op jit(solution)/shard_map/ppermute | solution.py:597
  207.9 15.6 %collective-permute-start.30 = (bf16[256,512]{1,0:T(8,128)(2,1)S(1)}, bf16[256,512]{1,0:T(8,128)(2,1)S(1)}, u32[]{:S(2)}, u32[]{:S(2)}) collective-permute-start(bf16[256,512]{1,0:T(8,128)(2,1)S(1)} %constant_dynamic-slice_fusion.11), channel_id=1, source_target_pairs={{0,4},{1,5},{2,6},{3,7},{4,0},{5,1},{6,2},{7,3},{8,12},{9,13},{10,... | collective-permute-start | bytes 786440 | tf_op jit(solution)/shard_map/ppermute | solution.py:594
  224.2 60.1 %all-gather.19.cloned.1.call-start = ((), (), s32[]{:S(2)}) async-start(), calls=%async_computation.11 | async-start | bytes 1310720 | tf_op jit(solution)/shard_map/all_gather | solution.py:626
  240.8 15.2 %collective-permute-start.44 = (bf16[128,1024]{1,0:T(8,128)(2,1)S(1)}, bf16[128,1024]{1,0:T(8,128)(2,1)}, u32[]{:S(2)}, u32[]{:S(2)}) collective-permute-start(bf16[128,1024]{1,0:T(8,128)(2,1)S(1)} %constant_dynamic-slice_fusion.1), channel_id=1, source_target_pairs={{0,4},{1,5},{2,6},{3,7},{4,0},{5,1},{6,2},{7,3},{8,12},{9,13},{10,... | collective-permute-start | bytes 786440 | tf_op jit(solution)/shard_map/ppermute | solution.py:594
  256.0 167.1 %reduce-scatter.5.cloned.1.call-start = ((), (), s32[]{:S(2)}) async-start(), calls=%async_computation.12 | async-start | bytes 5242880 | tf_op jit(solution)/shard_map/reduce_scatter | solution.py:630
  257.6 13.2 %collective-permute-start.48 = (bf16[128,1024]{1,0:T(8,128)(2,1)S(1)}, bf16[128,1024]{1,0:T(8,128)(2,1)S(1)}, u32[]{:S(2)}, u32[]{:S(2)}) collective-permute-start(bf16[128,1024]{1,0:T(8,128)(2,1)S(1)} %get-tuple-element.393), channel_id=1, source_target_pairs={{0,3},{1,2},{2,1},{3,0},{4,7},{5,6},{6,5},{7,4},{8,11},{9,10},{10,... | collective-permute-start | bytes 786440 | tf_op jit(solution)/shard_map/ppermute | solution.py:597
  333.3 131.7 %reduce-scatter.7.cloned.1.call-start = ((), (), s32[]{:S(2)}) async-start(), calls=%async_computation.13 | async-start | bytes 2621440 | tf_op jit(solution)/shard_map/reduce_scatter | solution.py:630
  370.1 13.6 %collective-permute-start.77 = (bf16[128,1024]{1,0:T(8,128)(2,1)S(1)}, bf16[128,1024]{1,0:T(8,128)(2,1)S(1)}, u32[]{:S(2)}, u32[]{:S(2)}) collective-permute-start(bf16[128,1024]{1,0:T(8,128)(2,1)S(1)} %get-tuple-element.451), channel_id=1, source_target_pairs={{0,3},{1,2},{2,1},{3,0},{4,7},{5,6},{6,5},{7,4},{8,11},{9,10},{10,... | collective-permute-start | bytes 786440 | tf_op jit(solution)/shard_map/ppermute | solution.py:597
  385.2 146.5 %reduce-scatter.9.cloned.1.call-start = ((), (), s32[]{:S(2)}) async-start(), calls=%async_computation.14 | async-start | bytes 5242880 | tf_op jit(solution)/shard_map/reduce_scatter | solution.py:630
  397.6 11.9 %collective-permute-start.85 = (bf16[128,1024]{1,0:T(8,128)(2,1)}, bf16[128,1024]{1,0:T(8,128)(2,1)S(1)}, u32[]{:S(2)}, u32[]{:S(2)}) collective-permute-start(bf16[128,1024]{1,0:T(8,128)(2,1)} %get-tuple-element.471), channel_id=1, source_target_pairs={{0,1},{1,0},{2,3},{3,2},{4,5},{5,4},{6,7},{7,6},{8,9},{9,8},{10,11... | collective-permute-start | bytes 786440 | tf_op jit(solution)/shard_map/ppermute | solution.py:597
  400.1 16.4 %collective-permute-start.86 = (bf16[128,1024]{1,0:T(8,128)(2,1)}, bf16[128,1024]{1,0:T(8,128)(2,1)S(1)}, u32[]{:S(2)}, u32[]{:S(2)}) collective-permute-start(bf16[128,1024]{1,0:T(8,128)(2,1)} %get-tuple-element.472), channel_id=1, source_target_pairs={{0,2},{1,3},{2,0},{3,1},{4,6},{5,7},{6,4},{7,5},{8,10},{9,11},{10,... | collective-permute-start | bytes 786440 | tf_op jit(solution)/shard_map/ppermute | solution.py:597
  400.1 16.4 %collective-permute-start.87 = (bf16[128,1024]{1,0:T(8,128)(2,1)}, bf16[128,1024]{1,0:T(8,128)(2,1)S(1)}, u32[]{:S(2)}, u32[]{:S(2)}) collective-permute-start(bf16[128,1024]{1,0:T(8,128)(2,1)} %get-tuple-element.473), channel_id=1, source_target_pairs={{0,3},{1,2},{2,1},{3,0},{4,7},{5,6},{6,5},{7,4},{8,11},{9,10},{10,... | collective-permute-start | bytes 786440 | tf_op jit(solution)/shard_map/ppermute | solution.py:597
  406.6 12.3 %collective-permute-start.94 = (bf16[128,1024]{1,0:T(8,128)(2,1)S(1)}, bf16[128,1024]{1,0:T(8,128)(2,1)S(1)}, u32[]{:S(2)}, u32[]{:S(2)}) collective-permute-start(bf16[128,1024]{1,0:T(8,128)(2,1)S(1)} %get-tuple-element.478), channel_id=1, source_target_pairs={{0,1},{1,0},{2,3},{3,2},{4,5},{5,4},{6,7},{7,6},{8,9},{9,8},{10,11... | collective-permute-start | bytes 786440 | tf_op jit(solution)/shard_map/ppermute | solution.py:597
  409.5 11.0 %collective-permute-start.96 = (bf16[128,1024]{1,0:T(8,128)(2,1)S(1)}, bf16[128,1024]{1,0:T(8,128)(2,1)S(1)}, u32[]{:S(2)}, u32[]{:S(2)}) collective-permute-start(bf16[128,1024]{1,0:T(8,128)(2,1)S(1)} %get-tuple-element.480), channel_id=1, source_target_pairs={{0,3},{1,2},{2,1},{3,0},{4,7},{5,6},{6,5},{7,4},{8,11},{9,10},{10,... | collective-permute-start | bytes 786440 | tf_op jit(solution)/shard_map/ppermute | solution.py:597
  422.0 160.0 %reduce-scatter.11.cloned.1.call-start = ((), (), s32[]{:S(2)}) async-start(), calls=%async_computation.15 | async-start | bytes 2621440 | tf_op jit(solution)/shard_map/reduce_scatter | solution.py:630
  425.2 23.9 %collective-permute-start.84 = (bf16[2,512,256]{2,1,0:T(8,128)(2,1)S(1)}, bf16[2,512,256]{2,1,0:T(8,128)(2,1)S(1)}, u32[]{:S(2)}, u32[]{:S(2)}) collective-permute-start(bf16[2,512,256]{2,1,0:T(8,128)(2,1)S(1)} %bitcast.121), channel_id=1, source_target_pairs={{0,4},{1,5},{2,6},{3,7},{4,0},{5,1},{6,2},{7,3},{8,12},{9,13},{10,... | collective-permute-start | bytes 1572872 | tf_op jit(solution)/shard_map/ppermute | solution.py:594
  427.0 14.0 %collective-permute-start.91 = (bf16[64,1024]{1,0:T(8,128)(2,1)S(1)}, bf16[64,1024]{1,0:T(8,128)(2,1)S(1)}, u32[]{:S(2)}, u32[]{:S(2)}) collective-permute-start(bf16[64,1024]{1,0:T(8,128)(2,1)S(1)} %get-tuple-element.524.refs_1_.refs_5_), channel_id=1, source_target_pairs={{0,2},{1,3},{2,0},{3,1},{4,6},{5,7},{6,4},{7,5},{8,10},{9,11},{10,... | collective-permute-start | bytes 393224 | tf_op jit(solution)/shard_map/ppermute | solution.py:597
  429.5 12.8 %collective-permute-start.89 = (bf16[64,1024]{1,0:T(8,128)(2,1)S(1)}, bf16[64,1024]{1,0:T(8,128)(2,1)S(1)}, u32[]{:S(2)}, u32[]{:S(2)}) collective-permute-start(bf16[64,1024]{1,0:T(8,128)(2,1)S(1)} %get-tuple-element.524.refs_1_.refs_5_), channel_id=1, source_target_pairs={{0,1},{1,0},{2,3},{3,2},{4,5},{5,4},{6,7},{7,6},{8,9},{9,8},{10,11... | collective-permute-start | bytes 393224 | tf_op jit(solution)/shard_map/ppermute | solution.py:597
  431.0 14.2 %collective-permute-start.90 = (bf16[64,1024]{1,0:T(8,128)(2,1)S(1)}, bf16[64,1024]{1,0:T(8,128)(2,1)S(1)}, u32[]{:S(2)}, u32[]{:S(2)}) collective-permute-start(bf16[64,1024]{1,0:T(8,128)(2,1)S(1)} %get-tuple-element.523.refs_0_.refs_4_), channel_id=1, source_target_pairs={{0,2},{1,3},{2,0},{3,1},{4,6},{5,7},{6,4},{7,5},{8,10},{9,11},{10,... | collective-permute-start | bytes 393224 | tf_op jit(solution)/shard_map/ppermute | solution.py:597
  432.1 16.7 %collective-permute-start.92 = (bf16[64,1024]{1,0:T(8,128)(2,1)S(1)}, bf16[64,1024]{1,0:T(8,128)(2,1)S(1)}, u32[]{:S(2)}, u32[]{:S(2)}) collective-permute-start(bf16[64,1024]{1,0:T(8,128)(2,1)S(1)} %collective-permute-done.88.refs_2_.refs_6_), channel_id=1, source_target_pairs={{0,2},{1,3},{2,0},{3,1},{4,6},{5,7},{6,4},{7,5},{8,10},{9,11},{10,... | collective-permute-start | bytes 393224 | tf_op jit(solution)/shard_map/ppermute | solution.py:597
  442.3 40.1 %collective-permute-start.100 = (bf16[128,1024]{1,0:T(8,128)(2,1)S(1)}, bf16[128,1024]{1,0:T(8,128)(2,1)S(1)}, u32[]{:S(2)}, u32[]{:S(2)}) collective-permute-start(bf16[128,1024]{1,0:T(8,128)(2,1)S(1)} %get-tuple-element.569.refs_0_.refs_8_), channel_id=1, source_target_pairs={{0,3},{1,2},{2,1},{3,0},{4,7},{5,6},{6,5},{7,4},{8,11},{9,10},{10,... | collective-permute-start | bytes 786440 | tf_op jit(solution)/shard_map/ppermute | solution.py:597
  445.2 37.2 %collective-permute-start.98 = (bf16[128,1024]{1,0:T(8,128)(2,1)S(1)}, bf16[128,1024]{1,0:T(8,128)(2,1)S(1)}, u32[]{:S(2)}, u32[]{:S(2)}) collective-permute-start(bf16[128,1024]{1,0:T(8,128)(2,1)S(1)} %get-tuple-element.569.refs_0_.refs_8_), channel_id=1, source_target_pairs={{0,1},{1,0},{2,3},{3,2},{4,5},{5,4},{6,7},{7,6},{8,9},{9,8},{10,11... | collective-permute-start | bytes 786440 | tf_op jit(solution)/shard_map/ppermute | solution.py:597
  448.8 33.6 %collective-permute-start.99 = (bf16[128,1024]{1,0:T(8,128)(2,1)S(1)}, bf16[128,1024]{1,0:T(8,128)(2,1)S(1)}, u32[]{:S(2)}, u32[]{:S(2)}) collective-permute-start(bf16[128,1024]{1,0:T(8,128)(2,1)S(1)} %get-tuple-element.569.refs_0_.refs_8_), channel_id=1, source_target_pairs={{0,2},{1,3},{2,0},{3,1},{4,6},{5,7},{6,4},{7,5},{8,10},{9,11},{10,... | collective-permute-start | bytes 786440 | tf_op jit(solution)/shard_map/ppermute | solution.py:597
  466.8 16.0 %collective-permute-start.97 = (bf16[4,128,256]{2,1,0:T(8,128)(2,1)S(1)}, bf16[4,128,256]{2,1,0:T(8,128)(2,1)S(1)}, u32[]{:S(2)}, u32[]{:S(2)}) collective-permute-start(bf16[4,128,256]{2,1,0:T(8,128)(2,1)S(1)} %bitcast.124), channel_id=1, source_target_pairs={{0,4},{1,5},{2,6},{3,7},{4,0},{5,1},{6,2},{7,3},{8,12},{9,13},{10,... | collective-permute-start | bytes 786440 | tf_op jit(solution)/shard_map/ppermute | solution.py:594
  498.9 15.5 %collective-permute-start.108 = (bf16[128,1024]{1,0:T(8,128)(2,1)S(1)}, bf16[128,1024]{1,0:T(8,128)(2,1)S(1)}, u32[]{:S(2)}, u32[]{:S(2)}) collective-permute-start(bf16[128,1024]{1,0:T(8,128)(2,1)S(1)} %copy-done.103), channel_id=1, source_target_pairs={{0,3},{1,2},{2,1},{3,0},{4,7},{5,6},{6,5},{7,4},{8,11},{9,10},{10,... | collective-permute-start | bytes 786440 | tf_op jit(solution)/shard_map/ppermute | solution.py:597
  504.4 13.7 %collective-permute-start.103 = (bf16[128,1024]{1,0:T(8,128)(2,1)S(1)}, bf16[128,1024]{1,0:T(8,128)(2,1)S(1)}, u32[]{:S(2)}, u32[]{:S(2)}) collective-permute-start(bf16[128,1024]{1,0:T(8,128)(2,1)S(1)} %get-tuple-element.541), channel_id=1, source_target_pairs={{0,1},{1,0},{2,3},{3,2},{4,5},{5,4},{6,7},{7,6},{8,9},{9,8},{10,11... | collective-permute-start | bytes 786440 | tf_op jit(solution)/shard_map/ppermute | solution.py:597
  505.4 13.9 %collective-permute-start.104 = (bf16[128,1024]{1,0:T(8,128)(2,1)S(1)}, bf16[128,1024]{1,0:T(8,128)(2,1)S(1)}, u32[]{:S(2)}, u32[]{:S(2)}) collective-permute-start(bf16[128,1024]{1,0:T(8,128)(2,1)S(1)} %get-tuple-element.542), channel_id=1, source_target_pairs={{0,2},{1,3},{2,0},{3,1},{4,6},{5,7},{6,4},{7,5},{8,10},{9,11},{10,... | collective-permute-start | bytes 786440 | tf_op jit(solution)/shard_map/ppermute | solution.py:597
  505.7 19.3 %collective-permute-start.105 = (bf16[128,1024]{1,0:T(8,128)(2,1)S(1)}, bf16[128,1024]{1,0:T(8,128)(2,1)S(1)}, u32[]{:S(2)}, u32[]{:S(2)}) collective-permute-start(bf16[128,1024]{1,0:T(8,128)(2,1)S(1)} %get-tuple-element.543), channel_id=1, source_target_pairs={{0,3},{1,2},{2,1},{3,0},{4,7},{5,6},{6,5},{7,4},{8,11},{9,10},{10,... | collective-permute-start | bytes 786440 | tf_op jit(solution)/shard_map/ppermute | solution.py:597
  535.2 35.6 %collective-permute-start.111 = (bf16[2,512,256]{2,1,0:T(8,128)(2,1)}, bf16[2,512,256]{2,1,0:T(8,128)(2,1)}, u32[]{:S(2)}, u32[]{:S(2)}) collective-permute-start(bf16[2,512,256]{2,1,0:T(8,128)(2,1)} %bitcast.122), channel_id=1, source_target_pairs={{0,4},{1,5},{2,6},{3,7},{4,0},{5,1},{6,2},{7,3},{8,12},{9,13},{10,... | collective-permute-start | bytes 1572872 | tf_op jit(solution)/shard_map/ppermute | solution.py:594
  536.4 43.9 %all-to-all-start.2 = ((bf16[32,104,128]{2,1,0:T(8,128)(2,1)}), bf16[32,104,128]{2,1,0:T(8,128)(2,1)}, u32[]{:S(2)}, u32[]{:S(2)}) async-start(bf16[32,104,128]{2,1,0:T(8,128)(2,1)} %reshape.580), calls=%async_computation.4 | async-start | bytes 1703936 | tf_op jit(solution)/shard_map/all_to_all | solution.py:689
  543.8 28.4 %collective-permute-start.110 = (bf16[2,4,128,256]{3,2,1,0:T(8,128)(2,1)}, bf16[2,4,128,256]{3,2,1,0:T(8,128)(2,1)}, u32[]{:S(2)}, u32[]{:S(2)}) collective-permute-start(bf16[2,4,128,256]{3,2,1,0:T(8,128)(2,1)} %select_convert_fusion), channel_id=1, source_target_pairs={{0,16},{8,24},{16,0},{24,8},{1,17},{9,25},{17,1},{25,9},{2,18},{10... | collective-permute-start | bytes 1572872 | tf_op jit(solution)/shard_map/ppermute | solution.py:649
  584.3 30.2 %collective-permute-start.112 = (bf16[2,4,128,256]{3,2,1,0:T(8,128)(2,1)}, bf16[2,4,128,256]{3,2,1,0:T(8,128)(2,1)}, u32[]{:S(2)}, u32[]{:S(2)}) collective-permute-start(bf16[2,4,128,256]{3,2,1,0:T(8,128)(2,1)} %pad_maximum_fusion.1), channel_id=1, source_target_pairs={{0,4},{1,5},{2,6},{3,7},{4,0},{5,1},{6,2},{7,3},{8,12},{9,13},{10,... | collective-permute-start | bytes 1572872 | tf_op jit(solution)/shard_map/ppermute | solution.py:594
  587.1 26.8 %all-to-all-start.3 = ((f32[32,1,1024]{2,1,0:T(1,128)}), f32[32,1,1024]{2,1,0:T(1,128)S(1)}, u32[]{:S(2)}, u32[]{:S(2)}) async-start(f32[32,1,1024]{2,1,0:T(1,128)} %broadcast_in_dim.86), calls=%async_computation.6 | async-start | bytes 262144 | tf_op jit(solution)/shard_map/all_to_all | solution.py:972
  (190 other events, 2224.2 us)
Sparse Core Ops, SparseCore 0:
  38.9 24.6 all-gather.20
  76.1 18.5 all-gather.22
  97.2 19.3 all-gather.24
  122.0 15.5 all-gather.12
  139.0 16.7 all-gather.14
  166.0 18.5 all-gather.26
  224.3 17.1 all-gather.16
  256.2 17.1 all-gather.18
  333.4 45.5 reduce-scatter.4
  385.3 28.7 reduce-scatter.6
  422.2 42.4 reduce-scatter.8
  495.6 29.9 reduce-scatter.10

commit v4 on v3

--- a/solution.py
+++ b/solution.py
@@ -686,8 +686,7 @@
 def to_owners(places, rows, capacity):
     owners = places.dp_size * places.tensor_size
     runs = rows.reshape(owners, capacity * rows.shape[1] // LANES, LANES)
-    moved = lax.all_to_all(runs, ("dp", "tensor"), split_axis=0, concat_axis=0, tiled=True)
-    return moved.reshape(rows.shape)
+    return lax.all_to_all(runs, ("dp", "tensor"), split_axis=0, concat_axis=0, tiled=True)
 
 
 def finish_kernel(*refs, count):
@@ -792,7 +791,7 @@
     wanted = after(wanted, moved, enc_in_share)
     found = wanted >= 0
     picked = jnp.take(embed_table, jnp.maximum(wanted, 0), axis=0, mode="clip")
-    replies = to_owners(places, picked, capacity)
+    replies = to_owners(places, picked, capacity).reshape(picked.shape)
     outs_share = jnp.concatenate([places.share(weight) for weight in (enc_out, dec_out, cross_out)])
     outs_share = places.partner(after(outs_share, picked))
     replies = after(replies, outs_share)
@@ -962,18 +961,19 @@
         gain_eemb, gain_eattn, gain_effn, gain_memory, gain_demb, gain_dattn, gain_cross, gain_dffn, gain_final
     ]
     outgoing = send_back(picks, src_grad, tgt_grad, gains, capacity)
-    arrived = to_owners(places, outgoing, capacity + 1).reshape(-1, capacity + 1, model)
+    arrived = to_owners(places, outgoing, capacity + 1)
     enc_grads = attend_grads(grad_q, grad_kv, enc_mixed, far(a1), after(grad_full, outgoing))
     enc_sum = places.sum_weights_now(enc_grads)
     enc_ffn_other = places.partner(after(enc_ffn_sum[1], outgoing))
     arrived = after(arrived, enc_sum, enc_ffn_other)
     last_other = places.partner(after(jnp.stack([dec_sum[1], enc_sum[1]]), arrived))
-    gain_sum = jnp.sum(arrived[:, capacity].astype(F32), axis=0)
+    slots = capacity * model // LANES
+    gain_sum = jnp.sum(arrived[:, slots:].astype(F32), axis=0).reshape(model)
     gain_grad = lax.all_to_all(
         jnp.broadcast_to(gain_sum[None], (arrived.shape[0], model)), ("dp", "tensor"), 0, 0, tiled=True
     )[: len(gains)]
     counts = jnp.sum(((wanted[:, None] == wanted[None, :]) & found[None, :]).astype(F32), axis=1)
-    rows = arrived[:, :capacity].reshape(-1, model).astype(F32) / jnp.maximum(counts, 1.0)[:, None]
+    rows = arrived[:, :slots].reshape(-1, model).astype(F32) / jnp.maximum(counts, 1.0)[:, None]
     target_rows = jnp.where(found, wanted, shard_rows)
     table_grad = jnp.zeros((shard_rows, model), F32).at[target_rows].add(rows, mode="drop")
 

time: 634 us -> 632 us (level)
    unnamed x259 -> x257, local copies, waits for them, and re-layouts: 35.3 us -> 35.3 us
where the time goes in v4:
time: 632 us; the launch traced here: 622 us
  waiting for transfers between devices  202 us (32%)
  starting transfers between devices  141 us (22%)
  Pallas kernels  137 us (22%)
  local copies, waits for them, and re-layouts  78.1 us (12%)
  other arithmetic  34.7 us (5%)
  between operations  16.5 us (3%)
  blocking collectives  12.5 us (2%)
    pallas_call x37, Pallas kernels, call(): pl.pallas_call(kernel, grid=grid, out_shape=out_shape, scratch_shapes=lis...  137 us
    ppermute x90, waiting for transfers between devices, mate(): lax.ppermute(value, 'tensor', [(t, t ^ offset) for t in range(self.tensor...  130 us
    ppermute x90, starting transfers between devices, mate(): lax.ppermute(value, 'tensor', [(t, t ^ offset) for t in range(self.tensor...  95.4 us
    ppermute x12, waiting for transfers between devices, partner(): lax.ppermute(value, 'tensor', [(t, t ^ self.group) for t in range(self.te...  37.1 us
    unnamed x257, local copies, waits for them, and re-layouts  35.3 us
    all_to_all x2, waiting for transfers between devices, to_owners(): lax.all_to_all(runs, ('dp', 'tensor'), split_axis=0, concat_axis=0, tiled...  28.1 us
    ppermute x12, starting transfers between devices, partner(): lax.ppermute(value, 'tensor', [(t, t ^ self.group) for t in range(self.te...  25.5 us
  transfers between devices with their start and end apart: 128, of which 60 were waited for; matrix products, arithmetic and copies ran while one was open for 12% of the time, Pallas kernels for 20%

profile of v4, /device:TPU:0, one launch (start us, length us, event | category | flops | bytes accessed | tf_op | source)
XLA Modules:
  0.0 622.1 jit_solution(7464140688606034902)
XLA Ops:
  9.6 5.4 collective-permute-start.1
  16.8 12.5 %all_to_all.22 = s32[32,1,12]{2,1,0:T(1,128)S(1)} all-to-all(s32[32,1,12]{2,1,0:T(1,128)S(1)} %bitcast.127), channel_id=1, replica_groups=mesh['dp'=4,'tensor'=8] {'dp','tensor'}, dimensions={0} | all-to-all | bytes 3072 | tf_op jit(solution)/shard_map/all_to_all | solution.py:789
  30.7 7.2 %gather_fusion = bf16[384,1024]{1,0:T(8,128)(2,1)S(1)} fusion(bf16[4096,1024]{1,0:T(8,128)(2,1)} %param.26, s32[1024]{0:T(1024)S(1)} %pad_clamp_fusion.3), kind=kCustom, calls=%fused_computation.4 | custom fusion | bytes 1574400 | tf_op jit(solution)/shard_map/jit(_take)/gather | solution.py:793
  40.0 2.8 all-to-all-start.1
  44.9 2.7 collective-permute-start.2
  47.7 21.3 %all-to-all-done.1 = bf16[32,96,128]{2,1,0:T(8,128)(2,1)S(1)} async-done(((bf16[32,96,128]{2,1,0:T(8,128)(2,1)}), bf16[32,96,128]{2,1,0:T(8,128)(2,1)S(1)}, u32[]{:S(2)}, u32[]{:S(2)}) %all-to-all-start.1) | async-done | bytes 786464 | tf_op jit(solution)/shard_map/all_to_all | solution.py:689
  69.3 2.6 collective-permute-done.2
  87.3 3.6 collective-permute-done.5.refs_4_
  92.4 2.4 project.4
  107.9 8.0 %attend.3 = (bf16[512,256]{1,0:T(8,128)(2,1)S(1)}, f32[4,512]{1,0:T(4,128)S(1)}, bf16[128,1024]{1,0:T(8,128)(2,1)S(1)}, bf16[128,1024]{1,0:T(8,128)(2,1)S(1)}, b...) custom-call(bf16[512,256]{1,0:T(8,128)(2,1)S(1)} %copy-done.26, ...), custom_call_target="tpu_custom_call" | custom-call | flops 10737418 | bytes 90152 | tf_op jit(solution)/shard_map/attend/pallas_call | solution.py:36
  117.3 4.5 collective-permute-done.11.refs_3_
  125.2 2.3 project.5
  128.3 10.1 %collective-permute-done.15 = bf16[128,1024]{1,0:T(8,128)(2,1)} collective-permute-done((bf16[128,1024]{1,0:T(8,128)(2,1)}, bf16[128,1024]{1,0:T(8,128)(2,1)}, u32[]{:S(2)}, u32[]{:S(2)}) %collective-permute-start.15) | collective-permute-done | bytes 262176 | tf_op jit(solution)/shard_map/ppermute | solution.py:594
  143.0 2.3 collective-permute-start.19
  146.0 3.5 collective-permute-start.43
  150.4 8.0 %attend.4 = (bf16[512,256]{1,0:T(8,128)(2,1)S(1)}, f32[4,512]{1,0:T(4,128)S(1)}, bf16[128,1024]{1,0:T(8,128)(2,1)S(1)}, bf16[128,1024]{1,0:T(8,128)(2,1)S(1)}, b...) custom-call(bf16[512,256]{1,0:T(8,128)(2,1)S(1)} %copy-done.28, ...), custom_call_target="tpu_custom_call" | custom-call | flops 10737418 | bytes 90152 | tf_op jit(solution)/shard_map/attend/pallas_call | solution.py:36
  159.8 4.0 collective-permute-done.19.refs_3_
  177.3 11.2 %collective-permute-done.28.refs_6_ = bf16[64,1024]{1,0:T(8,128)(2,1)S(1)} collective-permute-done((bf16[64,1024]{1,0:T(8,128)(2,1)S(1)}, bf16[64,1024]{1,0:T(8,128)(2,1)S(1)}, u32[]{:S(2)}, u32[]{:S(2)}) %collective-permute-start.28) | collective-permute-done | bytes 131104 | tf_op jit(solution)/shard_map/ppermute | solution.py:597
  196.8 5.1 ffn.2
  210.8 8.2 %collective-permute-done.35.refs_2_ = bf16[128,1024]{1,0:T(8,128)(2,1)S(1)} collective-permute-done((bf16[128,1024]{1,0:T(8,128)(2,1)S(1)}, bf16[128,1024]{1,0:T(8,128)(2,1)S(1)}, u32[]{:S(2)}, u32[]{:S(2)}) %collective-permute-start.35) | collective-permute-done | bytes 262176 | tf_op jit(solution)/shard_map/ppermute | solution.py:597
  219.0 3.4 collective-permute-done.36.refs_3_
  233.2 2.5 collective-permute-done.41.refs_6_.refs_18_
  240.8 2.4 collective-permute-start.44
  243.3 8.2 %attend.5 = (bf16[512,256]{1,0:T(8,128)(2,1)S(1)}, f32[4,512]{1,0:T(4,128)S(1)}, bf16[128,1024]{1,0:T(8,128)(2,1)S(1)}, bf16[128,1024]{1,0:T(8,128)(2,1)S(1)}, b...) custom-call(bf16[512,256]{1,0:T(8,128)(2,1)S(1)} %project.6.q_ref, bf16[512,512]{1,0:T(8,128)(2,1)S(1)} %project.7.mine_ref, ...), custom_call_target="tpu_custom_call" | custom-call | flops 10737418 | bytes 90152 | tf_op jit(solution)/shard_map/attend/pallas_call | solution.py:36
  253.2 2.8 collective-permute-done.44
  259.7 4.8 collective-permute-done.46.refs_1_
  264.5 2.3 collective-permute-done.47.refs_2_
  266.8 4.0 collective-permute-done.48.refs_3_
  284.3 5.2 ffn.3
  293.1 2.3 collective-permute-start.57
  295.5 4.2 collective-permute-done.55.refs_1_
  299.8 3.0 collective-permute-done.57.refs_3_
  315.9 5.1 ffn_back.2
  324.6 6.1 ffn_grads.2
  342.5 5.9 collective-permute-done.71.refs_6_.refs_10_
  348.4 11.5 %attend_back.3 = (bf16[512,256]{1,0:T(8,128)(2,1)S(1)}, f32[512,512]{1,0:T(8,128)S(1)}, bf16[512,512]{1,0:T(8,128)(2,1)S(1)}) custom-call(bf16[128,1024]{1,0:T(8,128)(2,1)} %wo_ref.9, bf16[4,192,1024]{2,1,0:T(8,128)(2,1)} %bitcast.101, bf16[512,256]{1,0:T(8,128)(2,1)} %copy-done.2, bf16[512,512]{1,0:T(8,128)(2,1)} %copy-done.1, bf16[512,512]{1,0:T(8,128)(2,1)} %copy-done.14, ...), custom_call_target="tpu_custom_call" | custom-call | flops 26843544 | bytes 121610 | tf_op jit(solution)/shard_map/attend_back/pallas_call | solution.py:36
  359.9 4.3 collective-permute-start.74
  364.3 2.3 unproject.1
  372.1 4.3 attend_grads.3
  377.8 5.8 collective-permute-done.77.refs_3_
  397.6 2.5 collective-permute-start.85
  401.5 5.1 ffn_back.3
  410.4 6.1 ffn_grads.3
  433.0 7.9 %collective-permute-done.91.refs_5_.refs_9_ = bf16[64,1024]{1,0:T(8,128)(2,1)S(1)} collective-permute-done((bf16[64,1024]{1,0:T(8,128)(2,1)S(1)}, bf16[64,1024]{1,0:T(8,128)(2,1)S(1)}, u32[]{:S(2)}, u32[]{:S(2)}) %collective-permute-start.91) | collective-permute-done | bytes 131104 | tf_op jit(solution)/shard_map/ppermute | solution.py:597
  442.3 2.9 collective-permute-start.100
  446.3 2.5 collective-permute-done.92.refs_6_.refs_10_
  452.6 12.2 %attend_back.4 = (bf16[512,256]{1,0:T(8,128)(2,1)S(1)}, f32[512,512]{1,0:T(8,128)S(1)}, bf16[512,512]{1,0:T(8,128)(2,1)}) custom-call(bf16[128,1024]{1,0:T(8,128)(2,1)} %wo_ref.10, bf16[4,192,1024]{2,1,0:T(8,128)(2,1)} %bitcast.102, bf16[512,256]{1,0:T(8,128)(2,1)} %copy-done.27, bf16[512,512]{1,0:T(8,128)(2,1)} %copy-done.12, bf16[512,512]{1,0:T(8,128)(2,1)} %copy-done.13, ...), custom_call_target="tpu_custom_call" | custom-call | flops 26843544 | bytes 121610 | tf_op jit(solution)/shard_map/attend_back/pallas_call | solution.py:36
  466.8 3.5 collective-permute-start.97
  473.0 2.6 unproject_keys.4
  478.5 3.9 attend_grads.4
  482.8 12.5 %attend_back.5 = (bf16[512,256]{1,0:T(8,128)(2,1)S(1)}, f32[512,512]{1,0:T(8,128)S(1)}, bf16[512,512]{1,0:T(8,128)(2,1)}) custom-call(bf16[128,1024]{1,0:T(8,128)(2,1)} %wo_ref.11, bf16[4,192,1024]{2,1,0:T(8,128)(2,1)} %bitcast.103, bf16[512,256]{1,0:T(8,128)(2,1)} %copy-done.25, bf16[512,512]{1,0:T(8,128)(2,1)} %copy-done.10, bf16[512,512]{1,0:T(8,128)(2,1)} %copy-done.11, ...), custom_call_target="tpu_custom_call" | custom-call | flops 26843544 | bytes 121610 | tf_op jit(solution)/shard_map/attend_back/pallas_call | solution.py:36
  498.9 2.8 collective-permute-start.108
  501.7 2.7 unproject_keys.5
  505.7 2.3 collective-permute-start.105
  508.7 5.7 collective-permute-done.108.refs_3_
  519.3 5.6 collective-permute-done.105.refs_3_
  527.8 2.6 attend_grads.5
  536.6 3.6 all-to-all-start.2
  549.9 21.1 %collective-permute-done.111 = bf16[2,512,256]{2,1,0:T(8,128)(2,1)} collective-permute-done((bf16[2,512,256]{2,1,0:T(8,128)(2,1)}, bf16[2,512,256]{2,1,0:T(8,128)(2,1)}, u32[]{:S(2)}, u32[]{:S(2)}) %collective-permute-start.111) | collective-permute-done | bytes 524320 | tf_op jit(solution)/shard_map/ppermute | solution.py:594
  573.6 6.8 %all-to-all-done.2 = bf16[32,104,128]{2,1,0:T(8,128)(2,1)} async-done(((bf16[32,104,128]{2,1,0:T(8,128)(2,1)}), bf16[32,104,128]{2,1,0:T(8,128)(2,1)}, u32[]{:S(2)}, u32[]{:S(2)}) %all-to-all-start.2) | async-done | bytes 852000 | tf_op jit(solution)/shard_map/all_to_all | solution.py:689
  585.8 4.2 all-to-all-start.3
  590.0 2.5 slice_convert_fusion
  594.0 11.0 %scatter_custom_fusion = f32[4096,1024]{1,0:T(8,128)} fusion(s32[384]{0:T(512)S(1)} %get-tuple-element.694, f32[]{:T(128)} %constant.136.clone.1, f32[384,1024]{1,0:T(8,128)S(1)} %reshape.588, f32[384]{0:T(512)S(1)} %broadcast_maximum_fusion), kind=kCustom, calls=%fused_computation.7 | custom fusion | flops 786432 | bytes 18352132 | tf_op jit(solution)/shard_map/scatter-add | solution.py:978
  605.0 6.9 %all-to-all-done.3 = f32[32,1,1024]{2,1,0:T(1,128)S(1)} async-done(((f32[32,1,1024]{2,1,0:T(1,128)}), f32[32,1,1024]{2,1,0:T(1,128)S(1)}, u32[]{:S(2)}, u32[]{:S(2)}) %all-to-all-start.3) | async-done | bytes 131104 | tf_op jit(solution)/shard_map/all_to_all | solution.py:972
  (599 shorter events, 247.9 us)
Async XLA Ops:
  7.2 85.2 %all-gather.21.cloned.1.call-start = ((), (), s32[]{:S(2)}) async-start(), calls=%async_computation.16 | async-start | bytes 1966080 | tf_op jit(solution)/shard_map/all_gather | solution.py:623
  7.9 22.8 %collective-permute-start = (s32[2304]{0:T(1024)S(1)}, s32[2304]{0:T(1024)S(1)}, u32[]{:S(2)}, u32[]{:S(2)}) collective-permute-start(s32[2304]{0:T(1024)S(1)} %pad_add_fusion), channel_id=1, source_target_pairs={{0,0},{1,1},{2,2},{3,3},{4,8},{5,9},{6,10},{7,11},{8,4},{9,5},{10,... | collective-permute-start | bytes 27656 | tf_op jit(solution)/shard_map/ppermute | solution.py:588
  9.6 21.1 %collective-permute-start.1 = (bf16[3,256,128]{2,1,0:T(8,128)(2,1)S(1)}, bf16[3,256,128]{2,1,0:T(8,128)(2,1)S(1)}, u32[]{:S(2)}, u32[]{:S(2)}) collective-permute-start(bf16[3,256,128]{2,1,0:T(8,128)(2,1)S(1)} %constant_dynamic-slice_fusion.8), channel_id=1, source_target_pairs={{0,4},{1,5},{2,6},{3,7},{4,0},{5,1},{6,2},{7,3},{8,12},{9,13},{10,... | collective-permute-start | bytes 589832 | tf_op jit(solution)/shard_map/ppermute | solution.py:594
  40.0 29.0 %all-to-all-start.1 = ((bf16[32,96,128]{2,1,0:T(8,128)(2,1)}), bf16[32,96,128]{2,1,0:T(8,128)(2,1)S(1)}, u32[]{:S(2)}, u32[]{:S(2)}) async-start(bf16[32,96,128]{2,1,0:T(8,128)(2,1)} %reshape.577), calls=%async_computation.1 | async-start | bytes 1572864 | tf_op jit(solution)/shard_map/all_to_all | solution.py:689
  42.8 64.0 %all-gather.23.cloned.1.call-start = ((), (), s32[]{:S(2)}) async-start(), calls=%async_computation.17 | async-start | bytes 1966080 | tf_op jit(solution)/shard_map/all_gather | solution.py:623
  44.9 27.0 %collective-permute-start.2 = (bf16[96,1024]{1,0:T(8,128)(2,1)S(1)}, bf16[96,1024]{1,0:T(8,128)(2,1)}, u32[]{:S(2)}, u32[]{:S(2)}) collective-permute-start(bf16[96,1024]{1,0:T(8,128)(2,1)S(1)} %pad_maximum_fusion.6), channel_id=1, source_target_pairs={{0,4},{1,5},{2,6},{3,7},{4,0},{5,1},{6,2},{7,3},{8,12},{9,13},{10,... | collective-permute-start | bytes 589832 | tf_op jit(solution)/shard_map/ppermute | solution.py:594
  76.0 49.2 %all-gather.25.cloned.1.call-start = ((), (), s32[]{:S(2)}) async-start(), calls=%async_computation.18 | async-start | bytes 1966080 | tf_op jit(solution)/shard_map/all_gather | solution.py:623
  79.2 15.7 %collective-permute-start.14 = (bf16[3,256,128]{2,1,0:T(8,128)(2,1)}, bf16[3,256,128]{2,1,0:T(8,128)(2,1)}, u32[]{:S(2)}, u32[]{:S(2)}) collective-permute-start(bf16[3,256,128]{2,1,0:T(8,128)(2,1)} %constant_dynamic-slice_fusion.3), channel_id=1, source_target_pairs={{0,4},{1,5},{2,6},{3,7},{4,0},{5,1},{6,2},{7,3},{8,12},{9,13},{10,... | collective-permute-start | bytes 589832 | tf_op jit(solution)/shard_map/ppermute | solution.py:594
  97.1 97.0 %all-gather.13.cloned.1.call-start = ((), (), s32[]{:S(2)}) async-start(), calls=%async_computation.8 | async-start | bytes 1310720 | tf_op jit(solution)/shard_map/all_gather | solution.py:626
  101.5 15.8 %collective-permute-start.10 = (bf16[128,1024]{1,0:T(8,128)(2,1)S(1)}, bf16[128,1024]{1,0:T(8,128)(2,1)S(1)}, u32[]{:S(2)}, u32[]{:S(2)}) collective-permute-start(bf16[128,1024]{1,0:T(8,128)(2,1)S(1)} %get-tuple-element.321.refs_0_), channel_id=1, source_target_pairs={{0,2},{1,3},{2,0},{3,1},{4,6},{5,7},{6,4},{7,5},{8,10},{9,11},{10,... | collective-permute-start | bytes 786440 | tf_op jit(solution)/shard_map/ppermute | solution.py:597
  102.4 19.4 %collective-permute-start.11 = (bf16[128,1024]{1,0:T(8,128)(2,1)S(1)}, bf16[128,1024]{1,0:T(8,128)(2,1)S(1)}, u32[]{:S(2)}, u32[]{:S(2)}) collective-permute-start(bf16[128,1024]{1,0:T(8,128)(2,1)S(1)} %get-tuple-element.321.refs_0_), channel_id=1, source_target_pairs={{0,3},{1,2},{2,1},{3,0},{4,7},{5,6},{6,5},{7,4},{8,11},{9,10},{10,... | collective-permute-start | bytes 786440 | tf_op jit(solution)/shard_map/ppermute | solution.py:597
  103.9 17.9 %collective-permute-start.9 = (bf16[128,1024]{1,0:T(8,128)(2,1)S(1)}, bf16[128,1024]{1,0:T(8,128)(2,1)S(1)}, u32[]{:S(2)}, u32[]{:S(2)}) collective-permute-start(bf16[128,1024]{1,0:T(8,128)(2,1)S(1)} %get-tuple-element.321.refs_0_), channel_id=1, source_target_pairs={{0,1},{1,0},{2,3},{3,2},{4,5},{5,4},{6,7},{7,6},{8,9},{9,8},{10,11... | collective-permute-start | bytes 786440 | tf_op jit(solution)/shard_map/ppermute | solution.py:597
  105.1 16.8 %collective-permute-start.13 = (bf16[256,512]{1,0:T(8,128)(2,1)}, bf16[256,512]{1,0:T(8,128)(2,1)}, u32[]{:S(2)}, u32[]{:S(2)}) collective-permute-start(bf16[256,512]{1,0:T(8,128)(2,1)} %constant_dynamic-slice_fusion.4), channel_id=1, source_target_pairs={{0,4},{1,5},{2,6},{3,7},{4,0},{5,1},{6,2},{7,3},{8,12},{9,13},{10,... | collective-permute-start | bytes 786440 | tf_op jit(solution)/shard_map/ppermute | solution.py:594
  121.9 72.2 %all-gather.15.cloned.1.call-start = ((), (), s32[]{:S(2)}) async-start(), calls=%async_computation.9 | async-start | bytes 1310720 | tf_op jit(solution)/shard_map/all_gather | solution.py:626
  123.7 14.8 %collective-permute-start.15 = (bf16[128,1024]{1,0:T(8,128)(2,1)}, bf16[128,1024]{1,0:T(8,128)(2,1)}, u32[]{:S(2)}, u32[]{:S(2)}) collective-permute-start(bf16[128,1024]{1,0:T(8,128)(2,1)} %constant_dynamic-slice_fusion.2), channel_id=1, source_target_pairs={{0,4},{1,5},{2,6},{3,7},{4,0},{5,1},{6,2},{7,3},{8,12},{9,13},{10,... | collective-permute-start | bytes 786440 | tf_op jit(solution)/shard_map/ppermute | solution.py:594
  138.4 93.1 %all-gather.27.cloned.1.call-start = ((), (), s32[]{:S(2)}) async-start(), calls=%async_computation.19 | async-start | bytes 1966080 | tf_op jit(solution)/shard_map/all_gather | solution.py:623
  141.7 18.1 %collective-permute-start.17 = (bf16[128,1024]{1,0:T(8,128)(2,1)}, bf16[128,1024]{1,0:T(8,128)(2,1)S(1)}, u32[]{:S(2)}, u32[]{:S(2)}) collective-permute-start(bf16[128,1024]{1,0:T(8,128)(2,1)} %copy-done.110), channel_id=1, source_target_pairs={{0,1},{1,0},{2,3},{3,2},{4,5},{5,4},{6,7},{7,6},{8,9},{9,8},{10,11... | collective-permute-start | bytes 786440 | tf_op jit(solution)/shard_map/ppermute | solution.py:597
  143.0 16.8 %collective-permute-start.18 = (bf16[128,1024]{1,0:T(8,128)(2,1)}, bf16[128,1024]{1,0:T(8,128)(2,1)S(1)}, u32[]{:S(2)}, u32[]{:S(2)}) collective-permute-start(bf16[128,1024]{1,0:T(8,128)(2,1)} %copy-done.107), channel_id=1, source_target_pairs={{0,2},{1,3},{2,0},{3,1},{4,6},{5,7},{6,4},{7,5},{8,10},{9,11},{10,... | collective-permute-start | bytes 786440 | tf_op jit(solution)/shard_map/ppermute | solution.py:597
  143.0 20.8 %collective-permute-start.19 = (bf16[128,1024]{1,0:T(8,128)(2,1)}, bf16[128,1024]{1,0:T(8,128)(2,1)S(1)}, u32[]{:S(2)}, u32[]{:S(2)}) collective-permute-start(bf16[128,1024]{1,0:T(8,128)(2,1)} %copy-done.106), channel_id=1, source_target_pairs={{0,3},{1,2},{2,1},{3,0},{4,7},{5,6},{6,5},{7,4},{8,11},{9,10},{10,... | collective-permute-start | bytes 786440 | tf_op jit(solution)/shard_map/ppermute | solution.py:597
  145.3 18.6 %collective-permute-start.20 = (bf16[128,1024]{1,0:T(8,128)(2,1)S(1)}, bf16[128,1024]{1,0:T(8,128)(2,1)S(1)}, u32[]{:S(2)}, u32[]{:S(2)}) collective-permute-start(bf16[128,1024]{1,0:T(8,128)(2,1)S(1)} %bitcast.124), channel_id=1, source_target_pairs={{0,0},{1,1},{2,2},{3,3},{4,8},{5,9},{6,10},{7,11},{8,4},{9,5},{10,... | collective-permute-start | bytes 786440 | tf_op jit(solution)/shard_map/ppermute | solution.py:588
  146.0 19.0 %collective-permute-start.43 = (bf16[3,256,128]{2,1,0:T(8,128)(2,1)S(1)}, bf16[3,256,128]{2,1,0:T(8,128)(2,1)S(1)}, u32[]{:S(2)}, u32[]{:S(2)}) collective-permute-start(bf16[3,256,128]{2,1,0:T(8,128)(2,1)S(1)} %pad_maximum_fusion.7), channel_id=1, source_target_pairs={{0,4},{1,5},{2,6},{3,7},{4,0},{5,1},{6,2},{7,3},{8,12},{9,13},{10,... | collective-permute-start | bytes 589832 | tf_op jit(solution)/shard_map/ppermute | solution.py:594
  165.9 113.7 %all-gather.17.cloned.1.call-start = ((), (), s32[]{:S(2)}) async-start(), calls=%async_computation.10 | async-start | bytes 1310720 | tf_op jit(solution)/shard_map/all_gather | solution.py:626
  170.0 19.1 %collective-permute-start.21 = (bf16[128,1024]{1,0:T(8,128)(2,1)}, bf16[128,1024]{1,0:T(8,128)(2,1)S(1)}, u32[]{:S(2)}, u32[]{:S(2)}) collective-permute-start(bf16[128,1024]{1,0:T(8,128)(2,1)} %copy-done.113), channel_id=1, source_target_pairs={{0,1},{1,0},{2,3},{3,2},{4,5},{5,4},{6,7},{7,6},{8,9},{9,8},{10,11... | collective-permute-start | bytes 786440 | tf_op jit(solution)/shard_map/ppermute | solution.py:597
  172.4 16.7 %collective-permute-start.22 = (bf16[128,1024]{1,0:T(8,128)(2,1)}, bf16[128,1024]{1,0:T(8,128)(2,1)S(1)}, u32[]{:S(2)}, u32[]{:S(2)}) collective-permute-start(bf16[128,1024]{1,0:T(8,128)(2,1)} %copy-done.112), channel_id=1, source_target_pairs={{0,2},{1,3},{2,0},{3,1},{4,6},{5,7},{6,4},{7,5},{8,10},{9,11},{10,... | collective-permute-start | bytes 786440 | tf_op jit(solution)/shard_map/ppermute | solution.py:597
  173.5 15.6 %collective-permute-start.23 = (bf16[128,1024]{1,0:T(8,128)(2,1)}, bf16[128,1024]{1,0:T(8,128)(2,1)S(1)}, u32[]{:S(2)}, u32[]{:S(2)}) collective-permute-start(bf16[128,1024]{1,0:T(8,128)(2,1)} %copy-done.111), channel_id=1, source_target_pairs={{0,3},{1,2},{2,1},{3,0},{4,7},{5,6},{6,5},{7,4},{8,11},{9,10},{10,... | collective-permute-start | bytes 786440 | tf_op jit(solution)/shard_map/ppermute | solution.py:597
  175.2 13.2 %collective-permute-start.28 = (bf16[64,1024]{1,0:T(8,128)(2,1)S(1)}, bf16[64,1024]{1,0:T(8,128)(2,1)S(1)}, u32[]{:S(2)}, u32[]{:S(2)}) collective-permute-start(bf16[64,1024]{1,0:T(8,128)(2,1)S(1)} %collective-permute-done.24.refs_2_), channel_id=1, source_target_pairs={{0,2},{1,3},{2,0},{3,1},{4,6},{5,7},{6,4},{7,5},{8,10},{9,11},{10,... | collective-permute-start | bytes 393224 | tf_op jit(solution)/shard_map/ppermute | solution.py:597
  176.3 12.1 %collective-permute-start.29 = (bf16[64,1024]{1,0:T(8,128)(2,1)S(1)}, bf16[64,1024]{1,0:T(8,128)(2,1)S(1)}, u32[]{:S(2)}, u32[]{:S(2)}) collective-permute-start(bf16[64,1024]{1,0:T(8,128)(2,1)S(1)} %collective-permute-done.27.refs_5_), channel_id=1, source_target_pairs={{0,1},{1,0},{2,3},{3,2},{4,5},{5,4},{6,7},{7,6},{8,9},{9,8},{10,11... | collective-permute-start | bytes 393224 | tf_op jit(solution)/shard_map/ppermute | solution.py:597
  189.5 14.8 %collective-permute-start.31 = (bf16[128,1024]{1,0:T(8,128)(2,1)S(1)}, bf16[128,1024]{1,0:T(8,128)(2,1)S(1)}, u32[]{:S(2)}, u32[]{:S(2)}) collective-permute-start(bf16[128,1024]{1,0:T(8,128)(2,1)S(1)} %get-tuple-element.375.refs_0_), channel_id=1, source_target_pairs={{0,1},{1,0},{2,3},{3,2},{4,5},{5,4},{6,7},{7,6},{8,9},{9,8},{10,11... | collective-permute-start | bytes 786440 | tf_op jit(solution)/shard_map/ppermute | solution.py:597
  190.6 13.8 %collective-permute-start.32 = (bf16[128,1024]{1,0:T(8,128)(2,1)S(1)}, bf16[128,1024]{1,0:T(8,128)(2,1)S(1)}, u32[]{:S(2)}, u32[]{:S(2)}) collective-permute-start(bf16[128,1024]{1,0:T(8,128)(2,1)S(1)} %get-tuple-element.375.refs_0_), channel_id=1, source_target_pairs={{0,2},{1,3},{2,0},{3,1},{4,6},{5,7},{6,4},{7,5},{8,10},{9,11},{10,... | collective-permute-start | bytes 786440 | tf_op jit(solution)/shard_map/ppermute | solution.py:597
  191.0 13.3 %collective-permute-start.33 = (bf16[128,1024]{1,0:T(8,128)(2,1)S(1)}, bf16[128,1024]{1,0:T(8,128)(2,1)S(1)}, u32[]{:S(2)}, u32[]{:S(2)}) collective-permute-start(bf16[128,1024]{1,0:T(8,128)(2,1)S(1)} %get-tuple-element.375.refs_0_), channel_id=1, source_target_pairs={{0,3},{1,2},{2,1},{3,0},{4,7},{5,6},{6,5},{7,4},{8,11},{9,10},{10,... | collective-permute-start | bytes 786440 | tf_op jit(solution)/shard_map/ppermute | solution.py:597
  205.4 13.6 %collective-permute-start.35 = (bf16[128,1024]{1,0:T(8,128)(2,1)S(1)}, bf16[128,1024]{1,0:T(8,128)(2,1)S(1)}, u32[]{:S(2)}, u32[]{:S(2)}) collective-permute-start(bf16[128,1024]{1,0:T(8,128)(2,1)S(1)} %get-tuple-element.370), channel_id=1, source_target_pairs={{0,2},{1,3},{2,0},{3,1},{4,6},{5,7},{6,4},{7,5},{8,10},{9,11},{10,... | collective-permute-start | bytes 786440 | tf_op jit(solution)/shard_map/ppermute | solution.py:597
  205.9 16.5 %collective-permute-start.36 = (bf16[128,1024]{1,0:T(8,128)(2,1)S(1)}, bf16[128,1024]{1,0:T(8,128)(2,1)S(1)}, u32[]{:S(2)}, u32[]{:S(2)}) collective-permute-start(bf16[128,1024]{1,0:T(8,128)(2,1)S(1)} %get-tuple-element.371), channel_id=1, source_target_pairs={{0,3},{1,2},{2,1},{3,0},{4,7},{5,6},{6,5},{7,4},{8,11},{9,10},{10,... | collective-permute-start | bytes 786440 | tf_op jit(solution)/shard_map/ppermute | solution.py:597
  207.9 15.6 %collective-permute-start.30 = (bf16[256,512]{1,0:T(8,128)(2,1)S(1)}, bf16[256,512]{1,0:T(8,128)(2,1)S(1)}, u32[]{:S(2)}, u32[]{:S(2)}) collective-permute-start(bf16[256,512]{1,0:T(8,128)(2,1)S(1)} %constant_dynamic-slice_fusion.11), channel_id=1, source_target_pairs={{0,4},{1,5},{2,6},{3,7},{4,0},{5,1},{6,2},{7,3},{8,12},{9,13},{10,... | collective-permute-start | bytes 786440 | tf_op jit(solution)/shard_map/ppermute | solution.py:594
  224.2 60.0 %all-gather.19.cloned.1.call-start = ((), (), s32[]{:S(2)}) async-start(), calls=%async_computation.11 | async-start | bytes 1310720 | tf_op jit(solution)/shard_map/all_gather | solution.py:626
  240.8 15.2 %collective-permute-start.44 = (bf16[128,1024]{1,0:T(8,128)(2,1)S(1)}, bf16[128,1024]{1,0:T(8,128)(2,1)}, u32[]{:S(2)}, u32[]{:S(2)}) collective-permute-start(bf16[128,1024]{1,0:T(8,128)(2,1)S(1)} %constant_dynamic-slice_fusion.1), channel_id=1, source_target_pairs={{0,4},{1,5},{2,6},{3,7},{4,0},{5,1},{6,2},{7,3},{8,12},{9,13},{10,... | collective-permute-start | bytes 786440 | tf_op jit(solution)/shard_map/ppermute | solution.py:594
  256.1 167.0 %reduce-scatter.5.cloned.1.call-start = ((), (), s32[]{:S(2)}) async-start(), calls=%async_computation.12 | async-start | bytes 5242880 | tf_op jit(solution)/shard_map/reduce_scatter | solution.py:630
  257.6 13.2 %collective-permute-start.48 = (bf16[128,1024]{1,0:T(8,128)(2,1)S(1)}, bf16[128,1024]{1,0:T(8,128)(2,1)S(1)}, u32[]{:S(2)}, u32[]{:S(2)}) collective-permute-start(bf16[128,1024]{1,0:T(8,128)(2,1)S(1)} %get-tuple-element.393), channel_id=1, source_target_pairs={{0,3},{1,2},{2,1},{3,0},{4,7},{5,6},{6,5},{7,4},{8,11},{9,10},{10,... | collective-permute-start | bytes 786440 | tf_op jit(solution)/shard_map/ppermute | solution.py:597
  333.3 131.7 %reduce-scatter.7.cloned.1.call-start = ((), (), s32[]{:S(2)}) async-start(), calls=%async_computation.13 | async-start | bytes 2621440 | tf_op jit(solution)/shard_map/reduce_scatter | solution.py:630
  370.1 13.6 %collective-permute-start.77 = (bf16[128,1024]{1,0:T(8,128)(2,1)S(1)}, bf16[128,1024]{1,0:T(8,128)(2,1)S(1)}, u32[]{:S(2)}, u32[]{:S(2)}) collective-permute-start(bf16[128,1024]{1,0:T(8,128)(2,1)S(1)} %get-tuple-element.451), channel_id=1, source_target_pairs={{0,3},{1,2},{2,1},{3,0},{4,7},{5,6},{6,5},{7,4},{8,11},{9,10},{10,... | collective-permute-start | bytes 786440 | tf_op jit(solution)/shard_map/ppermute | solution.py:597
  385.2 146.5 %reduce-scatter.9.cloned.1.call-start = ((), (), s32[]{:S(2)}) async-start(), calls=%async_computation.14 | async-start | bytes 5242880 | tf_op jit(solution)/shard_map/reduce_scatter | solution.py:630
  397.6 11.9 %collective-permute-start.85 = (bf16[128,1024]{1,0:T(8,128)(2,1)}, bf16[128,1024]{1,0:T(8,128)(2,1)S(1)}, u32[]{:S(2)}, u32[]{:S(2)}) collective-permute-start(bf16[128,1024]{1,0:T(8,128)(2,1)} %get-tuple-element.471), channel_id=1, source_target_pairs={{0,1},{1,0},{2,3},{3,2},{4,5},{5,4},{6,7},{7,6},{8,9},{9,8},{10,11... | collective-permute-start | bytes 786440 | tf_op jit(solution)/shard_map/ppermute | solution.py:597
  400.0 16.4 %collective-permute-start.86 = (bf16[128,1024]{1,0:T(8,128)(2,1)}, bf16[128,1024]{1,0:T(8,128)(2,1)S(1)}, u32[]{:S(2)}, u32[]{:S(2)}) collective-permute-start(bf16[128,1024]{1,0:T(8,128)(2,1)} %get-tuple-element.472), channel_id=1, source_target_pairs={{0,2},{1,3},{2,0},{3,1},{4,6},{5,7},{6,4},{7,5},{8,10},{9,11},{10,... | collective-permute-start | bytes 786440 | tf_op jit(solution)/shard_map/ppermute | solution.py:597
  400.0 16.4 %collective-permute-start.87 = (bf16[128,1024]{1,0:T(8,128)(2,1)}, bf16[128,1024]{1,0:T(8,128)(2,1)S(1)}, u32[]{:S(2)}, u32[]{:S(2)}) collective-permute-start(bf16[128,1024]{1,0:T(8,128)(2,1)} %get-tuple-element.473), channel_id=1, source_target_pairs={{0,3},{1,2},{2,1},{3,0},{4,7},{5,6},{6,5},{7,4},{8,11},{9,10},{10,... | collective-permute-start | bytes 786440 | tf_op jit(solution)/shard_map/ppermute | solution.py:597
  406.6 12.3 %collective-permute-start.94 = (bf16[128,1024]{1,0:T(8,128)(2,1)S(1)}, bf16[128,1024]{1,0:T(8,128)(2,1)S(1)}, u32[]{:S(2)}, u32[]{:S(2)}) collective-permute-start(bf16[128,1024]{1,0:T(8,128)(2,1)S(1)} %get-tuple-element.478), channel_id=1, source_target_pairs={{0,1},{1,0},{2,3},{3,2},{4,5},{5,4},{6,7},{7,6},{8,9},{9,8},{10,11... | collective-permute-start | bytes 786440 | tf_op jit(solution)/shard_map/ppermute | solution.py:597
  409.5 11.0 %collective-permute-start.96 = (bf16[128,1024]{1,0:T(8,128)(2,1)S(1)}, bf16[128,1024]{1,0:T(8,128)(2,1)S(1)}, u32[]{:S(2)}, u32[]{:S(2)}) collective-permute-start(bf16[128,1024]{1,0:T(8,128)(2,1)S(1)} %get-tuple-element.480), channel_id=1, source_target_pairs={{0,3},{1,2},{2,1},{3,0},{4,7},{5,6},{6,5},{7,4},{8,11},{9,10},{10,... | collective-permute-start | bytes 786440 | tf_op jit(solution)/shard_map/ppermute | solution.py:597
  422.0 158.4 %reduce-scatter.11.cloned.1.call-start = ((), (), s32[]{:S(2)}) async-start(), calls=%async_computation.15 | async-start | bytes 2621440 | tf_op jit(solution)/shard_map/reduce_scatter | solution.py:630
  425.2 23.9 %collective-permute-start.84 = (bf16[2,512,256]{2,1,0:T(8,128)(2,1)S(1)}, bf16[2,512,256]{2,1,0:T(8,128)(2,1)S(1)}, u32[]{:S(2)}, u32[]{:S(2)}) collective-permute-start(bf16[2,512,256]{2,1,0:T(8,128)(2,1)S(1)} %bitcast.122), channel_id=1, source_target_pairs={{0,4},{1,5},{2,6},{3,7},{4,0},{5,1},{6,2},{7,3},{8,12},{9,13},{10,... | collective-permute-start | bytes 1572872 | tf_op jit(solution)/shard_map/ppermute | solution.py:594
  427.0 14.0 %collective-permute-start.91 = (bf16[64,1024]{1,0:T(8,128)(2,1)S(1)}, bf16[64,1024]{1,0:T(8,128)(2,1)S(1)}, u32[]{:S(2)}, u32[]{:S(2)}) collective-permute-start(bf16[64,1024]{1,0:T(8,128)(2,1)S(1)} %get-tuple-element.524.refs_1_.refs_5_), channel_id=1, source_target_pairs={{0,2},{1,3},{2,0},{3,1},{4,6},{5,7},{6,4},{7,5},{8,10},{9,11},{10,... | collective-permute-start | bytes 393224 | tf_op jit(solution)/shard_map/ppermute | solution.py:597
  429.5 12.8 %collective-permute-start.89 = (bf16[64,1024]{1,0:T(8,128)(2,1)S(1)}, bf16[64,1024]{1,0:T(8,128)(2,1)S(1)}, u32[]{:S(2)}, u32[]{:S(2)}) collective-permute-start(bf16[64,1024]{1,0:T(8,128)(2,1)S(1)} %get-tuple-element.524.refs_1_.refs_5_), channel_id=1, source_target_pairs={{0,1},{1,0},{2,3},{3,2},{4,5},{5,4},{6,7},{7,6},{8,9},{9,8},{10,11... | collective-permute-start | bytes 393224 | tf_op jit(solution)/shard_map/ppermute | solution.py:597
  431.0 14.2 %collective-permute-start.90 = (bf16[64,1024]{1,0:T(8,128)(2,1)S(1)}, bf16[64,1024]{1,0:T(8,128)(2,1)S(1)}, u32[]{:S(2)}, u32[]{:S(2)}) collective-permute-start(bf16[64,1024]{1,0:T(8,128)(2,1)S(1)} %get-tuple-element.523.refs_0_.refs_4_), channel_id=1, source_target_pairs={{0,2},{1,3},{2,0},{3,1},{4,6},{5,7},{6,4},{7,5},{8,10},{9,11},{10,... | collective-permute-start | bytes 393224 | tf_op jit(solution)/shard_map/ppermute | solution.py:597
  432.1 16.7 %collective-permute-start.92 = (bf16[64,1024]{1,0:T(8,128)(2,1)S(1)}, bf16[64,1024]{1,0:T(8,128)(2,1)S(1)}, u32[]{:S(2)}, u32[]{:S(2)}) collective-permute-start(bf16[64,1024]{1,0:T(8,128)(2,1)S(1)} %collective-permute-done.88.refs_2_.refs_6_), channel_id=1, source_target_pairs={{0,2},{1,3},{2,0},{3,1},{4,6},{5,7},{6,4},{7,5},{8,10},{9,11},{10,... | collective-permute-start | bytes 393224 | tf_op jit(solution)/shard_map/ppermute | solution.py:597
  442.3 40.2 %collective-permute-start.100 = (bf16[128,1024]{1,0:T(8,128)(2,1)S(1)}, bf16[128,1024]{1,0:T(8,128)(2,1)S(1)}, u32[]{:S(2)}, u32[]{:S(2)}) collective-permute-start(bf16[128,1024]{1,0:T(8,128)(2,1)S(1)} %get-tuple-element.569.refs_0_.refs_8_), channel_id=1, source_target_pairs={{0,3},{1,2},{2,1},{3,0},{4,7},{5,6},{6,5},{7,4},{8,11},{9,10},{10,... | collective-permute-start | bytes 786440 | tf_op jit(solution)/shard_map/ppermute | solution.py:597
  445.2 37.3 %collective-permute-start.98 = (bf16[128,1024]{1,0:T(8,128)(2,1)S(1)}, bf16[128,1024]{1,0:T(8,128)(2,1)S(1)}, u32[]{:S(2)}, u32[]{:S(2)}) collective-permute-start(bf16[128,1024]{1,0:T(8,128)(2,1)S(1)} %get-tuple-element.569.refs_0_.refs_8_), channel_id=1, source_target_pairs={{0,1},{1,0},{2,3},{3,2},{4,5},{5,4},{6,7},{7,6},{8,9},{9,8},{10,11... | collective-permute-start | bytes 786440 | tf_op jit(solution)/shard_map/ppermute | solution.py:597
  448.8 33.6 %collective-permute-start.99 = (bf16[128,1024]{1,0:T(8,128)(2,1)S(1)}, bf16[128,1024]{1,0:T(8,128)(2,1)S(1)}, u32[]{:S(2)}, u32[]{:S(2)}) collective-permute-start(bf16[128,1024]{1,0:T(8,128)(2,1)S(1)} %get-tuple-element.569.refs_0_.refs_8_), channel_id=1, source_target_pairs={{0,2},{1,3},{2,0},{3,1},{4,6},{5,7},{6,4},{7,5},{8,10},{9,11},{10,... | collective-permute-start | bytes 786440 | tf_op jit(solution)/shard_map/ppermute | solution.py:597
  466.8 16.0 %collective-permute-start.97 = (bf16[4,128,256]{2,1,0:T(8,128)(2,1)S(1)}, bf16[4,128,256]{2,1,0:T(8,128)(2,1)S(1)}, u32[]{:S(2)}, u32[]{:S(2)}) collective-permute-start(bf16[4,128,256]{2,1,0:T(8,128)(2,1)S(1)} %bitcast.125), channel_id=1, source_target_pairs={{0,4},{1,5},{2,6},{3,7},{4,0},{5,1},{6,2},{7,3},{8,12},{9,13},{10,... | collective-permute-start | bytes 786440 | tf_op jit(solution)/shard_map/ppermute | solution.py:594
  498.9 15.5 %collective-permute-start.108 = (bf16[128,1024]{1,0:T(8,128)(2,1)S(1)}, bf16[128,1024]{1,0:T(8,128)(2,1)S(1)}, u32[]{:S(2)}, u32[]{:S(2)}) collective-permute-start(bf16[128,1024]{1,0:T(8,128)(2,1)S(1)} %copy-done.103), channel_id=1, source_target_pairs={{0,3},{1,2},{2,1},{3,0},{4,7},{5,6},{6,5},{7,4},{8,11},{9,10},{10,... | collective-permute-start | bytes 786440 | tf_op jit(solution)/shard_map/ppermute | solution.py:597
  504.4 13.7 %collective-permute-start.103 = (bf16[128,1024]{1,0:T(8,128)(2,1)S(1)}, bf16[128,1024]{1,0:T(8,128)(2,1)S(1)}, u32[]{:S(2)}, u32[]{:S(2)}) collective-permute-start(bf16[128,1024]{1,0:T(8,128)(2,1)S(1)} %get-tuple-element.541), channel_id=1, source_target_pairs={{0,1},{1,0},{2,3},{3,2},{4,5},{5,4},{6,7},{7,6},{8,9},{9,8},{10,11... | collective-permute-start | bytes 786440 | tf_op jit(solution)/shard_map/ppermute | solution.py:597
  505.4 13.9 %collective-permute-start.104 = (bf16[128,1024]{1,0:T(8,128)(2,1)S(1)}, bf16[128,1024]{1,0:T(8,128)(2,1)S(1)}, u32[]{:S(2)}, u32[]{:S(2)}) collective-permute-start(bf16[128,1024]{1,0:T(8,128)(2,1)S(1)} %get-tuple-element.542), channel_id=1, source_target_pairs={{0,2},{1,3},{2,0},{3,1},{4,6},{5,7},{6,4},{7,5},{8,10},{9,11},{10,... | collective-permute-start | bytes 786440 | tf_op jit(solution)/shard_map/ppermute | solution.py:597
  505.7 19.3 %collective-permute-start.105 = (bf16[128,1024]{1,0:T(8,128)(2,1)S(1)}, bf16[128,1024]{1,0:T(8,128)(2,1)S(1)}, u32[]{:S(2)}, u32[]{:S(2)}) collective-permute-start(bf16[128,1024]{1,0:T(8,128)(2,1)S(1)} %get-tuple-element.543), channel_id=1, source_target_pairs={{0,3},{1,2},{2,1},{3,0},{4,7},{5,6},{6,5},{7,4},{8,11},{9,10},{10,... | collective-permute-start | bytes 786440 | tf_op jit(solution)/shard_map/ppermute | solution.py:597
  535.4 35.7 %collective-permute-start.111 = (bf16[2,512,256]{2,1,0:T(8,128)(2,1)}, bf16[2,512,256]{2,1,0:T(8,128)(2,1)}, u32[]{:S(2)}, u32[]{:S(2)}) collective-permute-start(bf16[2,512,256]{2,1,0:T(8,128)(2,1)} %bitcast.123), channel_id=1, source_target_pairs={{0,4},{1,5},{2,6},{3,7},{4,0},{5,1},{6,2},{7,3},{8,12},{9,13},{10,... | collective-permute-start | bytes 1572872 | tf_op jit(solution)/shard_map/ppermute | solution.py:594
  536.6 43.8 %all-to-all-start.2 = ((bf16[32,104,128]{2,1,0:T(8,128)(2,1)}), bf16[32,104,128]{2,1,0:T(8,128)(2,1)}, u32[]{:S(2)}, u32[]{:S(2)}) async-start(bf16[32,104,128]{2,1,0:T(8,128)(2,1)} %reshape.581), calls=%async_computation.4 | async-start | bytes 1703936 | tf_op jit(solution)/shard_map/all_to_all | solution.py:689
  544.0 28.4 %collective-permute-start.110 = (bf16[2,4,128,256]{3,2,1,0:T(8,128)(2,1)}, bf16[2,4,128,256]{3,2,1,0:T(8,128)(2,1)}, u32[]{:S(2)}, u32[]{:S(2)}) collective-permute-start(bf16[2,4,128,256]{3,2,1,0:T(8,128)(2,1)} %select_convert_fusion), channel_id=1, source_target_pairs={{0,16},{8,24},{16,0},{24,8},{1,17},{9,25},{17,1},{25,9},{2,18},{10... | collective-permute-start | bytes 1572872 | tf_op jit(solution)/shard_map/ppermute | solution.py:649
  582.3 30.3 %collective-permute-start.112 = (bf16[2,4,128,256]{3,2,1,0:T(8,128)(2,1)}, bf16[2,4,128,256]{3,2,1,0:T(8,128)(2,1)}, u32[]{:S(2)}, u32[]{:S(2)}) collective-permute-start(bf16[2,4,128,256]{3,2,1,0:T(8,128)(2,1)} %pad_maximum_fusion.1), channel_id=1, source_target_pairs={{0,4},{1,5},{2,6},{3,7},{4,0},{5,1},{6,2},{7,3},{8,12},{9,13},{10,... | collective-permute-start | bytes 1572872 | tf_op jit(solution)/shard_map/ppermute | solution.py:594
  585.8 26.2 %all-to-all-start.3 = ((f32[32,1,1024]{2,1,0:T(1,128)}), f32[32,1,1024]{2,1,0:T(1,128)S(1)}, u32[]{:S(2)}, u32[]{:S(2)}) async-start(f32[32,1,1024]{2,1,0:T(1,128)} %broadcast_in_dim.90), calls=%async_computation.6 | async-start | bytes 262144 | tf_op jit(solution)/shard_map/all_to_all | solution.py:972
  (189 other events, 2220.1 us)
Sparse Core Ops, SparseCore 0:
  38.9 24.6 all-gather.20
  76.1 18.5 all-gather.22
  97.2 19.3 all-gather.24
  122.0 15.5 all-gather.12
  139.0 16.7 all-gather.14
  166.0 18.5 all-gather.26
  224.4 17.0 all-gather.16
  256.2 17.0 all-gather.18
  333.4 45.5 reduce-scatter.4
  385.3 28.7 reduce-scatter.6
  422.1 42.4 reduce-scatter.8
  495.6 29.8 reduce-scatter.10
